TPU v7x, 32 devices: a whole 2x2x4 slice. The times are simulated.
32 devices in a mesh: seq: 4 (over x, core), expert: 8 (over z, y).
Axes of the slice: x: 2, y: 2, z: 4, core: 2. Of those that a mesh axis runs over, the one named last changes fastest.
Arguments:
- tokens: bfloat16 [8, 896, 2048], P('expert', 'seq'), may hold values from -96 to 96
- slot_keys: bfloat16 [2048, 64], P(None, 'expert'), may hold values from -2 to 2
- w_in: bfloat16 [8, 2048, 6144], P('expert', None, 'seq'), may hold values from -0.125 to 0.125
- w_out: bfloat16 [8, 6144, 2048], P('expert', 'seq'), may hold values from -0.078125 to 0.078125
Outputs:
- mixed: bfloat16 [8, 896, 2048], P('expert', 'seq')
All inputs are finite; a program needn't handle non-finite values.
Results may differ from a plain program's by a relative error of at most 0.012.
Values may be sent and summed in bfloat16 or wider, within the bound.
No kernel may reach another device: no remote copies, remote signals or barrier semaphores. Data moves between devices by JAX's collectives and lax.ppermute only.
A program may use at most 64 MiB of HBM per device.

v0:
```python
import jax
import jax.numpy as jnp
from jax import lax
from jax.sharding import PartitionSpec as P


def on_device(tokens, slot_keys, w_in, w_out):
    token_rows = tokens[0]
    model_width = token_rows.shape[1]
    logits = jnp.dot(
        token_rows,
        lax.all_gather(slot_keys, "expert", axis=1, tiled=True),
        preferred_element_type=jnp.float32,
    )
    slot_count = logits.shape[1]
    local_top = jnp.max(logits, axis=0)
    top_score = lax.pmax(local_top, "seq")
    weights = jnp.exp(logits - top_score[None, :]).astype(jnp.bfloat16)
    local_total = jnp.sum(weights.astype(jnp.float32), axis=0)
    local_sum = jnp.einsum("tj,td->jd", weights, token_rows, preferred_element_type=jnp.float32)
    share_sum = lax.psum_scatter(local_sum, "seq", scatter_dimension=0, tiled=True)
    all_totals = lax.psum(local_total, "seq")
    share_rows = share_sum.shape[0]
    own_start = lax.axis_index("seq") * share_rows
    share_total = lax.dynamic_slice_in_dim(all_totals, own_start, share_rows, 0)
    share_inputs = (share_sum / share_total[:, None]).astype(jnp.bfloat16)
    slot_inputs = lax.all_gather(share_inputs, "seq", axis=0, tiled=True)
    expert_count = lax.axis_size("expert")
    per_expert = slot_count // expert_count
    grouped = slot_inputs.reshape(1, expert_count, per_expert, model_width)
    received = lax.all_to_all(grouped, "expert", split_axis=1, concat_axis=0, tiled=True)
    layout = received.shape
    flat_rows = received.reshape(-1, layout[3])
    hidden = jax.nn.gelu(
        jnp.dot(flat_rows, w_in[0], preferred_element_type=jnp.float32), approximate=True
    ).astype(jnp.bfloat16)
    group_term = jnp.dot(hidden, w_out[0], preferred_element_type=jnp.float32)
    group_terms = group_term.reshape(layout[0], layout[1], layout[2], group_term.shape[1])
    row_top = jnp.max(logits, axis=1)
    raised = jnp.exp(logits - row_top[:, None])
    mix_weights = (raised / jnp.sum(raised, axis=1)[:, None]).astype(jnp.bfloat16)
    group_sum = lax.psum_scatter(group_terms, "seq", scatter_dimension=3, tiled=True)
    outputs = group_sum.astype(jnp.bfloat16)
    returned_rows = lax.all_to_all(outputs, "expert", split_axis=0, concat_axis=1, tiled=True)
    slices = returned_rows.reshape(slot_count, returned_rows.shape[3])
    mixed_out = jnp.dot(
        mix_weights,
        lax.all_gather(slices, "seq", axis=1, tiled=True),
        preferred_element_type=jnp.float32,
    )
    return mixed_out.astype(jnp.bfloat16)[None]


def solution(mesh):
    placed = (
        P("expert", "seq", None),
        P(None, "expert"),
        P("expert", None, "seq"),
        P("expert", "seq", None),
    )
    return jax.shard_map(
        on_device, mesh=mesh, in_specs=placed, out_specs=P("expert", "seq", None), check_vma=False
    )
```

profile of v0, /device:TPU:0, one launch (start us, length us, event | category | flops | bytes accessed | tf_op | source)
XLA Modules:
  0.0 146.0 jit_solution(1918878131802778419)
XLA Ops:
  6.5 0.0 copy-start
  6.5 0.0 reduce-scatter.3.cloned.1.call-start
  6.5 32.9 %all_gather.9 = bf16[2048,64]{0,1:T(8,128)(2,1)S(1)} all-gather(bf16[2048,8]{0,1:T(8,128)(2,1)} %param.5), channel_id=1, replica_groups=mesh['seq'=4,'expert'=8] {'expert'}, dimensions={1}, use_global_device_ids=true | all-gather | bytes 294912 | tf_op jit(solution)/shard_map/all_gather | solution.py:12
  39.4 0.0 copy-done
  39.4 0.5 fusion.42
  39.9 5.7 %pmax.7 = f32[64]{0:T(128)S(1)} all-reduce(f32[64]{0:T(128)S(1)} %get-tuple-element.8), channel_id=1, replica_groups=mesh['seq'=4,'expert'=8] {'seq'}, use_global_device_ids=true, to_apply=%region_3.0 | all-reduce | flops 64 | bytes 512 | tf_op jit(solution)/shard_map/pmax | solution.py:17
  45.6 1.1 fusion.8
  46.7 0.0 reduce-scatter.3.cloned.1.call-update
  46.8 0.0 reduce-scatter.5.cloned.1.call-start
  46.8 0.2 fusion.35
  47.0 6.6 %psum.7 = f32[64]{0:T(128)S(1)} all-reduce(f32[64]{0:T(128)S(1)} %get-tuple-element.6), channel_id=1, replica_groups=mesh['seq'=4,'expert'=8] {'seq'}, use_global_device_ids=true, to_apply=%region_6.0 | all-reduce | flops 64 | bytes 512 | tf_op jit(solution)/shard_map/psum | solution.py:22
  53.6 0.1 dynamic_slice.3
  53.7 16.1 %reduce-scatter.3.cloned.1.call-done = f32[16,2048]{1,0:T(8,128)} async-done(((f32[64,2048]{1,0:T(8,128)}), f32[16,2048]{1,0:T(8,128)}) %reduce-scatter.3.cloned.1.call-update) | async-done | bytes 131088 | tf_op jit(solution)/shard_map/reduce_scatter | solution.py:21
  69.8 1.0 divide_convert_fusion
  70.8 5.8 %all_gather.10 = bf16[64,2048]{1,0:T(8,128)(2,1)S(1)} all-gather(bf16[16,2048]{1,0:T(8,128)(2,1)S(1)} %divide_convert_fusion), channel_id=1, replica_groups=mesh['seq'=4,'expert'=8] {'seq'}, dimensions={0}, use_global_device_ids=true | all-gather | bytes 327680 | tf_op jit(solution)/shard_map/all_gather | solution.py:27
  76.5 14.7 %all_to_all.8 = bf16[1,8,8,2048]{3,2,0,1:T(8,128)(2,1)S(1)} all-to-all(bf16[1,8,8,2048]{3,2,0,1:T(8,128)(2,1)S(1)} %bitcast.44), channel_id=1, replica_groups=mesh['seq'=4,'expert'=8] {'expert'}, dimensions={1} | all-to-all | bytes 524288 | tf_op jit(solution)/shard_map/all_to_all | solution.py:31
  91.3 7.7 %fusion.5 = f32[8,1,8,2048]{3,2,0,1:T(8,128)} fusion(bf16[1,1536,2048]{2,1,0:T(8,128)(2,1)} %param.7, bf16[1,2048,1536]{2,1,0:T(8,128)(2,1)} %param.6, bf16[1,8,8,2048]{3,2,0,1:T(8,128)(2,1)S(1)} %all_to_all.8), kind=kOutput, calls=%fused_computation.6 | convolution fusion | flops 806191104 | bytes 13369344 | tf_op jit(solution)/shard_map/dot_general | solution.py:37
  99.0 0.0 reduce-scatter.5.cloned.1.call-update
  99.0 19.9 %reduce-scatter.5.cloned.1.call-done = f32[8,1,8,512]{3,2,0,1:T(8,128)} async-done(((f32[8,1,8,2048]{3,2,0,1:T(8,128)}), f32[8,1,8,512]{3,2,0,1:T(8,128)}) %reduce-scatter.5.cloned.1.call-update) | async-done | bytes 131088 | tf_op jit(solution)/shard_map/reduce_scatter | solution.py:42
  118.9 0.9 convert_bitcast_fusion
  119.8 12.2 %all_to_all.9 = bf16[8,1,8,512]{3,2,1,0:T(8,128)(2,1)S(1)} all-to-all(bf16[8,1,8,512]{3,2,1,0:T(8,128)(2,1)S(1)} %convert_bitcast_fusion), channel_id=1, replica_groups=mesh['seq'=4,'expert'=8] {'expert'}, dimensions={0} | all-to-all | bytes 131072 | tf_op jit(solution)/shard_map/all_to_all | solution.py:44
  132.0 5.8 %all_gather.11 = bf16[64,2048]{1,0:T(8,128)(2,1)S(1)} all-gather(bf16[64,512]{1,0:T(8,128)(2,1)S(1)} %bitcast.45), channel_id=1, replica_groups=mesh['seq'=4,'expert'=8] {'seq'}, dimensions={1}, use_global_device_ids=true | all-gather | bytes 327680 | tf_op jit(solution)/shard_map/all_gather | solution.py:48
  137.8 1.4 fusion.4
Async XLA Ops:
  6.5 32.9 %copy-start = (bf16[1,224,2048]{2,1,0:T(8,128)(2,1)S(1)}, bf16[1,224,2048]{2,1,0:T(8,128)(2,1)}, u32[]{:S(2)}) copy-start(bf16[1,224,2048]{2,1,0:T(8,128)(2,1)} %param.4) | copy-start | bytes 2752516
  6.5 63.2 %reduce-scatter.3.cloned.1.call-start = ((), (), s32[]{:S(2)}) async-start(), calls=%async_computation.4 | async-start | bytes 655360 | tf_op jit(solution)/shard_map/reduce_scatter | solution.py:21
  46.8 72.1 %reduce-scatter.5.cloned.1.call-start = ((), (), s32[]{:S(2)}) async-start(), calls=%async_computation.5 | async-start | bytes 655360 | tf_op jit(solution)/shard_map/reduce_scatter | solution.py:42
Sparse Core Ops, SparseCore 0:
  46.9 22.8 reduce-scatter.2
  99.1 19.7 reduce-scatter.4
where the time goes:
time: 146 us
  blocking collectives  83.7 us (57%)
  waiting for transfers between devices  36 us (25%)
  between operations  13.4 us (9%)
  matrix products  10.7 us (7%)
  other arithmetic  2.09 us (1%)
    all_gather x1, blocking collectives, on_device(): lax.all_gather(slot_keys, 'expert', axis=1, tiled=True)  32.9 us
    reduce_scatter x1, waiting for transfers between devices, on_device(): lax.psum_scatter(group_terms, 'seq', scatter_dimension=3, tiled=True)  19.9 us
    reduce_scatter x1, waiting for transfers between devices, on_device(): lax.psum_scatter(local_sum, 'seq', scatter_dimension=0, tiled=True)  16.1 us
    all_to_all x1, blocking collectives, on_device(): lax.all_to_all(grouped, 'expert', split_axis=1, concat_axis=0, tiled=True)  14.7 us
    all_to_all x1, blocking collectives, on_device(): lax.all_to_all(outputs, 'expert', split_axis=0, concat_axis=1, tiled=True)  12.2 us
    dot_general x1, matrix products, on_device(): group_term = jnp.dot(hidden, w_out[0], preferred_element_type=jnp.float32)  7.68 us
    psum x1, blocking collectives, on_device(): all_totals = lax.psum(local_total, 'seq')  6.62 us
    all_gather x1, blocking collectives, on_device(): slot_inputs = lax.all_gather(share_inputs, 'seq', axis=0, tiled=True)  5.78 us
  transfers between devices with their start and end apart: 2, of which 2 were waited for; matrix products, arithmetic and copies ran while one was open for 0% of the time, Pallas kernels for 0%

commit v1 on v0

v1 whole, which is shorter than its diff:
```python
import functools

import jax
import jax.numpy as jnp
from jax import lax
from jax.experimental import pallas as pl
from jax.experimental.pallas import tpu as pltpu
from jax.sharding import Mesh, PartitionSpec as P

F32 = jnp.float32
BF16 = jnp.bfloat16
LANES = 128
SWAP = ((0, 1), (1, 0))


def column_halves(half):
    core = lax.axis_index("core")
    own = pl.ds(pl.multiple_of(core * half, LANES), half)
    other = pl.ds(pl.multiple_of((1 - core) * half, LANES), half)
    return own, other


def three_terms(value):
    first = value.astype(BF16).astype(F32)
    rest = value - first
    second = rest.astype(BF16).astype(F32)
    return first, second, rest - second


def stats_tile(top, total):
    shape = top.shape[:-1] + (LANES,)
    lane = lax.broadcasted_iota(jnp.int32, shape, len(shape) - 1)
    tile = jnp.zeros(shape, F32)
    for place, term in enumerate(three_terms(top) + three_terms(total)):
        tile = jnp.where(lane == place, term, tile)
    return tile


def read_stats(tile):
    top = tile[..., 0:1] + tile[..., 1:2] + tile[..., 2:3]
    total = tile[..., 3:4] + tile[..., 4:5] + tile[..., 5:6]
    return top, total


def dispatch_kernel(got_ref, swapped_ref, tok_ref, keep_ref, stats_ref, send_ref, mix_ref):
    half = got_ref.shape[2]
    slots = keep_ref.shape[0]
    own, other = column_halves(half)
    rows_by_cols = (((1,), (1,)), ((), ()))
    logits = lax.dot_general(
        got_ref[...].reshape(slots, half), tok_ref[:, own], rows_by_cols, preferred_element_type=F32
    ) + lax.dot_general(
        swapped_ref[...].reshape(slots, half), tok_ref[:, other], rows_by_cols, preferred_element_type=F32
    )
    top = jnp.max(logits, axis=1, keepdims=True)
    weights = jnp.exp(logits - top).astype(BF16)
    total = jnp.sum(weights.astype(F32), axis=1, keepdims=True)
    send_ref[:, :half] = jnp.dot(weights, tok_ref[:, other], preferred_element_type=F32).astype(BF16)
    send_ref[:, half:] = stats_tile(top, total).astype(BF16)
    keep_ref[...] = jnp.dot(weights, tok_ref[:, own], preferred_element_type=F32)
    lane = lax.broadcasted_iota(jnp.int32, stats_ref.shape, 1)
    stats_ref[...] = jnp.where(lane == 0, top, total)
    raised = jnp.exp(logits - jnp.max(logits, axis=0, keepdims=True))
    mix_ref[...] = (raised / jnp.sum(raised, axis=0, keepdims=True)).astype(BF16)


def chip_sum_kernel(keep_ref, stats_ref, came_ref, out_ref):
    half = keep_ref.shape[1]
    experts, chips, rows, _ = out_ref.shape
    top, total = stats_ref[:, 0:1], stats_ref[:, 1:2]
    came_top, came_total = read_stats(came_ref[:, half:].astype(F32))
    new_top = jnp.maximum(top, came_top)
    scale, came_scale = jnp.exp(top - new_top), jnp.exp(came_top - new_top)
    sums = (keep_ref[...] * scale + came_ref[:, :half].astype(F32) * came_scale).astype(BF16)
    tile = stats_tile(new_top, total * scale + came_total * came_scale).astype(BF16)
    sums = sums.reshape(experts, rows, half)
    tile = tile.reshape(experts, rows, LANES)
    for chip in range(chips):
        out_ref[:, chip, :, :half] = sums
        out_ref[:, chip, :, half:] = tile


def slot_inputs_of(ref):
    seqs, chips, rows, width = ref.shape
    half = width - LANES
    stats = [read_stats(ref[:, chip, :, half:].astype(F32)) for chip in range(chips)]
    top = functools.reduce(jnp.maximum, [s[0] for s in stats])
    scales = [jnp.exp(s[0] - top) for s in stats]
    total = sum(scale * s[1] for scale, s in zip(scales, stats))
    summed = sum(ref[:, chip, :, :half].astype(F32) * scales[chip] for chip in range(chips))
    return (summed / total).reshape(seqs * rows, half).astype(BF16)


def expert_kernel(
    chunks, mine_ref, swapped_ref, w_in_ref, w_out_ref, keep_ref, send_ref,
    w_in_buf, w_out_buf, acc_in, acc_out, hidden, sem_in, sem_out,
):
    width, units = w_in_buf.shape
    half = width // 2
    core = lax.axis_index("core")
    own, other = column_halves(half)
    step_in, step_out = width // chunks, units // chunks
    half_chunks = chunks // 2

    def row_start(k):
        side = core if k < half_chunks else 1 - core
        return pl.multiple_of(side * half + (k % half_chunks) * step_in, LANES)

    copies_in, copies_out = [], []
    for k in range(chunks):
        rows = pl.ds(row_start(k), step_in)
        copies_in.append(pltpu.make_async_copy(w_in_ref.at[rows], w_in_buf.at[rows], sem_in.at[k]))
        copies_in[-1].start()
    for k in range(chunks):
        rows = pl.ds(k * step_out, step_out)
        copies_out.append(pltpu.make_async_copy(w_out_ref.at[rows], w_out_buf.at[rows], sem_out.at[k]))
        copies_out[-1].start()
    sides = (slot_inputs_of(mine_ref), slot_inputs_of(swapped_ref))
    for k in range(chunks):
        copies_in[k].wait()
        start = (k % half_chunks) * step_in
        term = jnp.dot(
            sides[k // half_chunks][:, start : start + step_in],
            w_in_buf[pl.ds(row_start(k), step_in), :],
            preferred_element_type=F32,
        )
        acc_in[...] = term if k == 0 else acc_in[...] + term
    hidden[...] = jax.nn.gelu(acc_in[...], approximate=True).astype(BF16)
    for k in range(chunks):
        copies_out[k].wait()
        rows = pl.ds(k * step_out, step_out)
        left = hidden[:, k * step_out : (k + 1) * step_out]
        sent = jnp.dot(left, w_out_buf[rows, other], preferred_element_type=F32)
        acc_out[...] = sent if k == 0 else acc_out[...] + sent
        kept = jnp.dot(left, w_out_buf[rows, own], preferred_element_type=F32)
        keep_ref[...] = kept if k == 0 else keep_ref[...] + kept
    send_ref[...] = acc_out[...].astype(BF16)


def pair_sum_kernel(keep_ref, came_ref, out_ref):
    seqs, chips, rows, half = out_ref.shape
    sums = (keep_ref[...] + came_ref[...].astype(F32)).astype(BF16).reshape(seqs, rows, half)
    for chip in range(chips):
        out_ref[:, chip] = sums


def mix_kernel(mix_ref, mine_ref, swapped_ref, out_ref):
    experts, chips, rows, half = mine_ref.shape
    for cols, ref in zip(column_halves(half), (mine_ref, swapped_ref)):
        summed = sum(ref[:, chip].astype(F32) for chip in range(chips))
        slot_outputs = summed.reshape(experts * rows, half).astype(BF16)
        out_ref[:, cols] = lax.dot_general(
            mix_ref[...], slot_outputs, (((0,), (0,)), ((), ())), preferred_element_type=F32
        ).astype(BF16)


def call(kernel, outs, *args, scratch=(), in_hbm=(), flops=0, limit=16 << 20):
    size = sum(a.size * a.dtype.itemsize for a in args)
    specs = [
        pl.BlockSpec(memory_space=pltpu.HBM if i in in_hbm else pltpu.VMEM) for i in range(len(args))
    ]
    return pl.pallas_call(
        kernel,
        out_shape=[jax.ShapeDtypeStruct(shape, dtype) for shape, dtype in outs],
        in_specs=specs,
        out_specs=[pl.BlockSpec(memory_space=pltpu.VMEM)] * len(outs),
        scratch_shapes=list(scratch),
        compiler_params=pltpu.CompilerParams(vmem_limit_bytes=limit),
        cost_estimate=pl.CostEstimate(flops=flops, bytes_accessed=size, transcendentals=0),
    )(*args)


def on_device(tokens, slot_keys, w_in, w_out):
    token_rows = tokens[0]
    count, width = token_rows.shape
    half = width // 2
    per_expert = slot_keys.shape[1]
    experts, chips = lax.axis_size("expert"), lax.axis_size("chip")
    slots = experts * per_expert
    units = w_in.shape[2]

    keys = lax.dynamic_slice_in_dim(slot_keys.T, lax.axis_index("core") * half, half, 1)
    keys = jnp.broadcast_to(keys[None], (experts, per_expert, half))
    got = lax.all_to_all(keys, "expert", split_axis=0, concat_axis=0, tiled=True)
    swapped = lax.ppermute(got, "core", SWAP)
    keep, stats, send, mix = call(
        dispatch_kernel,
        [
            ((slots, half), F32),
            ((slots, LANES), F32),
            ((slots, half + LANES), BF16),
            ((slots, count), BF16),
        ],
        got, swapped, token_rows,
        flops=4 * slots * count * width,
    )
    came = lax.ppermute(send, "core", SWAP)
    (packed,) = call(
        chip_sum_kernel,
        [((experts, chips, per_expert, half + LANES), BF16)],
        keep, stats, came,
    )
    both = ("expert", "chip")
    flat = packed.reshape((experts * chips,) + packed.shape[2:])
    mine = lax.all_to_all(flat, both, split_axis=0, concat_axis=0, tiled=True)
    swapped = lax.ppermute(mine, "core", SWAP)
    chunks = 4
    keep, send = call(
        functools.partial(expert_kernel, chunks),
        [((slots, half), F32), ((slots, half), BF16)],
        mine.reshape(packed.shape), swapped.reshape(packed.shape), w_in[0], w_out[0],
        scratch=[
            pltpu.VMEM((width, units), BF16),
            pltpu.VMEM((units, width), BF16),
            pltpu.VMEM((slots, units), F32),
            pltpu.VMEM((slots, half), F32),
            pltpu.VMEM((slots, units), BF16),
            pltpu.SemaphoreType.DMA((chunks,)),
            pltpu.SemaphoreType.DMA((chunks,)),
        ],
        in_hbm=(2, 3),
        flops=4 * slots * width * units,
        limit=40 << 20,
    )
    came = lax.ppermute(send, "core", SWAP)
    (packed,) = call(pair_sum_kernel, [((experts, chips, per_expert, half), BF16)], keep, came)
    flat = packed.reshape((experts * chips,) + packed.shape[2:])
    mine = lax.all_to_all(flat, both, split_axis=0, concat_axis=0, tiled=True)
    swapped = lax.ppermute(mine, "core", SWAP)
    (mixed,) = call(
        mix_kernel,
        [((count, width), BF16)],
        mix, mine.reshape(packed.shape), swapped.reshape(packed.shape),
        flops=2 * slots * count * width,
    )
    return mixed[None]


def solution(mesh):
    sizes, names = [], []
    for name in mesh.axis_names:
        if name == "seq":
            sizes += [mesh.shape[name] // 2, 2]
            names += ["chip", "core"]
        else:
            sizes.append(mesh.shape[name])
            names.append(name)
    split = Mesh(mesh.devices.reshape(sizes), tuple(names))
    seq = ("chip", "core")
    placed = (
        P("expert", seq, None),
        P(None, "expert"),
        P("expert", None, seq),
        P("expert", seq, None),
    )
    return jax.shard_map(
        on_device, mesh=split, in_specs=placed, out_specs=P("expert", seq, None), check_vma=False
    )
```

time: 146 us -> 63.7 us (0.44)
  blocking collectives: 83.7 us -> 42 us
  waiting for transfers between devices: 36 us -> 6.89 us
  between operations: 13.4 us -> 0.04 us
  matrix products: 10.7 us -> 0 us
  local copies, waits for them, and re-layouts: 0.08 us -> 7.52 us
  Pallas kernels: 0 us -> 6.44 us
  other arithmetic: 2.09 us -> 0 us
    all_gather x3 -> x0, blocking collectives: 44.4 us -> none  [the longest x1 32.9 us: on_device(): lax.all_gather(slot_keys, 'expert', axis=1, tiled=True)]
    reduce_scatter x2 -> x0, waiting for transfers between devices: 35.9 us -> none  [the longest x1 19.9 us: on_device(): lax.psum_scatter(group_terms, 'seq', scatter_dimension=3, tiled=True)]
    all_to_all x2 -> x3, blocking collectives: 27 us -> 42 us  [the longest x2 27.6 us: on_device(): mine = lax.all_to_all(flat, both, split_axis=0, concat_axis=0, tiled=True)]
    dot_general x4 -> x0, matrix products: 10.7 us -> none  [the longest x1 7.68 us: on_device(): group_term = jnp.dot(hidden, w_out[0], preferred_element_type=jnp.float32)]
    unnamed x2 -> x8, local copies, waits for them, and re-layouts: 0.01 us -> 7.51 us
    ppermute x0 -> x5, waiting for transfers between devices: none -> 6.89 us  [the longest x2 3.11 us: on_device(): swapped = lax.ppermute(mine, 'core', SWAP)]
    psum x1 -> x0, blocking collectives: 6.62 us -> none  [on_device(): all_totals = lax.psum(local_total, 'seq')]
    pallas_call x0 -> x5, Pallas kernels: none -> 6.44 us  [call(): pl.pallas_call(kernel, out_shape=[jax.ShapeDtypeStruct(shape, dtype) for...]
  transfers between devices with their start and end apart: 2 -> 5, of which waited for: 2 -> 5; matrix products, arithmetic and copies ran while one was open for 0% -> 0% of each run, Pallas kernels for 0% -> 0%
where the time goes in v1:
time: 63.7 us; the launch traced here: 63.3 us
  blocking collectives  42 us (66%)
  local copies, waits for them, and re-layouts  7.52 us (12%)
  waiting for transfers between devices  6.89 us (11%)
  Pallas kernels  6.44 us (10%)
    all_to_all x2, blocking collectives, on_device(): mine = lax.all_to_all(flat, both, split_axis=0, concat_axis=0, tiled=True)  27.6 us
    all_to_all x1, blocking collectives, on_device(): lax.all_to_all(keys, 'expert', split_axis=0, concat_axis=0, tiled=True)  14.4 us
    unnamed x8, local copies, waits for them, and re-layouts  7.51 us
    pallas_call x5, Pallas kernels, call(): pl.pallas_call(kernel, out_shape=[jax.ShapeDtypeStruct(shape, dtype) for...  6.44 us
    ppermute x2, waiting for transfers between devices, on_device(): swapped = lax.ppermute(mine, 'core', SWAP)  3.11 us
    ppermute x2, waiting for transfers between devices, on_device(): came = lax.ppermute(send, 'core', SWAP)  2.43 us
    ppermute x1, waiting for transfers between devices, on_device(): swapped = lax.ppermute(got, 'core', SWAP)  1.35 us
  transfers between devices with their start and end apart: 5, of which 5 were waited for; matrix products, arithmetic and copies ran while one was open for 0% of the time, Pallas kernels for 0%

profile of v1, /device:TPU:0, one launch (start us, length us, event | category | flops | bytes accessed | tf_op | source)
XLA Modules:
  0.0 63.3 jit_solution(9679068510515144416)
XLA Ops:
  0.0 0.0 copy-start
  0.0 0.8 %copy-done = bf16[2048,8]{0,1:T(8,128)(2,1)S(1)} copy-done((bf16[2048,8]{0,1:T(8,128)(2,1)S(1)}, bf16[2048,8]{0,1:T(8,128)(2,1)}, u32[]{:S(2)}) %copy-start) | copy-done | bytes 32792
  0.8 14.4 %all_to_all.15.got_ref = bf16[8,8,1024]{2,1,0:T(8,128)(2,1)S(1)} all-to-all(bf16[8,8,1024]{2,1,0:T(8,128)(2,1)S(1)} %broadcast_in_dim.4), channel_id=1, replica_groups=mesh['chip'=2,'core'=2,'expert'=8] {'expert'}, dimensions={0} | all-to-all | bytes 262144 | tf_op jit(solution)/shard_map/all_to_all | solution.py:184
  15.2 0.0 collective-permute-start
  15.2 1.3 %collective-permute-done.swapped_ref = bf16[8,8,1024]{2,1,0:T(8,128)(2,1)S(1)} collective-permute-done((bf16[8,8,1024]{2,1,0:T(8,128)(2,1)S(1)}, bf16[8,8,1024]{2,1,0:T(8,128)(2,1)S(1)}, u32[]{:S(2)}, u32[]{:S(2)}) %collective-permute-start) | collective-permute-done | bytes 131104 | tf_op jit(solution)/shard_map/ppermute | solution.py:185
  16.6 0.0 copy-start.3
  16.6 1.2 %copy-done.3 = bf16[1,224,2048]{2,1,0:T(8,128)(2,1)S(1)} copy-done((bf16[1,224,2048]{2,1,0:T(8,128)(2,1)S(1)}, bf16[1,224,2048]{2,1,0:T(8,128)(2,1)}, u32[]{:S(2)}) %copy-start.3) | copy-done | bytes 917528
  17.8 0.9 %shard_map.46 = (f32[64,1024]{1,0:T(8,128)S(1)}, f32[64,128]{1,0:T(8,128)S(1)}, bf16[64,1152]{1,0:T(8,128)(2,1)S(1)}, bf16[64,224]{1,0:T(8,128)(2,1)S(1)}) custom-call(bf16[8,8,1024]{2,1,0:T(8,128)(2,1)S(1)} %all_to_all.15.got_ref, bf16[8,8,1024]{2,1,0:T(8,128)(2,1)S(1)} %collective-permute-done.swapped_ref, bf16[224,2048]{1,0:T(8,128)(2,1)S(1)} %bitcast.18), custom_call_target="tpu_custom_call" | custom-call | flops 117440512 | bytes 1179648 | tf_op jit(solution)/shard_map/pallas_call | solution.py:162
  18.7 0.2 collective-permute-start.1
  18.9 1.2 %collective-permute-done.1.came_ref = bf16[64,1152]{1,0:T(8,128)(2,1)S(1)} collective-permute-done((bf16[64,1152]{1,0:T(8,128)(2,1)S(1)}, bf16[64,1152]{1,0:T(8,128)(2,1)S(1)}, u32[]{:S(2)}, u32[]{:S(2)}) %collective-permute-start.1) | collective-permute-done | bytes 147488 | tf_op jit(solution)/shard_map/ppermute | solution.py:197
  20.1 0.3 shard_map.47
  20.5 14.2 %all_to_all.16 = bf16[16,8,1152]{2,1,0:T(8,128)(2,1)S(1)} all-to-all(bf16[16,8,1152]{2,1,0:T(8,128)(2,1)S(1)} %bitcast.15), channel_id=1, replica_groups=mesh['chip'=2,'core'=2,'expert'=8] {'expert','chip'}, dimensions={0} | all-to-all | bytes 589824 | tf_op jit(solution)/shard_map/all_to_all | solution.py:205
  34.6 0.0 collective-permute-start.2
  34.7 1.6 %collective-permute-done.2 = bf16[16,8,1152]{2,1,0:T(8,128)(2,1)S(1)} collective-permute-done((bf16[16,8,1152]{2,1,0:T(8,128)(2,1)S(1)}, bf16[16,8,1152]{2,1,0:T(8,128)(2,1)S(1)}, u32[]{:S(2)}, u32[]{:S(2)}) %collective-permute-start.2) | collective-permute-done | bytes 294944 | tf_op jit(solution)/shard_map/ppermute | solution.py:206
  36.2 0.0 copy-start.1
  36.2 2.8 %copy-done.1 = bf16[1,2048,1536]{2,1,0:T(8,128)(2,1)S(1)} copy-done((bf16[1,2048,1536]{2,1,0:T(8,128)(2,1)S(1)}, bf16[1,2048,1536]{2,1,0:T(8,128)(2,1)}, u32[]{:S(2)}) %copy-start.1) | copy-done | bytes 6291480
  39.0 0.0 copy-start.2
  39.0 2.8 %copy-done.2 = bf16[1,1536,2048]{2,1,0:T(8,128)(2,1)S(1)} copy-done((bf16[1,1536,2048]{2,1,0:T(8,128)(2,1)S(1)}, bf16[1,1536,2048]{2,1,0:T(8,128)(2,1)}, u32[]{:S(2)}) %copy-start.2) | copy-done | bytes 6291480
  41.8 3.8 %shard_map.48 = (f32[64,1024]{1,0:T(8,128)S(1)}, bf16[64,1024]{1,0:T(8,128)(2,1)S(1)}) custom-call(bf16[8,2,8,1152]{3,2,1,0:T(8,128)(2,1)S(1)} %bitcast.14, bf16[8,2,8,1152]{3,2,1,0:T(8,128)(2,1)S(1)} %bitcast.19, bf16[2048,1536]{1,0:T(8,128)(2,1)S(1)} %bitcast.12, bf16[1536,2048]{1,0:T(8,128)(2,1)S(1)} %bitcast.13), custom_call_target="tpu_custom_call" | custom-call | flops 805306368 | bytes 13172736 | tf_op jit(solution)/shard_map/pallas_call | solution.py:162
  45.6 0.2 collective-permute-start.3
  45.8 1.2 %collective-permute-done.3.came_ref = bf16[64,1024]{1,0:T(8,128)(2,1)S(1)} collective-permute-done((bf16[64,1024]{1,0:T(8,128)(2,1)S(1)}, bf16[64,1024]{1,0:T(8,128)(2,1)S(1)}, u32[]{:S(2)}, u32[]{:S(2)}) %collective-permute-start.3) | collective-permute-done | bytes 131104 | tf_op jit(solution)/shard_map/ppermute | solution.py:225
  47.0 13.4 %all_to_all.17 = bf16[16,8,1024]{2,1,0:T(8,128)(2,1)S(1)} all-to-all(bf16[16,8,1024]{2,1,0:T(8,128)(2,1)S(1)} %bitcast.16), channel_id=1, replica_groups=mesh['chip'=2,'core'=2,'expert'=8] {'expert','chip'}, dimensions={0} | all-to-all | bytes 524288 | tf_op jit(solution)/shard_map/all_to_all | solution.py:228
  60.5 0.0 collective-permute-start.4
  60.5 1.5 %collective-permute-done.4 = bf16[16,8,1024]{2,1,0:T(8,128)(2,1)S(1)} collective-permute-done((bf16[16,8,1024]{2,1,0:T(8,128)(2,1)S(1)}, bf16[16,8,1024]{2,1,0:T(8,128)(2,1)S(1)}, u32[]{:S(2)}, u32[]{:S(2)}) %collective-permute-start.4) | collective-permute-done | bytes 262176 | tf_op jit(solution)/shard_map/ppermute | solution.py:229
  62.0 1.3 %shard_map.50 = bf16[224,2048]{1,0:T(8,128)(2,1)} custom-call(bf16[64,224]{1,0:T(8,128)(2,1)S(1)} %get-tuple-element.11.mix_ref, bf16[8,2,8,1024]{3,2,1,0:T(8,128)(2,1)S(1)} %bitcast.17, bf16[8,2,8,1024]{3,2,1,0:T(8,128)(2,1)S(1)} %bitcast.20), custom_call_target="tpu_custom_call" | custom-call | flops 58720256 | bytes 552960 | tf_op jit(solution)/shard_map/pallas_call | solution.py:162
  (3 shorter events, 0.0 us)
Async XLA Ops:
  0.0 0.8 %copy-start = (bf16[2048,8]{0,1:T(8,128)(2,1)S(1)}, bf16[2048,8]{0,1:T(8,128)(2,1)}, u32[]{:S(2)}) copy-start(bf16[2048,8]{0,1:T(8,128)(2,1)} %param.5) | copy-start | bytes 98308
  15.2 1.3 %collective-permute-start = (bf16[8,8,1024]{2,1,0:T(8,128)(2,1)S(1)}, bf16[8,8,1024]{2,1,0:T(8,128)(2,1)S(1)}, u32[]{:S(2)}, u32[]{:S(2)}) collective-permute-start(bf16[8,8,1024]{2,1,0:T(8,128)(2,1)S(1)} %all_to_all.15.got_ref), channel_id=1, source_target_pairs={{0,8},{8,0},{1,9},{9,1},{2,10},{10,2},{3,11},{11,3},{4,12},{12,4},... | collective-permute-start | bytes 393224 | tf_op jit(solution)/shard_map/ppermute | solution.py:185
  16.6 1.2 %copy-start.3 = (bf16[1,224,2048]{2,1,0:T(8,128)(2,1)S(1)}, bf16[1,224,2048]{2,1,0:T(8,128)(2,1)}, u32[]{:S(2)}) copy-start(bf16[1,224,2048]{2,1,0:T(8,128)(2,1)} %param.4) | copy-start | bytes 2752516
  18.7 1.4 %collective-permute-start.1 = (bf16[64,1152]{1,0:T(8,128)(2,1)S(1)}, bf16[64,1152]{1,0:T(8,128)(2,1)S(1)}, u32[]{:S(2)}, u32[]{:S(2)}) collective-permute-start(bf16[64,1152]{1,0:T(8,128)(2,1)S(1)} %get-tuple-element.14), channel_id=1, source_target_pairs={{0,8},{8,0},{1,9},{9,1},{2,10},{10,2},{3,11},{11,3},{4,12},{12,4},... | collective-permute-start | bytes 442376 | tf_op jit(solution)/shard_map/ppermute | solution.py:197
  34.6 1.6 %collective-permute-start.2 = (bf16[16,8,1152]{2,1,0:T(8,128)(2,1)S(1)}, bf16[16,8,1152]{2,1,0:T(8,128)(2,1)S(1)}, u32[]{:S(2)}, u32[]{:S(2)}) collective-permute-start(bf16[16,8,1152]{2,1,0:T(8,128)(2,1)S(1)} %all_to_all.16), channel_id=1, source_target_pairs={{0,8},{8,0},{1,9},{9,1},{2,10},{10,2},{3,11},{11,3},{4,12},{12,4},... | collective-permute-start | bytes 884744 | tf_op jit(solution)/shard_map/ppermute | solution.py:206
  36.2 2.8 %copy-start.1 = (bf16[1,2048,1536]{2,1,0:T(8,128)(2,1)S(1)}, bf16[1,2048,1536]{2,1,0:T(8,128)(2,1)}, u32[]{:S(2)}) copy-start(bf16[1,2048,1536]{2,1,0:T(8,128)(2,1)} %param.6) | copy-start | bytes 18874372
  39.0 2.8 %copy-start.2 = (bf16[1,1536,2048]{2,1,0:T(8,128)(2,1)S(1)}, bf16[1,1536,2048]{2,1,0:T(8,128)(2,1)}, u32[]{:S(2)}) copy-start(bf16[1,1536,2048]{2,1,0:T(8,128)(2,1)} %param.7) | copy-start | bytes 18874372
  45.6 1.4 %collective-permute-start.3 = (bf16[64,1024]{1,0:T(8,128)(2,1)S(1)}, bf16[64,1024]{1,0:T(8,128)(2,1)S(1)}, u32[]{:S(2)}, u32[]{:S(2)}) collective-permute-start(bf16[64,1024]{1,0:T(8,128)(2,1)S(1)} %get-tuple-element.16), channel_id=1, source_target_pairs={{0,8},{8,0},{1,9},{9,1},{2,10},{10,2},{3,11},{11,3},{4,12},{12,4},... | collective-permute-start | bytes 393224 | tf_op jit(solution)/shard_map/ppermute | solution.py:225
  60.5 1.5 %collective-permute-start.4 = (bf16[16,8,1024]{2,1,0:T(8,128)(2,1)S(1)}, bf16[16,8,1024]{2,1,0:T(8,128)(2,1)S(1)}, u32[]{:S(2)}, u32[]{:S(2)}) collective-permute-start(bf16[16,8,1024]{2,1,0:T(8,128)(2,1)S(1)} %all_to_all.17), channel_id=1, source_target_pairs={{0,8},{8,0},{1,9},{9,1},{2,10},{10,2},{3,11},{11,3},{4,12},{12,4},... | collective-permute-start | bytes 786440 | tf_op jit(solution)/shard_map/ppermute | solution.py:229

commit v2 on v1

--- a/solution.py
+++ b/solution.py
@@ -91,50 +91,41 @@
     return (summed / total).reshape(seqs * rows, half).astype(BF16)
 
 
+def fetch_kernel(sides, *refs):
+    count = len(sides)
+    core = lax.axis_index("core")
+    copies = []
+    for i, side in enumerate(sides):
+        rows = refs[count + i].shape[0]
+        block = {"own": core, "other": 1 - core, "first": 0}[side]
+        source = refs[i].at[pl.ds(pl.multiple_of(block * rows, LANES // 4), rows)]
+        copies.append(pltpu.make_async_copy(source, refs[count + i], refs[2 * count].at[i]))
+    for copy in copies:
+        copy.start()
+    for copy in copies:
+        copy.wait()
+
+
 def expert_kernel(
-    chunks, mine_ref, swapped_ref, w_in_ref, w_out_ref, keep_ref, send_ref,
-    w_in_buf, w_out_buf, acc_in, acc_out, hidden, sem_in, sem_out,
+    mine_ref, swapped_ref, w_own_ref, w_other_ref, w_first_ref, w_out_ref, keep_ref, send_ref,
+    w_second, sem,
 ):
-    width, units = w_in_buf.shape
-    half = width // 2
-    core = lax.axis_index("core")
+    half = w_own_ref.shape[0]
+    rows = w_first_ref.shape[0]
     own, other = column_halves(half)
-    step_in, step_out = width // chunks, units // chunks
-    half_chunks = chunks // 2
-
-    def row_start(k):
-        side = core if k < half_chunks else 1 - core
-        return pl.multiple_of(side * half + (k % half_chunks) * step_in, LANES)
-
-    copies_in, copies_out = [], []
-    for k in range(chunks):
-        rows = pl.ds(row_start(k), step_in)
-        copies_in.append(pltpu.make_async_copy(w_in_ref.at[rows], w_in_buf.at[rows], sem_in.at[k]))
-        copies_in[-1].start()
-    for k in range(chunks):
-        rows = pl.ds(k * step_out, step_out)
-        copies_out.append(pltpu.make_async_copy(w_out_ref.at[rows], w_out_buf.at[rows], sem_out.at[k]))
-        copies_out[-1].start()
-    sides = (slot_inputs_of(mine_ref), slot_inputs_of(swapped_ref))
-    for k in range(chunks):
-        copies_in[k].wait()
-        start = (k % half_chunks) * step_in
-        term = jnp.dot(
-            sides[k // half_chunks][:, start : start + step_in],
-            w_in_buf[pl.ds(row_start(k), step_in), :],
-            preferred_element_type=F32,
-        )
-        acc_in[...] = term if k == 0 else acc_in[...] + term
-    hidden[...] = jax.nn.gelu(acc_in[...], approximate=True).astype(BF16)
-    for k in range(chunks):
-        copies_out[k].wait()
-        rows = pl.ds(k * step_out, step_out)
-        left = hidden[:, k * step_out : (k + 1) * step_out]
-        sent = jnp.dot(left, w_out_buf[rows, other], preferred_element_type=F32)
-        acc_out[...] = sent if k == 0 else acc_out[...] + sent
-        kept = jnp.dot(left, w_out_buf[rows, own], preferred_element_type=F32)
-        keep_ref[...] = kept if k == 0 else keep_ref[...] + kept
-    send_ref[...] = acc_out[...].astype(BF16)
+    copy = pltpu.make_async_copy(w_out_ref.at[pl.ds(rows, rows)], w_second, sem)
+    copy.start()
+    summed = jnp.dot(
+        slot_inputs_of(mine_ref), w_own_ref[...], preferred_element_type=F32
+    ) + jnp.dot(slot_inputs_of(swapped_ref), w_other_ref[...], preferred_element_type=F32)
+    hidden = jax.nn.gelu(summed, approximate=True).astype(BF16)
+    first, second = hidden[:, :rows], hidden[:, rows:]
+    sent = jnp.dot(first, w_first_ref[:, other], preferred_element_type=F32)
+    kept = jnp.dot(first, w_first_ref[:, own], preferred_element_type=F32)
+    copy.wait()
+    sent += jnp.dot(second, w_second[:, other], preferred_element_type=F32)
+    send_ref[...] = sent.astype(BF16)
+    keep_ref[...] = kept + jnp.dot(second, w_second[:, own], preferred_element_type=F32)
 
 
 def pair_sum_kernel(keep_ref, came_ref, out_ref):
@@ -154,20 +145,40 @@
         ).astype(BF16)
 
 
-def call(kernel, outs, *args, scratch=(), in_hbm=(), flops=0, limit=16 << 20):
-    size = sum(a.size * a.dtype.itemsize for a in args)
-    specs = [
-        pl.BlockSpec(memory_space=pltpu.HBM if i in in_hbm else pltpu.VMEM) for i in range(len(args))
-    ]
+def nbytes(arrays):
+    return sum(a.size * a.dtype.itemsize for a in arrays)
+
+
+def call(kernel, outs, *args, scratch=(), in_hbm=(), stay=False, flops=0, limit=16 << 20):
     return pl.pallas_call(
         kernel,
-        out_shape=[jax.ShapeDtypeStruct(shape, dtype) for shape, dtype in outs],
-        in_specs=specs,
+        out_shape=[
+            (pltpu.VMEM if stay else jax.ShapeDtypeStruct)(shape, dtype) for shape, dtype in outs
+        ],
+        in_specs=[
+            pl.BlockSpec(memory_space=pltpu.HBM if i in in_hbm else pltpu.VMEM)
+            for i in range(len(args))
+        ],
         out_specs=[pl.BlockSpec(memory_space=pltpu.VMEM)] * len(outs),
         scratch_shapes=list(scratch),
         compiler_params=pltpu.CompilerParams(vmem_limit_bytes=limit),
-        cost_estimate=pl.CostEstimate(flops=flops, bytes_accessed=size, transcendentals=0),
+        cost_estimate=pl.CostEstimate(flops=flops, bytes_accessed=nbytes(args), transcendentals=0),
     )(*args)
+
+
+def fetch(after, *parts):
+    after, *arrays = lax.optimization_barrier((after,) + tuple(a for a, _, _ in parts))
+    outs = [((rows,) + a.shape[1:], a.dtype) for a, _, rows in parts]
+    near = call(
+        functools.partial(fetch_kernel, [side for _, side, _ in parts]),
+        outs,
+        *[pltpu.with_memory_space_constraint(a, pltpu.HBM) for a in arrays],
+        scratch=[pltpu.SemaphoreType.DMA((len(parts),))],
+        in_hbm=range(len(parts)),
+        stay=True,
+        limit=4 << 20,
+    )
+    return after, near
 
 
 def on_device(tokens, slot_keys, w_in, w_out):
@@ -182,7 +193,11 @@
     keys = lax.dynamic_slice_in_dim(slot_keys.T, lax.axis_index("core") * half, half, 1)
     keys = jnp.broadcast_to(keys[None], (experts, per_expert, half))
     got = lax.all_to_all(keys, "expert", split_axis=0, concat_axis=0, tiled=True)
+    got, (near_rows, w_own) = fetch(
+        got, (token_rows, "first", count), (w_in[0], "own", half)
+    )
     swapped = lax.ppermute(got, "core", SWAP)
+    swapped, near_rows, w_own = lax.optimization_barrier((swapped, near_rows, w_own))
     keep, stats, send, mix = call(
         dispatch_kernel,
         [
@@ -191,10 +206,12 @@
             ((slots, half + LANES), BF16),
             ((slots, count), BF16),
         ],
-        got, swapped, token_rows,
+        got, swapped, near_rows,
         flops=4 * slots * count * width,
     )
+    send, (w_other,) = fetch(send, (w_in[0], "other", half))
     came = lax.ppermute(send, "core", SWAP)
+    came, w_other = lax.optimization_barrier((came, w_other))
     (packed,) = call(
         chip_sum_kernel,
         [((experts, chips, per_expert, half + LANES), BF16)],
@@ -203,24 +220,19 @@
     both = ("expert", "chip")
     flat = packed.reshape((experts * chips,) + packed.shape[2:])
     mine = lax.all_to_all(flat, both, split_axis=0, concat_axis=0, tiled=True)
+    mine, (w_first,) = fetch(mine, (w_out[0], "first", units // 2))
     swapped = lax.ppermute(mine, "core", SWAP)
-    chunks = 4
+    swapped, w_first = lax.optimization_barrier((swapped, w_first))
+    held = (w_own, w_other, w_first)
     keep, send = call(
-        functools.partial(expert_kernel, chunks),
+        expert_kernel,
         [((slots, half), F32), ((slots, half), BF16)],
-        mine.reshape(packed.shape), swapped.reshape(packed.shape), w_in[0], w_out[0],
-        scratch=[
-            pltpu.VMEM((width, units), BF16),
-            pltpu.VMEM((units, width), BF16),
-            pltpu.VMEM((slots, units), F32),
-            pltpu.VMEM((slots, half), F32),
-            pltpu.VMEM((slots, units), BF16),
-            pltpu.SemaphoreType.DMA((chunks,)),
-            pltpu.SemaphoreType.DMA((chunks,)),
-        ],
-        in_hbm=(2, 3),
+        mine.reshape(packed.shape), swapped.reshape(packed.shape), *held,
+        pltpu.with_memory_space_constraint(w_out[0], pltpu.HBM),
+        scratch=[pltpu.VMEM((units // 2, width), BF16), pltpu.SemaphoreType.DMA],
+        in_hbm=(5,),
         flops=4 * slots * width * units,
-        limit=40 << 20,
+        limit=24 << 20,
     )
     came = lax.ppermute(send, "core", SWAP)
     (packed,) = call(pair_sum_kernel, [((experts, chips, per_expert, half), BF16)], keep, came)

time: 63.7 us -> 59 us (0.926)
  local copies, waits for them, and re-layouts: 7.52 us -> 0.77 us
  Pallas kernels: 6.44 us -> 11.9 us
  waiting for transfers between devices: 6.89 us -> 2.53 us
  starting transfers between devices: 0.43 us -> 1.13 us
    unnamed x8 -> x2, local copies, waits for them, and re-layouts: 7.51 us -> 0.76 us
    pallas_call x5 -> x8, Pallas kernels: 6.44 us -> 11.9 us  [call(): pl.pallas_call(kernel, out_shape=[(pltpu.VMEM if stay else jax.ShapeDtype...]
    ppermute x2, waiting for transfers between devices: 3.11 us -> 1.54 us  [on_device(): swapped = lax.ppermute(mine, 'core', SWAP)]
    ppermute x2, waiting for transfers between devices: 2.43 us -> 0.99 us  [on_device(): came = lax.ppermute(send, 'core', SWAP)]
    ppermute x1, waiting for transfers between devices: 1.35 us -> 0.01 us  [on_device(): swapped = lax.ppermute(got, 'core', SWAP)]
    ppermute x2, starting transfers between devices: 0.42 us -> 1.12 us  [on_device(): came = lax.ppermute(send, 'core', SWAP)]
  transfers between devices with their start and end apart: 5 -> 5, of which waited for: 5 -> 2; matrix products, arithmetic and copies ran while one was open for 0% -> 0% of each run, Pallas kernels for 0% -> 10%
where the time goes in v2:
time: 59 us; the launch traced here: 58.6 us
  blocking collectives  42.2 us (72%)
  Pallas kernels  11.9 us (20%)
  waiting for transfers between devices  2.53 us (4%)
  starting transfers between devices  1.13 us (2%)
  local copies, waits for them, and re-layouts  0.77 us (1%)
    all_to_all x2, blocking collectives, on_device(): mine = lax.all_to_all(flat, both, split_axis=0, concat_axis=0, tiled=True)  27.7 us
    all_to_all x1, blocking collectives, on_device(): lax.all_to_all(keys, 'expert', split_axis=0, concat_axis=0, tiled=True)  14.4 us
    pallas_call x8, Pallas kernels, call(): pl.pallas_call(kernel, out_shape=[(pltpu.VMEM if stay else jax.ShapeDtype...  11.9 us
    ppermute x2, waiting for transfers between devices, on_device(): swapped = lax.ppermute(mine, 'core', SWAP)  1.54 us
  transfers between devices with their start and end apart: 5, of which 2 were waited for; matrix products, arithmetic and copies ran while one was open for 0% of the time, Pallas kernels for 10%

profile of v2, /device:TPU:0, one launch (start us, length us, event | category | flops | bytes accessed | tf_op | source)
XLA Modules:
  0.0 58.6 jit_solution(11148729587490029058)
XLA Ops:
  0.0 0.0 copy-start
  0.0 0.8 %copy-done = bf16[2048,8]{0,1:T(8,128)(2,1)S(1)} copy-done((bf16[2048,8]{0,1:T(8,128)(2,1)S(1)}, bf16[2048,8]{0,1:T(8,128)(2,1)}, u32[]{:S(2)}) %copy-start) | copy-done | bytes 32792
  0.8 14.4 %all_to_all.15.got_ref = bf16[8,8,1024]{2,1,0:T(8,128)(2,1)S(1)} all-to-all(bf16[8,8,1024]{2,1,0:T(8,128)(2,1)S(1)} %broadcast_in_dim.4), channel_id=1, replica_groups=mesh['chip'=2,'core'=2,'expert'=8] {'expert'}, dimensions={0} | all-to-all | bytes 262144 | tf_op jit(solution)/shard_map/all_to_all | solution.py:195
  15.2 0.0 collective-permute-start
  15.2 2.2 %shard_map.46 = (bf16[224,2048]{1,0:T(8,128)(2,1)S(1)}, bf16[1024,1536]{1,0:T(8,128)(2,1)S(1)}) custom-call(bf16[224,2048]{1,0:T(8,128)(2,1)} %bitcast.22, bf16[2048,1536]{1,0:T(8,128)(2,1)} %bitcast.18), custom_call_target="tpu_custom_call" | custom-call | bytes 7208960 | tf_op jit(solution)/shard_map/pallas_call | solution.py:153
  17.4 0.0 collective-permute-done.swapped_ref
  17.4 0.9 %shard_map.47 = (f32[64,1024]{1,0:T(8,128)S(1)}, f32[64,128]{1,0:T(8,128)S(1)}, bf16[64,1152]{1,0:T(8,128)(2,1)S(1)}, bf16[64,224]{1,0:T(8,128)(2,1)S(1)}) custom-call(bf16[8,8,1024]{2,1,0:T(8,128)(2,1)S(1)} %all_to_all.15.got_ref, bf16[8,8,1024]{2,1,0:T(8,128)(2,1)S(1)} %collective-permute-done.swapped_ref, bf16[224,2048]{1,0:T(8,128)(2,1)S(1)} %get-tuple-element.33.tok_ref), custom_call_target="tpu_custom_call" | custom-call | flops 117440512 | bytes 1179648 | tf_op jit(solution)/shard_map/pallas_call | solution.py:153
  18.4 0.6 collective-permute-start.1
  18.9 1.9 %shard_map.48.w_other_ref = bf16[1024,1536]{1,0:T(8,128)(2,1)S(1)} custom-call(bf16[2048,1536]{1,0:T(8,128)(2,1)} %bitcast.19), custom_call_target="tpu_custom_call" | custom-call | bytes 6291456 | tf_op jit(solution)/shard_map/pallas_call | solution.py:153
  20.8 0.0 collective-permute-done.1.came_ref
  20.9 0.3 shard_map.49
  21.2 14.1 %all_to_all.16 = bf16[16,8,1152]{2,1,0:T(8,128)(2,1)S(1)} all-to-all(bf16[16,8,1152]{2,1,0:T(8,128)(2,1)S(1)} %bitcast.12), channel_id=1, replica_groups=mesh['chip'=2,'core'=2,'expert'=8] {'expert','chip'}, dimensions={0} | all-to-all | bytes 589824 | tf_op jit(solution)/shard_map/all_to_all | solution.py:222
  35.3 0.0 collective-permute-start.2
  35.3 1.9 %shard_map.50.w_first_ref = bf16[768,2048]{1,0:T(8,128)(2,1)S(1)} custom-call(bf16[1536,2048]{1,0:T(8,128)(2,1)} %bitcast.20), custom_call_target="tpu_custom_call" | custom-call | bytes 6291456 | tf_op jit(solution)/shard_map/pallas_call | solution.py:153
  37.2 0.0 collective-permute-done.2
  37.2 3.3 %shard_map.51 = (f32[64,1024]{1,0:T(8,128)S(1)}, bf16[64,1024]{1,0:T(8,128)(2,1)S(1)}) custom-call(bf16[8,2,8,1152]{3,2,1,0:T(8,128)(2,1)S(1)} %bitcast.13, bf16[8,2,8,1152]{3,2,1,0:T(8,128)(2,1)S(1)} %bitcast.16, bf16[1024,1536]{1,0:T(8,128)(2,1)S(1)} %get-tuple-element.44.w_own_ref, bf16[1024,1536]{1,0:T(8,128)(2,1)S(1)} %shard_map.48.w_other_ref, ...), custom_call_target="tpu_custom_call" | custom-call | flops 805306368 | bytes 16318464 | tf_op jit(solution)/shard_map/pallas_call | solution.py:153
  40.5 0.6 collective-permute-start.3
  41.1 1.0 %collective-permute-done.3.came_ref = bf16[64,1024]{1,0:T(8,128)(2,1)S(1)} collective-permute-done((bf16[64,1024]{1,0:T(8,128)(2,1)S(1)}, bf16[64,1024]{1,0:T(8,128)(2,1)S(1)}, u32[]{:S(2)}, u32[]{:S(2)}) %collective-permute-start.3) | collective-permute-done | bytes 131104 | tf_op jit(solution)/shard_map/ppermute | solution.py:237
  42.1 13.6 %all_to_all.17 = bf16[16,8,1024]{2,1,0:T(8,128)(2,1)S(1)} all-to-all(bf16[16,8,1024]{2,1,0:T(8,128)(2,1)S(1)} %bitcast.14), channel_id=1, replica_groups=mesh['chip'=2,'core'=2,'expert'=8] {'expert','chip'}, dimensions={0} | all-to-all | bytes 524288 | tf_op jit(solution)/shard_map/all_to_all | solution.py:240
  55.7 0.0 collective-permute-start.4
  55.7 1.5 %collective-permute-done.4 = bf16[16,8,1024]{2,1,0:T(8,128)(2,1)S(1)} collective-permute-done((bf16[16,8,1024]{2,1,0:T(8,128)(2,1)S(1)}, bf16[16,8,1024]{2,1,0:T(8,128)(2,1)S(1)}, u32[]{:S(2)}, u32[]{:S(2)}) %collective-permute-start.4) | collective-permute-done | bytes 262176 | tf_op jit(solution)/shard_map/ppermute | solution.py:241
  57.3 1.3 %shard_map.53 = bf16[224,2048]{1,0:T(8,128)(2,1)} custom-call(bf16[64,224]{1,0:T(8,128)(2,1)S(1)} %get-tuple-element.34.mix_ref, bf16[8,2,8,1024]{3,2,1,0:T(8,128)(2,1)S(1)} %bitcast.15, bf16[8,2,8,1024]{3,2,1,0:T(8,128)(2,1)S(1)} %bitcast.17), custom_call_target="tpu_custom_call" | custom-call | flops 58720256 | bytes 552960 | tf_op jit(solution)/shard_map/pallas_call | solution.py:153
  (3 shorter events, 0.0 us)
Async XLA Ops:
  0.0 0.8 %copy-start = (bf16[2048,8]{0,1:T(8,128)(2,1)S(1)}, bf16[2048,8]{0,1:T(8,128)(2,1)}, u32[]{:S(2)}) copy-start(bf16[2048,8]{0,1:T(8,128)(2,1)} %param.5) | copy-start | bytes 98308
  15.2 2.2 %collective-permute-start = (bf16[8,8,1024]{2,1,0:T(8,128)(2,1)S(1)}, bf16[8,8,1024]{2,1,0:T(8,128)(2,1)S(1)}, u32[]{:S(2)}, u32[]{:S(2)}) collective-permute-start(bf16[8,8,1024]{2,1,0:T(8,128)(2,1)S(1)} %all_to_all.15.got_ref), channel_id=1, source_target_pairs={{0,8},{8,0},{1,9},{9,1},{2,10},{10,2},{3,11},{11,3},{4,12},{12,4},... | collective-permute-start | bytes 393224 | tf_op jit(solution)/shard_map/ppermute | solution.py:199
  18.4 2.5 %collective-permute-start.1 = (bf16[64,1152]{1,0:T(8,128)(2,1)S(1)}, bf16[64,1152]{1,0:T(8,128)(2,1)S(1)}, u32[]{:S(2)}, u32[]{:S(2)}) collective-permute-start(bf16[64,1152]{1,0:T(8,128)(2,1)S(1)} %get-tuple-element.38), channel_id=1, source_target_pairs={{0,8},{8,0},{1,9},{9,1},{2,10},{10,2},{3,11},{11,3},{4,12},{12,4},... | collective-permute-start | bytes 442376 | tf_op jit(solution)/shard_map/ppermute | solution.py:213
  35.3 1.9 %collective-permute-start.2 = (bf16[16,8,1152]{2,1,0:T(8,128)(2,1)S(1)}, bf16[16,8,1152]{2,1,0:T(8,128)(2,1)S(1)}, u32[]{:S(2)}, u32[]{:S(2)}) collective-permute-start(bf16[16,8,1152]{2,1,0:T(8,128)(2,1)S(1)} %all_to_all.16), channel_id=1, source_target_pairs={{0,8},{8,0},{1,9},{9,1},{2,10},{10,2},{3,11},{11,3},{4,12},{12,4},... | collective-permute-start | bytes 884744 | tf_op jit(solution)/shard_map/ppermute | solution.py:224
  40.5 1.6 %collective-permute-start.3 = (bf16[64,1024]{1,0:T(8,128)(2,1)S(1)}, bf16[64,1024]{1,0:T(8,128)(2,1)S(1)}, u32[]{:S(2)}, u32[]{:S(2)}) collective-permute-start(bf16[64,1024]{1,0:T(8,128)(2,1)S(1)} %get-tuple-element.48), channel_id=1, source_target_pairs={{0,8},{8,0},{1,9},{9,1},{2,10},{10,2},{3,11},{11,3},{4,12},{12,4},... | collective-permute-start | bytes 393224 | tf_op jit(solution)/shard_map/ppermute | solution.py:237
  55.7 1.5 %collective-permute-start.4 = (bf16[16,8,1024]{2,1,0:T(8,128)(2,1)S(1)}, bf16[16,8,1024]{2,1,0:T(8,128)(2,1)S(1)}, u32[]{:S(2)}, u32[]{:S(2)}) collective-permute-start(bf16[16,8,1024]{2,1,0:T(8,128)(2,1)S(1)} %all_to_all.17), channel_id=1, source_target_pairs={{0,8},{8,0},{1,9},{9,1},{2,10},{10,2},{3,11},{11,3},{4,12},{12,4},... | collective-permute-start | bytes 786440 | tf_op jit(solution)/shard_map/ppermute | solution.py:241

commit v3 on v2

v3 whole, which is shorter than its diff:
```python
import functools
import math

import jax
import jax.numpy as jnp
from jax import lax
from jax.experimental import pallas as pl
from jax.experimental.pallas import tpu as pltpu
from jax.sharding import Mesh, PartitionSpec as P

F32 = jnp.float32
BF16 = jnp.bfloat16
LANES = 128
SWAP = ((0, 1), (1, 0))
ROWS_BY_ROWS = (((1,), (1,)), ((), ()))


def column_halves(half):
    core = lax.axis_index("core")
    own = pl.ds(pl.multiple_of(core * half, LANES), half)
    other = pl.ds(pl.multiple_of((1 - core) * half, LANES), half)
    return own, other


def three_terms(value):
    first = value.astype(BF16).astype(F32)
    rest = value - first
    second = rest.astype(BF16).astype(F32)
    return first, second, rest - second


def stats_tile(top, total):
    shape = top.shape[:-1] + (LANES,)
    lane = lax.broadcasted_iota(jnp.int32, shape, len(shape) - 1)
    tile = jnp.zeros(shape, F32)
    for place, term in enumerate(three_terms(top) + three_terms(total)):
        tile = jnp.where(lane == place, term, tile)
    return tile


def read_stats(tile):
    top = tile[..., 0:1] + tile[..., 1:2] + tile[..., 2:3]
    total = tile[..., 3:4] + tile[..., 4:5] + tile[..., 5:6]
    return top, total


def copy_parts(sem, pairs):
    copies = [pltpu.make_async_copy(src, dst, sem.at[i]) for i, (src, dst) in enumerate(pairs)]
    for copy in copies:
        copy.start()
    return copies


def block_rows(start, count):
    return pl.ds(pl.multiple_of(start, LANES), count)


def first_fetch_kernel(tok_ref, w_in_ref, near_tok, near_w, sem):
    half = w_in_ref.shape[0] // 2
    rows = near_w.shape[0]
    start = lax.axis_index("core") * half
    pairs = [(tok_ref, near_tok), (w_in_ref.at[block_rows(start, rows)], near_w)]
    for copy in copy_parts(sem, pairs):
        copy.wait()


def own_logits_kernel(got_ref, tok_ref, w_in_ref, part_ref, near_w, sem):
    slots = part_ref.shape[0]
    half = got_ref.shape[2]
    rows = near_w.shape[0]
    start = lax.axis_index("core") * half + (half - rows)
    copies = copy_parts(sem, [(w_in_ref.at[block_rows(start, rows)], near_w)])
    own, _ = column_halves(half)
    part_ref[...] = lax.dot_general(
        got_ref[...].reshape(slots, half), tok_ref[:, own], ROWS_BY_ROWS, preferred_element_type=F32
    )
    for copy in copies:
        copy.wait()


def send_sums_kernel(swapped_ref, part_ref, tok_ref, logits_ref, weights_ref, stats_ref, send_ref):
    half = swapped_ref.shape[2]
    slots = part_ref.shape[0]
    _, other = column_halves(half)
    logits = part_ref[...] + lax.dot_general(
        swapped_ref[...].reshape(slots, half), tok_ref[:, other], ROWS_BY_ROWS,
        preferred_element_type=F32,
    )
    logits_ref[...] = logits
    top = jnp.max(logits, axis=1, keepdims=True)
    weights = jnp.exp(logits - top).astype(BF16)
    weights_ref[...] = weights
    total = jnp.sum(weights.astype(F32), axis=1, keepdims=True)
    send_ref[:, :half] = jnp.dot(weights, tok_ref[:, other], preferred_element_type=F32).astype(BF16)
    send_ref[:, half:] = stats_tile(top, total).astype(BF16)
    lane = lax.broadcasted_iota(jnp.int32, stats_ref.shape, 1)
    stats_ref[...] = jnp.where(lane == 0, top, total)


def keep_sums_kernel(logits_ref, weights_ref, tok_ref, w_in_ref, keep_ref, mix_ref, near_w, sem):
    half = keep_ref.shape[1]
    start = (1 - lax.axis_index("core")) * half
    copies = copy_parts(sem, [(w_in_ref.at[block_rows(start, near_w.shape[0])], near_w)])
    own, _ = column_halves(half)
    keep_ref[...] = jnp.dot(weights_ref[...], tok_ref[:, own], preferred_element_type=F32)
    logits = logits_ref[...]
    raised = jnp.exp(logits - jnp.max(logits, axis=0, keepdims=True))
    mix_ref[...] = (raised / jnp.sum(raised, axis=0, keepdims=True)).astype(BF16)
    for copy in copies:
        copy.wait()


def chip_sum_kernel(keep_ref, stats_ref, came_ref, out_ref):
    half = keep_ref.shape[1]
    experts, chips, rows, _ = out_ref.shape
    top, total = stats_ref[:, 0:1], stats_ref[:, 1:2]
    came_top, came_total = read_stats(came_ref[:, half:].astype(F32))
    new_top = jnp.maximum(top, came_top)
    scale, came_scale = jnp.exp(top - new_top), jnp.exp(came_top - new_top)
    sums = (keep_ref[...] * scale + came_ref[:, :half].astype(F32) * came_scale).astype(BF16)
    tile = stats_tile(new_top, total * scale + came_total * came_scale).astype(BF16)
    sums = sums.reshape(experts, rows, half)
    tile = tile.reshape(experts, rows, LANES)
    for chip in range(chips):
        out_ref[:, chip, :, :half] = sums
        out_ref[:, chip, :, half:] = tile


def slot_inputs_of(ref):
    seqs, chips, rows, width = ref.shape
    half = width - LANES
    stats = [read_stats(ref[:, chip, :, half:].astype(F32)) for chip in range(chips)]
    top = functools.reduce(jnp.maximum, [s[0] for s in stats])
    scales = [jnp.exp(s[0] - top) for s in stats]
    total = sum(scale * s[1] for scale, s in zip(scales, stats))
    summed = sum(ref[:, chip, :, :half].astype(F32) * scales[chip] for chip in range(chips))
    return (summed / total).reshape(seqs * rows, half).astype(BF16)


def row_blocks_dot(left, blocks):
    start, total = 0, 0
    for block in blocks:
        rows = block.shape[0]
        total += jnp.dot(left[:, start : start + rows], block[...], preferred_element_type=F32)
        start += rows
    return total


def own_hidden_kernel(
    mine_ref, w_first_ref, w_second_ref, w_in_ref, w_out_ref, acc_ref, near_in, near_out, sem
):
    half = w_in_ref.shape[0] // 2
    rows = near_in.shape[0]
    start = (1 - lax.axis_index("core")) * half + (half - rows)
    _, other = column_halves(half)
    copies = copy_parts(sem, [
        (w_in_ref.at[block_rows(start, rows)], near_in),
        (w_out_ref.at[pl.ds(0, near_out.shape[0]), other], near_out),
    ])
    acc_ref[...] = row_blocks_dot(slot_inputs_of(mine_ref), (w_first_ref, w_second_ref))
    for copy in copies:
        copy.wait()


def send_terms_kernel(
    acc_ref, swapped_ref, w_first_ref, w_second_ref, w_sent_ref, w_out_ref,
    send_ref, hidden_ref, near_kept, rest, sem,
):
    own, other = column_halves(w_out_ref.shape[1] // 2)
    start = w_sent_ref.shape[0]
    copies = copy_parts(sem, [
        (w_out_ref.at[pl.ds(start, rest.shape[0]), other], rest),
        (w_out_ref.at[pl.ds(0, near_kept.shape[0]), own], near_kept),
    ])
    summed = acc_ref[...] + row_blocks_dot(slot_inputs_of(swapped_ref), (w_first_ref, w_second_ref))
    hidden = jax.nn.gelu(summed, approximate=True).astype(BF16)
    hidden_ref[...] = hidden
    sent = jnp.dot(hidden[:, :start], w_sent_ref[...], preferred_element_type=F32)
    copies[0].wait()
    sent += jnp.dot(hidden[:, start:], rest[...], preferred_element_type=F32)
    send_ref[...] = sent.astype(BF16)
    copies[1].wait()


def keep_terms_kernel(hidden_ref, w_kept_ref, w_out_ref, keep_ref, rest, sem):
    own, _ = column_halves(w_out_ref.shape[1] // 2)
    start = w_kept_ref.shape[0]
    copies = copy_parts(sem, [(w_out_ref.at[pl.ds(start, rest.shape[0]), own], rest)])
    kept = jnp.dot(hidden_ref[:, :start], w_kept_ref[...], preferred_element_type=F32)
    copies[0].wait()
    keep_ref[...] = kept + jnp.dot(hidden_ref[:, start:], rest[...], preferred_element_type=F32)


def pair_sum_kernel(keep_ref, came_ref, out_ref):
    seqs, chips, rows, half = out_ref.shape
    sums = (keep_ref[...] + came_ref[...].astype(F32)).astype(BF16).reshape(seqs, rows, half)
    for chip in range(chips):
        out_ref[:, chip] = sums


def mixed_half(mix_ref, ref):
    experts, chips, rows, half = ref.shape
    summed = sum(ref[:, chip].astype(F32) for chip in range(chips))
    slot_outputs = summed.reshape(experts * rows, half).astype(BF16)
    return lax.dot_general(
        mix_ref[...], slot_outputs, (((0,), (0,)), ((), ())), preferred_element_type=F32
    ).astype(BF16)


def own_mix_kernel(mix_ref, mine_ref, half_ref):
    half_ref[...] = mixed_half(mix_ref, mine_ref)


def mix_kernel(mix_ref, swapped_ref, half_ref, out_ref, rest, sem):
    own, other = column_halves(half_ref.shape[1])
    copies = copy_parts(sem, [(half_ref, out_ref.at[:, own])])
    rest[...] = mixed_half(mix_ref, swapped_ref)
    last = pltpu.make_async_copy(rest, out_ref.at[:, other], sem.at[1])
    last.start()
    copies[0].wait()
    last.wait()


def call(kernel, outs, *args, scratch=(), copies=0, in_hbm=(), stay=(), flops=0, limit=8 << 20):
    if copies:
        scratch = tuple(scratch) + (pltpu.SemaphoreType.DMA((copies,)),)
    shapes, out_specs = [], []
    for i, (shape, dtype) in enumerate(outs):
        shapes.append((pltpu.VMEM if i in stay else jax.ShapeDtypeStruct)(shape, dtype))
        out_specs.append(pl.BlockSpec(memory_space=pltpu.VMEM))
    return pl.pallas_call(
        kernel,
        out_shape=shapes,
        in_specs=[
            pl.BlockSpec(memory_space=pltpu.HBM if i in in_hbm else pltpu.VMEM)
            for i in range(len(args))
        ],
        out_specs=out_specs,
        scratch_shapes=list(scratch),
        compiler_params=pltpu.CompilerParams(vmem_limit_bytes=limit),
        cost_estimate=pl.CostEstimate(
            flops=flops,
            bytes_accessed=sum(math.prod(shape) * jnp.dtype(dtype).itemsize for shape, dtype in outs),
            transcendentals=0,
        ),
    )(*[
        pltpu.with_memory_space_constraint(a, pltpu.HBM) if i in in_hbm else a
        for i, a in enumerate(args)
    ])


def share(count, numerator, denominator):
    return max(LANES, count * numerator // denominator // LANES * LANES)


def on_device(tokens, slot_keys, w_in, w_out):
    token_rows, w_in, w_out = tokens[0], w_in[0], w_out[0]
    count, width = token_rows.shape
    half = width // 2
    per_expert = slot_keys.shape[1]
    experts, chips = lax.axis_size("expert"), lax.axis_size("chip")
    slots = experts * per_expert
    units = w_in.shape[1]
    own_rows, other_rows = share(half, 5, 8), share(half, 1, 2)
    sent_rows, kept_rows = share(units, 1, 4), share(units, 1, 3)

    keys = lax.dynamic_slice_in_dim(slot_keys.T, lax.axis_index("core") * half, half, 1)
    keys = jnp.broadcast_to(keys[None], (experts, per_expert, half))
    got = lax.all_to_all(keys, "expert", split_axis=0, concat_axis=0, tiled=True)
    near_tok, w_own_first = call(
        first_fetch_kernel,
        [(token_rows.shape, BF16), ((own_rows, units), BF16)],
        token_rows, w_in,
        copies=2, in_hbm=(0, 1), stay=(0, 1),
    )
    got, near_tok, w_own_first = lax.optimization_barrier((got, near_tok, w_own_first))
    swapped = lax.ppermute(got, "core", SWAP)
    part, w_own_second = call(
        own_logits_kernel,
        [((slots, count), F32), ((half - own_rows, units), BF16)],
        got, near_tok, w_in,
        copies=1, in_hbm=(2,), stay=(1,), flops=2 * slots * count * half,
    )
    logits, weights, stats, send = call(
        send_sums_kernel,
        [
            ((slots, count), F32),
            ((slots, count), BF16),
            ((slots, LANES), F32),
            ((slots, half + LANES), BF16),
        ],
        swapped, part, near_tok,
        flops=4 * slots * count * half,
    )
    came = lax.ppermute(send, "core", SWAP)
    keep, mix, w_other_first = call(
        keep_sums_kernel,
        [((slots, half), F32), ((slots, count), BF16), ((other_rows, units), BF16)],
        logits, weights, near_tok, w_in,
        copies=1, in_hbm=(3,), stay=(2,), flops=2 * slots * count * half,
    )
    (packed,) = call(
        chip_sum_kernel,
        [((experts, chips, per_expert, half + LANES), BF16)],
        keep, stats, came,
        limit=16 << 20,
    )
    both = ("expert", "chip")
    flat = packed.reshape((experts * chips,) + packed.shape[2:])
    mine = lax.all_to_all(flat, both, split_axis=0, concat_axis=0, tiled=True)
    swapped = lax.ppermute(mine, "core", SWAP)
    acc, w_other_second, w_sent = call(
        own_hidden_kernel,
        [((slots, units), F32), ((half - other_rows, units), BF16), ((sent_rows, half), BF16)],
        mine.reshape(packed.shape), w_own_first, w_own_second, w_in, w_out,
        copies=2, in_hbm=(3, 4), stay=(1, 2), flops=2 * slots * half * units, limit=16 << 20,
    )
    send, hidden, w_kept = call(
        send_terms_kernel,
        [((slots, half), BF16), ((slots, units), BF16), ((kept_rows, half), BF16)],
        acc, swapped.reshape(packed.shape), w_other_first, w_other_second, w_sent, w_out,
        scratch=[pltpu.VMEM((units - sent_rows, half), BF16)],
        copies=2, in_hbm=(5,), stay=(2,), flops=4 * slots * half * units, limit=16 << 20,
    )
    came = lax.ppermute(send, "core", SWAP)
    (keep,) = call(
        keep_terms_kernel,
        [((slots, half), F32)],
        hidden, w_kept, w_out,
        scratch=[pltpu.VMEM((units - kept_rows, half), BF16)],
        copies=1, in_hbm=(2,), flops=2 * slots * half * units,
    )
    (packed,) = call(
        pair_sum_kernel, [((experts, chips, per_expert, half), BF16)], keep, came, limit=16 << 20
    )
    flat = packed.reshape((experts * chips,) + packed.shape[2:])
    mine = lax.all_to_all(flat, both, split_axis=0, concat_axis=0, tiled=True)
    swapped = lax.ppermute(mine, "core", SWAP)
    (own_half,) = call(
        own_mix_kernel,
        [((count, half), BF16)],
        mix, mine.reshape(packed.shape),
        stay=(0,), flops=2 * slots * count * half, limit=16 << 20,
    )
    mixed = pl.pallas_call(
        mix_kernel,
        out_shape=jax.ShapeDtypeStruct((count, width), BF16),
        in_specs=[pl.BlockSpec(memory_space=pltpu.VMEM)] * 3,
        out_specs=pl.BlockSpec(memory_space=pltpu.HBM),
        scratch_shapes=[pltpu.VMEM((count, half), BF16), pltpu.SemaphoreType.DMA((2,))],
        compiler_params=pltpu.CompilerParams(vmem_limit_bytes=16 << 20),
        cost_estimate=pl.CostEstimate(
            flops=2 * slots * count * half, bytes_accessed=2 * count * width, transcendentals=0
        ),
    )(mix, swapped.reshape(packed.shape), own_half)
    return mixed[None]


def solution(mesh):
    sizes, names = [], []
    for name in mesh.axis_names:
        if name == "seq":
            sizes += [mesh.shape[name] // 2, 2]
            names += ["chip", "core"]
        else:
            sizes.append(mesh.shape[name])
            names.append(name)
    split = Mesh(mesh.devices.reshape(sizes), tuple(names))
    seq = ("chip", "core")
    placed = (
        P("expert", seq, None),
        P(None, "expert"),
        P("expert", None, seq),
        P("expert", seq, None),
    )
    return jax.shard_map(
        on_device, mesh=split, in_specs=placed, out_specs=P("expert", seq, None), check_vma=False
    )
```

time: 59 us -> 59.4 us (level)
  blocking collectives: 42.2 us -> 27.3 us
  starting transfers between devices: 1.13 us -> 8.46 us
  waiting for transfers between devices: 2.53 us -> 6.72 us
  Pallas kernels: 11.9 us -> 14.9 us
  local copies, waits for them, and re-layouts: 0.77 us -> 1.43 us
    all_to_all x1 -> x0, blocking collectives: 14.4 us -> none  [on_device(): lax.all_to_all(keys, 'expert', split_axis=0, concat_axis=0, tiled=True)]
    all_to_all x0 -> x1, starting transfers between devices: none -> 7.31 us  [on_device(): lax.all_to_all(keys, 'expert', split_axis=0, concat_axis=0, tiled=True)]
    all_to_all x0 -> x1, waiting for transfers between devices: none -> 5.49 us  [on_device(): lax.all_to_all(keys, 'expert', split_axis=0, concat_axis=0, tiled=True)]
    pallas_call x8 -> x11, Pallas kernels: 11.9 us -> 14.9 us  [the longest x10 13.8 us: call(): pl.pallas_call(kernel, out_shape=shapes, in_specs=[pl.BlockSpec(memory_sp...]
    ppermute x2, waiting for transfers between devices: 0.99 us -> 0.01 us  [on_device(): came = lax.ppermute(send, 'core', SWAP)]
    broadcast_in_dim x1, local copies, waits for them, and re-layouts: 0.01 us -> 0.67 us  [on_device(): keys = jnp.broadcast_to(keys[None], (experts, per_expert, half))]
  transfers between devices with their start and end apart: 5 -> 6, of which waited for: 2 -> 2; matrix products, arithmetic and copies ran while one was open for 0% -> 0% of each run, Pallas kernels for 10% -> 16%
where the time goes in v3:
time: 59.4 us; the launch traced here: 58.9 us
  blocking collectives  27.3 us (46%)
  Pallas kernels  14.9 us (25%)
  starting transfers between devices  8.46 us (14%)
  waiting for transfers between devices  6.72 us (11%)
  local copies, waits for them, and re-layouts  1.43 us (2%)
    all_to_all x2, blocking collectives, on_device(): mine = lax.all_to_all(flat, both, split_axis=0, concat_axis=0, tiled=True)  27.3 us
    pallas_call x10, Pallas kernels, call(): pl.pallas_call(kernel, out_shape=shapes, in_specs=[pl.BlockSpec(memory_sp...  13.8 us
    all_to_all x1, starting transfers between devices, on_device(): lax.all_to_all(keys, 'expert', split_axis=0, concat_axis=0, tiled=True)  7.31 us
    all_to_all x1, waiting for transfers between devices, on_device(): lax.all_to_all(keys, 'expert', split_axis=0, concat_axis=0, tiled=True)  5.49 us
    ppermute x2, waiting for transfers between devices, on_device(): swapped = lax.ppermute(mine, 'core', SWAP)  1.23 us
  transfers between devices with their start and end apart: 6, of which 2 were waited for; matrix products, arithmetic and copies ran while one was open for 0% of the time, Pallas kernels for 16%

profile of v3, /device:TPU:0, one launch (start us, length us, event | category | flops | bytes accessed | tf_op | source)
XLA Modules:
  0.0 58.9 jit_solution(407103561866348800)
XLA Ops:
  0.0 0.0 copy-start
  0.0 0.8 %copy-done = bf16[2048,8]{0,1:T(8,128)(2,1)S(1)} copy-done((bf16[2048,8]{0,1:T(8,128)(2,1)S(1)}, bf16[2048,8]{0,1:T(8,128)(2,1)}, u32[]{:S(2)}) %copy-start) | copy-done | bytes 32792
  0.8 0.7 %broadcast_in_dim.4 = bf16[8,8,1024]{2,1,0:T(8,128)(2,1)} broadcast(bf16[8,1024]{1,0:T(8,128)(2,1)S(1)} %dynamic-slice_bitcast_fusion), dimensions={1,2} | broadcast | bytes 147456 | tf_op jit(solution)/shard_map/broadcast_in_dim | solution.py:268
  1.4 7.3 %all-to-all-start = ((bf16[8,8,1024]{2,1,0:T(8,128)(2,1)}), bf16[8,8,1024]{2,1,0:T(8,128)(2,1)S(1)}, u32[]{:S(2)}, u32[]{:S(2)}) async-start(bf16[8,8,1024]{2,1,0:T(8,128)(2,1)} %broadcast_in_dim.4), calls=%async_computation | async-start | bytes 262144 | tf_op jit(solution)/shard_map/all_to_all | solution.py:269
  8.7 1.9 %shard_map.46 = (bf16[224,2048]{1,0:T(8,128)(2,1)S(1)}, bf16[640,1536]{1,0:T(8,128)(2,1)S(1)}) custom-call(bf16[224,2048]{1,0:T(8,128)(2,1)} %bitcast.25, bf16[2048,1536]{1,0:T(8,128)(2,1)} %bitcast.18), custom_call_target="tpu_custom_call" | custom-call | bytes 2883584 | tf_op jit(solution)/shard_map/pallas_call | solution.py:231
  10.6 5.5 %all-to-all-done.got_ref = bf16[8,8,1024]{2,1,0:T(8,128)(2,1)S(1)} async-done(((bf16[8,8,1024]{2,1,0:T(8,128)(2,1)}), bf16[8,8,1024]{2,1,0:T(8,128)(2,1)S(1)}, u32[]{:S(2)}, u32[]{:S(2)}) %all-to-all-start) | async-done | bytes 131104 | tf_op jit(solution)/shard_map/all_to_all | solution.py:269
  16.1 0.0 collective-permute-start
  16.1 1.4 %shard_map.47 = (f32[64,224]{1,0:T(8,128)S(1)}, bf16[384,1536]{1,0:T(8,128)(2,1)S(1)}) custom-call(bf16[8,8,1024]{2,1,0:T(8,128)(2,1)S(1)} %all-to-all-done.got_ref, bf16[224,2048]{1,0:T(8,128)(2,1)S(1)} %get-tuple-element.28.tok_ref, bf16[2048,1536]{1,0:T(8,128)(2,1)} %bitcast.19), custom_call_target="tpu_custom_call" | custom-call | flops 29360128 | bytes 1236992 | tf_op jit(solution)/shard_map/pallas_call | solution.py:231
  17.5 0.0 collective-permute-done.swapped_ref
  17.5 0.6 %shard_map.48 = (f32[64,224]{1,0:T(8,128)S(1)}, bf16[64,224]{1,0:T(8,128)(2,1)S(1)}, f32[64,128]{1,0:T(8,128)S(1)}, bf16[64,1152]{1,0:T(8,128)(2,1)S(1)}) custom-call(bf16[8,8,1024]{2,1,0:T(8,128)(2,1)S(1)} %collective-permute-done.swapped_ref, f32[64,224]{1,0:T(8,128)S(1)} %get-tuple-element.29.part_ref, bf16[224,2048]{1,0:T(8,128)(2,1)S(1)} %get-tuple-element.28.tok_ref), custom_call_target="tpu_custom_call" | custom-call | flops 58720256 | bytes 266240 | tf_op jit(solution)/shard_map/pallas_call | solution.py:231
  18.1 0.6 collective-permute-start.1
  18.7 1.5 %shard_map.49 = (f32[64,1024]{1,0:T(8,128)S(1)}, bf16[64,224]{1,0:T(8,128)(2,1)S(1)}, bf16[512,1536]{1,0:T(8,128)(2,1)S(1)}) custom-call(f32[64,224]{1,0:T(8,128)S(1)} %get-tuple-element.30.logits_ref, bf16[64,224]{1,0:T(8,128)(2,1)S(1)} %get-tuple-element.31.weights_ref, bf16[224,2048]{1,0:T(8,128)(2,1)S(1)} %get-tuple-element.28.tok_ref, ...), custom_call_target="tpu_custom_call" | custom-call | flops 29360128 | bytes 1863680 | tf_op jit(solution)/shard_map/pallas_call | solution.py:231
  20.2 0.0 collective-permute-done.1.came_ref
  20.2 0.3 shard_map.50
  20.6 14.1 %all_to_all.15 = bf16[16,8,1152]{2,1,0:T(8,128)(2,1)S(1)} all-to-all(bf16[16,8,1152]{2,1,0:T(8,128)(2,1)S(1)} %bitcast.12), channel_id=1, replica_groups=mesh['chip'=2,'core'=2,'expert'=8] {'expert','chip'}, dimensions={0} | all-to-all | bytes 589824 | tf_op jit(solution)/shard_map/all_to_all | solution.py:310
  34.6 0.0 collective-permute-start.2
  34.6 2.4 %shard_map.51 = (f32[64,1536]{1,0:T(8,128)S(1)}, bf16[512,1536]{1,0:T(8,128)(2,1)S(1)}, bf16[384,1024]{1,0:T(8,128)(2,1)S(1)}) custom-call(bf16[8,2,8,1152]{3,2,1,0:T(8,128)(2,1)S(1)} %bitcast.13, bf16[640,1536]{1,0:T(8,128)(2,1)S(1)} %get-tuple-element.36.w_first_ref, bf16[384,1536]{1,0:T(8,128)(2,1)S(1)} %get-tuple-element.37.w_second_ref, ...), custom_call_target="tpu_custom_call" | custom-call | flops 201326592 | bytes 2752512 | tf_op jit(solution)/shard_map/pallas_call | solution.py:231
  37.0 0.0 collective-permute-done.2
  37.0 3.1 %shard_map.52 = (bf16[64,1024]{1,0:T(8,128)(2,1)S(1)}, bf16[64,1536]{1,0:T(8,128)(2,1)S(1)}, bf16[512,1024]{1,0:T(8,128)(2,1)S(1)}) custom-call(f32[64,1536]{1,0:T(8,128)S(1)} %get-tuple-element.38.acc_ref, bf16[8,2,8,1152]{3,2,1,0:T(8,128)(2,1)S(1)} %bitcast.16, bf16[512,1536]{1,0:T(8,128)(2,1)S(1)} %get-tuple-element.39.w_first_ref, ...), custom_call_target="tpu_custom_call" | custom-call | flops 402653184 | bytes 1376256 | tf_op jit(solution)/shard_map/pallas_call | solution.py:231
  40.1 0.6 collective-permute-start.3
  40.7 2.3 %shard_map.53.keep_ref = f32[64,1024]{1,0:T(8,128)S(1)} custom-call(bf16[64,1536]{1,0:T(8,128)(2,1)S(1)} %get-tuple-element.42.hidden_ref, bf16[512,1024]{1,0:T(8,128)(2,1)S(1)} %get-tuple-element.43.w_kept_ref, bf16[1536,2048]{1,0:T(8,128)(2,1)} %bitcast.24), custom_call_target="tpu_custom_call" | custom-call | flops 201326592 | bytes 262144 | tf_op jit(solution)/shard_map/pallas_call | solution.py:231
  43.0 0.0 collective-permute-done.3.came_ref
  43.0 13.3 %all_to_all.16 = bf16[16,8,1024]{2,1,0:T(8,128)(2,1)S(1)} all-to-all(bf16[16,8,1024]{2,1,0:T(8,128)(2,1)S(1)} %bitcast.15), channel_id=1, replica_groups=mesh['chip'=2,'core'=2,'expert'=8] {'expert','chip'}, dimensions={0} | all-to-all | bytes 524288 | tf_op jit(solution)/shard_map/all_to_all | solution.py:337
  56.3 0.0 collective-permute-start.4
  56.3 0.3 shard_map.55.half_ref
  56.6 1.2 %collective-permute-done.4 = bf16[16,8,1024]{2,1,0:T(8,128)(2,1)S(1)} collective-permute-done((bf16[16,8,1024]{2,1,0:T(8,128)(2,1)S(1)}, bf16[16,8,1024]{2,1,0:T(8,128)(2,1)S(1)}, u32[]{:S(2)}, u32[]{:S(2)}) %collective-permute-start.4) | collective-permute-done | bytes 262176 | tf_op jit(solution)/shard_map/ppermute | solution.py:338
  57.8 1.1 %shard_map.56 = bf16[224,2048]{1,0:T(8,128)(2,1)} custom-call(bf16[64,224]{1,0:T(8,128)(2,1)S(1)} %get-tuple-element.32.mix_ref, bf16[8,2,8,1024]{3,2,1,0:T(8,128)(2,1)S(1)} %bitcast.17, bf16[224,1024]{1,0:T(8,128)(2,1)S(1)} %shard_map.55.half_ref), custom_call_target="tpu_custom_call" | custom-call | flops 29360128 | bytes 917504 | tf_op jit(solution)/shard_map/pallas_call | solution.py:345
  (2 shorter events, 0.0 us)
Async XLA Ops:
  0.0 0.8 %copy-start = (bf16[2048,8]{0,1:T(8,128)(2,1)S(1)}, bf16[2048,8]{0,1:T(8,128)(2,1)}, u32[]{:S(2)}) copy-start(bf16[2048,8]{0,1:T(8,128)(2,1)} %param.5) | copy-start | bytes 98308
  1.4 14.7 %all-to-all-start = ((bf16[8,8,1024]{2,1,0:T(8,128)(2,1)}), bf16[8,8,1024]{2,1,0:T(8,128)(2,1)S(1)}, u32[]{:S(2)}, u32[]{:S(2)}) async-start(bf16[8,8,1024]{2,1,0:T(8,128)(2,1)} %broadcast_in_dim.4), calls=%async_computation | async-start | bytes 262144 | tf_op jit(solution)/shard_map/all_to_all | solution.py:269
  16.1 1.4 %collective-permute-start = (bf16[8,8,1024]{2,1,0:T(8,128)(2,1)S(1)}, bf16[8,8,1024]{2,1,0:T(8,128)(2,1)S(1)}, u32[]{:S(2)}, u32[]{:S(2)}) collective-permute-start(bf16[8,8,1024]{2,1,0:T(8,128)(2,1)S(1)} %all-to-all-done.got_ref), channel_id=1, source_target_pairs={{0,8},{8,0},{1,9},{9,1},{2,10},{10,2},{3,11},{11,3},{4,12},{12,4},... | collective-permute-start | bytes 393224 | tf_op jit(solution)/shard_map/ppermute | solution.py:277
  18.1 2.1 %collective-permute-start.1 = (bf16[64,1152]{1,0:T(8,128)(2,1)S(1)}, bf16[64,1152]{1,0:T(8,128)(2,1)S(1)}, u32[]{:S(2)}, u32[]{:S(2)}) collective-permute-start(bf16[64,1152]{1,0:T(8,128)(2,1)S(1)} %get-tuple-element.35), channel_id=1, source_target_pairs={{0,8},{8,0},{1,9},{9,1},{2,10},{10,2},{3,11},{11,3},{4,12},{12,4},... | collective-permute-start | bytes 442376 | tf_op jit(solution)/shard_map/ppermute | solution.py:295
  34.6 2.4 %collective-permute-start.2 = (bf16[16,8,1152]{2,1,0:T(8,128)(2,1)S(1)}, bf16[16,8,1152]{2,1,0:T(8,128)(2,1)S(1)}, u32[]{:S(2)}, u32[]{:S(2)}) collective-permute-start(bf16[16,8,1152]{2,1,0:T(8,128)(2,1)S(1)} %all_to_all.15), channel_id=1, source_target_pairs={{0,8},{8,0},{1,9},{9,1},{2,10},{10,2},{3,11},{11,3},{4,12},{12,4},... | collective-permute-start | bytes 884744 | tf_op jit(solution)/shard_map/ppermute | solution.py:311
  40.1 2.9 %collective-permute-start.3 = (bf16[64,1024]{1,0:T(8,128)(2,1)S(1)}, bf16[64,1024]{1,0:T(8,128)(2,1)S(1)}, u32[]{:S(2)}, u32[]{:S(2)}) collective-permute-start(bf16[64,1024]{1,0:T(8,128)(2,1)S(1)} %get-tuple-element.44), channel_id=1, source_target_pairs={{0,8},{8,0},{1,9},{9,1},{2,10},{10,2},{3,11},{11,3},{4,12},{12,4},... | collective-permute-start | bytes 393224 | tf_op jit(solution)/shard_map/ppermute | solution.py:325
  56.3 1.5 %collective-permute-start.4 = (bf16[16,8,1024]{2,1,0:T(8,128)(2,1)S(1)}, bf16[16,8,1024]{2,1,0:T(8,128)(2,1)S(1)}, u32[]{:S(2)}, u32[]{:S(2)}) collective-permute-start(bf16[16,8,1024]{2,1,0:T(8,128)(2,1)S(1)} %all_to_all.16), channel_id=1, source_target_pairs={{0,8},{8,0},{1,9},{9,1},{2,10},{10,2},{3,11},{11,3},{4,12},{12,4},... | collective-permute-start | bytes 786440 | tf_op jit(solution)/shard_map/ppermute | solution.py:338

commit v4 on v3

--- a/solution.py
+++ b/solution.py
@@ -64,12 +64,15 @@
         copy.wait()
 
 
-def own_logits_kernel(got_ref, tok_ref, w_in_ref, part_ref, near_w, sem):
+def own_logits_kernel(got_ref, tok_ref, w_in_ref, part_ref, near_own, near_other, sem):
     slots = part_ref.shape[0]
     half = got_ref.shape[2]
-    rows = near_w.shape[0]
-    start = lax.axis_index("core") * half + (half - rows)
-    copies = copy_parts(sem, [(w_in_ref.at[block_rows(start, rows)], near_w)])
+    core = lax.axis_index("core")
+    rows = near_own.shape[0]
+    copies = copy_parts(sem, [
+        (w_in_ref.at[block_rows(core * half + (half - rows), rows)], near_own),
+        (w_in_ref.at[block_rows((1 - core) * half, near_other.shape[0])], near_other),
+    ])
     own, _ = column_halves(half)
     part_ref[...] = lax.dot_general(
         got_ref[...].reshape(slots, half), tok_ref[:, own], ROWS_BY_ROWS, preferred_element_type=F32
@@ -97,9 +100,11 @@
     stats_ref[...] = jnp.where(lane == 0, top, total)
 
 
-def keep_sums_kernel(logits_ref, weights_ref, tok_ref, w_in_ref, keep_ref, mix_ref, near_w, sem):
+def keep_sums_kernel(
+    skip, logits_ref, weights_ref, tok_ref, w_in_ref, keep_ref, mix_ref, near_w, sem
+):
     half = keep_ref.shape[1]
-    start = (1 - lax.axis_index("core")) * half
+    start = (1 - lax.axis_index("core")) * half + skip
     copies = copy_parts(sem, [(w_in_ref.at[block_rows(start, near_w.shape[0])], near_w)])
     own, _ = column_halves(half)
     keep_ref[...] = jnp.dot(weights_ref[...], tok_ref[:, own], preferred_element_type=F32)
@@ -152,10 +157,9 @@
     half = w_in_ref.shape[0] // 2
     rows = near_in.shape[0]
     start = (1 - lax.axis_index("core")) * half + (half - rows)
-    _, other = column_halves(half)
     copies = copy_parts(sem, [
         (w_in_ref.at[block_rows(start, rows)], near_in),
-        (w_out_ref.at[pl.ds(0, near_out.shape[0]), other], near_out),
+        (w_out_ref.at[pl.ds(0, near_out.shape[0])], near_out),
     ])
     acc_ref[...] = row_blocks_dot(slot_inputs_of(mine_ref), (w_first_ref, w_second_ref))
     for copy in copies:
@@ -163,32 +167,37 @@
 
 
 def send_terms_kernel(
-    acc_ref, swapped_ref, w_first_ref, w_second_ref, w_sent_ref, w_out_ref,
-    send_ref, hidden_ref, near_kept, rest, sem,
+    acc_ref, swapped_ref, w_first_ref, w_second_ref, w_third_ref, w_near_ref, w_out_ref,
+    send_ref, hidden_ref, rest, sem,
 ):
-    own, other = column_halves(w_out_ref.shape[1] // 2)
-    start = w_sent_ref.shape[0]
+    _, other = column_halves(w_out_ref.shape[1] // 2)
+    near, pieces = w_near_ref.shape[0], sem.shape[0]
+    step = rest.shape[0] // pieces
     copies = copy_parts(sem, [
-        (w_out_ref.at[pl.ds(start, rest.shape[0]), other], rest),
-        (w_out_ref.at[pl.ds(0, near_kept.shape[0]), own], near_kept),
+        (w_out_ref.at[pl.ds(near + i * step, step)], rest.at[pl.ds(i * step, step)])
+        for i in range(pieces)
     ])
-    summed = acc_ref[...] + row_blocks_dot(slot_inputs_of(swapped_ref), (w_first_ref, w_second_ref))
+    summed = acc_ref[...] + row_blocks_dot(
+        slot_inputs_of(swapped_ref), (w_first_ref, w_second_ref, w_third_ref)
+    )
     hidden = jax.nn.gelu(summed, approximate=True).astype(BF16)
     hidden_ref[...] = hidden
-    sent = jnp.dot(hidden[:, :start], w_sent_ref[...], preferred_element_type=F32)
-    copies[0].wait()
-    sent += jnp.dot(hidden[:, start:], rest[...], preferred_element_type=F32)
+    sent = jnp.dot(hidden[:, :near], w_near_ref[:, other], preferred_element_type=F32)
+    for i, copy in enumerate(copies):
+        copy.wait()
+        rows = pl.ds(near + i * step, step)
+        sent += jnp.dot(
+            hidden_ref[:, rows], rest[pl.ds(i * step, step), other], preferred_element_type=F32
+        )
     send_ref[...] = sent.astype(BF16)
-    copies[1].wait()
-
-
-def keep_terms_kernel(hidden_ref, w_kept_ref, w_out_ref, keep_ref, rest, sem):
-    own, _ = column_halves(w_out_ref.shape[1] // 2)
-    start = w_kept_ref.shape[0]
-    copies = copy_parts(sem, [(w_out_ref.at[pl.ds(start, rest.shape[0]), own], rest)])
-    kept = jnp.dot(hidden_ref[:, :start], w_kept_ref[...], preferred_element_type=F32)
-    copies[0].wait()
-    keep_ref[...] = kept + jnp.dot(hidden_ref[:, start:], rest[...], preferred_element_type=F32)
+
+
+def keep_terms_kernel(hidden_ref, w_near_ref, w_rest_ref, keep_ref):
+    own, _ = column_halves(keep_ref.shape[1])
+    near = w_near_ref.shape[0]
+    keep_ref[...] = jnp.dot(
+        hidden_ref[:, :near], w_near_ref[:, own], preferred_element_type=F32
+    ) + jnp.dot(hidden_ref[:, near:], w_rest_ref[:, own], preferred_element_type=F32)
 
 
 def pair_sum_kernel(keep_ref, came_ref, out_ref):
@@ -261,8 +270,9 @@
     experts, chips = lax.axis_size("expert"), lax.axis_size("chip")
     slots = experts * per_expert
     units = w_in.shape[1]
-    own_rows, other_rows = share(half, 5, 8), share(half, 1, 2)
-    sent_rows, kept_rows = share(units, 1, 4), share(units, 1, 3)
+    own_rows = share(half, 3, 4)
+    other_rows = (share(half, 1, 4), share(half, 1, 2), half - share(half, 1, 4) - share(half, 1, 2))
+    near_units = share(units, 1, 6)
 
     keys = lax.dynamic_slice_in_dim(slot_keys.T, lax.axis_index("core") * half, half, 1)
     keys = jnp.broadcast_to(keys[None], (experts, per_expert, half))
@@ -275,11 +285,15 @@
     )
     got, near_tok, w_own_first = lax.optimization_barrier((got, near_tok, w_own_first))
     swapped = lax.ppermute(got, "core", SWAP)
-    part, w_own_second = call(
+    part, w_own_second, w_other_first = call(
         own_logits_kernel,
-        [((slots, count), F32), ((half - own_rows, units), BF16)],
+        [
+            ((slots, count), F32),
+            ((half - own_rows, units), BF16),
+            ((other_rows[0], units), BF16),
+        ],
         got, near_tok, w_in,
-        copies=1, in_hbm=(2,), stay=(1,), flops=2 * slots * count * half,
+        copies=2, in_hbm=(2,), stay=(1, 2), flops=2 * slots * count * half,
     )
     logits, weights, stats, send = call(
         send_sums_kernel,
@@ -293,9 +307,9 @@
         flops=4 * slots * count * half,
     )
     came = lax.ppermute(send, "core", SWAP)
-    keep, mix, w_other_first = call(
-        keep_sums_kernel,
-        [((slots, half), F32), ((slots, count), BF16), ((other_rows, units), BF16)],
+    keep, mix, w_other_second = call(
+        functools.partial(keep_sums_kernel, other_rows[0]),
+        [((slots, half), F32), ((slots, count), BF16), ((other_rows[1], units), BF16)],
         logits, weights, near_tok, w_in,
         copies=1, in_hbm=(3,), stay=(2,), flops=2 * slots * count * half,
     )
@@ -309,26 +323,26 @@
     flat = packed.reshape((experts * chips,) + packed.shape[2:])
     mine = lax.all_to_all(flat, both, split_axis=0, concat_axis=0, tiled=True)
     swapped = lax.ppermute(mine, "core", SWAP)
-    acc, w_other_second, w_sent = call(
+    acc, w_other_third, w_near = call(
         own_hidden_kernel,
-        [((slots, units), F32), ((half - other_rows, units), BF16), ((sent_rows, half), BF16)],
+        [((slots, units), F32), ((other_rows[2], units), BF16), ((near_units, width), BF16)],
         mine.reshape(packed.shape), w_own_first, w_own_second, w_in, w_out,
         copies=2, in_hbm=(3, 4), stay=(1, 2), flops=2 * slots * half * units, limit=16 << 20,
     )
-    send, hidden, w_kept = call(
+    w_other = (w_other_first, w_other_second, w_other_third)
+    pieces = math.gcd((units - near_units) // LANES, 5)
+    send, hidden, w_rest = call(
         send_terms_kernel,
-        [((slots, half), BF16), ((slots, units), BF16), ((kept_rows, half), BF16)],
-        acc, swapped.reshape(packed.shape), w_other_first, w_other_second, w_sent, w_out,
-        scratch=[pltpu.VMEM((units - sent_rows, half), BF16)],
-        copies=2, in_hbm=(5,), stay=(2,), flops=4 * slots * half * units, limit=16 << 20,
+        [((slots, half), BF16), ((slots, units), BF16), ((units - near_units, width), BF16)],
+        acc, swapped.reshape(packed.shape), *w_other, w_near, w_out,
+        copies=pieces, in_hbm=(6,), stay=(2,), flops=4 * slots * half * units, limit=16 << 20,
     )
     came = lax.ppermute(send, "core", SWAP)
     (keep,) = call(
         keep_terms_kernel,
         [((slots, half), F32)],
-        hidden, w_kept, w_out,
-        scratch=[pltpu.VMEM((units - kept_rows, half), BF16)],
-        copies=1, in_hbm=(2,), flops=2 * slots * half * units,
+        hidden, w_near, w_rest,
+        flops=2 * slots * half * units,
     )
     (packed,) = call(
         pair_sum_kernel, [((experts, chips, per_expert, half), BF16)], keep, came, limit=16 << 20

time: 59.4 us -> 57.9 us (0.975)
  Pallas kernels: 14.9 us -> 12.8 us
    pallas_call x10, Pallas kernels: 13.8 us -> 11.7 us  [call(): pl.pallas_call(kernel, out_shape=shapes, in_specs=[pl.BlockSpec(memory_sp...]
  transfers between devices with their start and end apart: 6 -> 6, of which waited for: 2 -> 3; matrix products, arithmetic and copies ran while one was open for 0% -> 0% of each run, Pallas kernels for 16% -> 13%
where the time goes in v4:
time: 57.9 us; the launch traced here: 57.5 us
  blocking collectives  27.7 us (48%)
  Pallas kernels  12.8 us (22%)
  starting transfers between devices  8.47 us (15%)
  waiting for transfers between devices  6.93 us (12%)
  local copies, waits for them, and re-layouts  1.43 us (2%)
    all_to_all x2, blocking collectives, on_device(): mine = lax.all_to_all(flat, both, split_axis=0, concat_axis=0, tiled=True)  27.7 us
    pallas_call x10, Pallas kernels, call(): pl.pallas_call(kernel, out_shape=shapes, in_specs=[pl.BlockSpec(memory_sp...  11.7 us
    all_to_all x1, starting transfers between devices, on_device(): lax.all_to_all(keys, 'expert', split_axis=0, concat_axis=0, tiled=True)  7.31 us
    all_to_all x1, waiting for transfers between devices, on_device(): lax.all_to_all(keys, 'expert', split_axis=0, concat_axis=0, tiled=True)  5.37 us
    ppermute x2, waiting for transfers between devices, on_device(): swapped = lax.ppermute(mine, 'core', SWAP)  1.23 us
  transfers between devices with their start and end apart: 6, of which 3 were waited for; matrix products, arithmetic and copies ran while one was open for 0% of the time, Pallas kernels for 13%

profile of v4, /device:TPU:0, one launch (start us, length us, event | category | flops | bytes accessed | tf_op | source)
XLA Modules:
  0.0 57.5 jit_solution(14012877914802791206)
XLA Ops:
  0.0 0.0 copy-start
  0.0 0.8 %copy-done = bf16[2048,8]{0,1:T(8,128)(2,1)S(1)} copy-done((bf16[2048,8]{0,1:T(8,128)(2,1)S(1)}, bf16[2048,8]{0,1:T(8,128)(2,1)}, u32[]{:S(2)}) %copy-start) | copy-done | bytes 32792
  0.8 0.7 %broadcast_in_dim.4 = bf16[8,8,1024]{2,1,0:T(8,128)(2,1)} broadcast(bf16[8,1024]{1,0:T(8,128)(2,1)S(1)} %dynamic-slice_bitcast_fusion), dimensions={1,2} | broadcast | bytes 147456 | tf_op jit(solution)/shard_map/broadcast_in_dim | solution.py:278
  1.4 7.3 %all-to-all-start = ((bf16[8,8,1024]{2,1,0:T(8,128)(2,1)}), bf16[8,8,1024]{2,1,0:T(8,128)(2,1)S(1)}, u32[]{:S(2)}, u32[]{:S(2)}) async-start(bf16[8,8,1024]{2,1,0:T(8,128)(2,1)} %broadcast_in_dim.4), calls=%async_computation | async-start | bytes 262144 | tf_op jit(solution)/shard_map/all_to_all | solution.py:279
  8.7 2.0 %shard_map.46 = (bf16[224,2048]{1,0:T(8,128)(2,1)S(1)}, bf16[768,1536]{1,0:T(8,128)(2,1)S(1)}) custom-call(bf16[224,2048]{1,0:T(8,128)(2,1)} %bitcast.24, bf16[2048,1536]{1,0:T(8,128)(2,1)} %bitcast.18), custom_call_target="tpu_custom_call" | custom-call | bytes 3276800 | tf_op jit(solution)/shard_map/pallas_call | solution.py:240
  10.7 5.4 %all-to-all-done.got_ref = bf16[8,8,1024]{2,1,0:T(8,128)(2,1)S(1)} async-done(((bf16[8,8,1024]{2,1,0:T(8,128)(2,1)}), bf16[8,8,1024]{2,1,0:T(8,128)(2,1)S(1)}, u32[]{:S(2)}, u32[]{:S(2)}) %all-to-all-start) | async-done | bytes 131104 | tf_op jit(solution)/shard_map/all_to_all | solution.py:279
  16.1 0.0 collective-permute-start
  16.1 1.5 %shard_map.47 = (f32[64,224]{1,0:T(8,128)S(1)}, bf16[256,1536]{1,0:T(8,128)(2,1)S(1)}, bf16[256,1536]{1,0:T(8,128)(2,1)S(1)}) custom-call(bf16[8,8,1024]{2,1,0:T(8,128)(2,1)S(1)} %all-to-all-done.got_ref, bf16[224,2048]{1,0:T(8,128)(2,1)S(1)} %get-tuple-element.29.tok_ref, bf16[2048,1536]{1,0:T(8,128)(2,1)} %bitcast.19), custom_call_target="tpu_custom_call" | custom-call | flops 29360128 | bytes 1630208 | tf_op jit(solution)/shard_map/pallas_call | solution.py:240
  17.6 0.0 collective-permute-done.swapped_ref
  17.6 0.6 %shard_map.48 = (f32[64,224]{1,0:T(8,128)S(1)}, bf16[64,224]{1,0:T(8,128)(2,1)S(1)}, f32[64,128]{1,0:T(8,128)S(1)}, bf16[64,1152]{1,0:T(8,128)(2,1)S(1)}) custom-call(bf16[8,8,1024]{2,1,0:T(8,128)(2,1)S(1)} %collective-permute-done.swapped_ref, f32[64,224]{1,0:T(8,128)S(1)} %get-tuple-element.30.part_ref, bf16[224,2048]{1,0:T(8,128)(2,1)S(1)} %get-tuple-element.29.tok_ref), custom_call_target="tpu_custom_call" | custom-call | flops 58720256 | bytes 266240 | tf_op jit(solution)/shard_map/pallas_call | solution.py:240
  18.2 0.6 collective-permute-start.1
  18.8 1.5 %shard_map.49 = (f32[64,1024]{1,0:T(8,128)S(1)}, bf16[64,224]{1,0:T(8,128)(2,1)S(1)}, bf16[512,1536]{1,0:T(8,128)(2,1)S(1)}) custom-call(f32[64,224]{1,0:T(8,128)S(1)} %get-tuple-element.31.logits_ref, bf16[64,224]{1,0:T(8,128)(2,1)S(1)} %get-tuple-element.32.weights_ref, bf16[224,2048]{1,0:T(8,128)(2,1)S(1)} %get-tuple-element.29.tok_ref, ...), custom_call_target="tpu_custom_call" | custom-call | flops 29360128 | bytes 1863680 | tf_op jit(solution)/shard_map/pallas_call | solution.py:240
  20.3 0.0 collective-permute-done.1.came_ref
  20.3 0.3 shard_map.50
  20.6 14.1 %all_to_all.15 = bf16[16,8,1152]{2,1,0:T(8,128)(2,1)S(1)} all-to-all(bf16[16,8,1152]{2,1,0:T(8,128)(2,1)S(1)} %bitcast.12), channel_id=1, replica_groups=mesh['chip'=2,'core'=2,'expert'=8] {'expert','chip'}, dimensions={0} | all-to-all | bytes 589824 | tf_op jit(solution)/shard_map/all_to_all | solution.py:324
  34.7 0.0 collective-permute-start.2
  34.7 1.8 %shard_map.51 = (f32[64,1536]{1,0:T(8,128)S(1)}, bf16[256,1536]{1,0:T(8,128)(2,1)S(1)}, bf16[256,2048]{1,0:T(8,128)(2,1)S(1)}) custom-call(bf16[8,2,8,1152]{3,2,1,0:T(8,128)(2,1)S(1)} %bitcast.13, bf16[768,1536]{1,0:T(8,128)(2,1)S(1)} %get-tuple-element.37.w_first_ref, bf16[256,1536]{1,0:T(8,128)(2,1)S(1)} %get-tuple-element.38.w_second_ref, ...), custom_call_target="tpu_custom_call" | custom-call | flops 201326592 | bytes 2228224 | tf_op jit(solution)/shard_map/pallas_call | solution.py:240
  36.5 0.0 collective-permute-done.2
  36.5 3.1 %shard_map.52 = (bf16[64,1024]{1,0:T(8,128)(2,1)S(1)}, bf16[64,1536]{1,0:T(8,128)(2,1)S(1)}, bf16[1280,2048]{1,0:T(8,128)(2,1)S(1)}) custom-call(f32[64,1536]{1,0:T(8,128)S(1)} %get-tuple-element.39.acc_ref, bf16[8,2,8,1152]{3,2,1,0:T(8,128)(2,1)S(1)} %bitcast.16, bf16[256,1536]{1,0:T(8,128)(2,1)S(1)} %get-tuple-element.40.w_first_ref, ...), custom_call_target="tpu_custom_call" | custom-call | flops 402653184 | bytes 5570560 | tf_op jit(solution)/shard_map/pallas_call | solution.py:240
  39.6 0.6 %collective-permute-start.3 = (bf16[64,1024]{1,0:T(8,128)(2,1)S(1)}, bf16[64,1024]{1,0:T(8,128)(2,1)S(1)}, u32[]{:S(2)}, u32[]{:S(2)}) collective-permute-start(bf16[64,1024]{1,0:T(8,128)(2,1)S(1)} %get-tuple-element.46), channel_id=1, source_target_pairs={{0,8},{8,0},{1,9},{9,1},{2,10},{10,2},{3,11},{11,3},{4,12},{12,4},... | collective-permute-start | bytes 393224 | tf_op jit(solution)/shard_map/ppermute | solution.py:340
  40.2 0.7 %shard_map.53.keep_ref = f32[64,1024]{1,0:T(8,128)S(1)} custom-call(bf16[64,1536]{1,0:T(8,128)(2,1)S(1)} %get-tuple-element.44.hidden_ref, bf16[256,2048]{1,0:T(8,128)(2,1)S(1)} %get-tuple-element.43.w_near_ref, bf16[1280,2048]{1,0:T(8,128)(2,1)S(1)} %get-tuple-element.45.w_rest_ref), custom_call_target="tpu_custom_call" | custom-call | flops 201326592 | bytes 262144 | tf_op jit(solution)/shard_map/pallas_call | solution.py:240
  40.8 0.3 collective-permute-done.3.came_ref
  41.2 13.6 %all_to_all.16 = bf16[16,8,1024]{2,1,0:T(8,128)(2,1)S(1)} all-to-all(bf16[16,8,1024]{2,1,0:T(8,128)(2,1)S(1)} %bitcast.15), channel_id=1, replica_groups=mesh['chip'=2,'core'=2,'expert'=8] {'expert','chip'}, dimensions={0} | all-to-all | bytes 524288 | tf_op jit(solution)/shard_map/all_to_all | solution.py:351
  54.8 0.0 collective-permute-start.4
  54.8 0.3 shard_map.55.half_ref
  55.1 1.2 %collective-permute-done.4 = bf16[16,8,1024]{2,1,0:T(8,128)(2,1)S(1)} collective-permute-done((bf16[16,8,1024]{2,1,0:T(8,128)(2,1)S(1)}, bf16[16,8,1024]{2,1,0:T(8,128)(2,1)S(1)}, u32[]{:S(2)}, u32[]{:S(2)}) %collective-permute-start.4) | collective-permute-done | bytes 262176 | tf_op jit(solution)/shard_map/ppermute | solution.py:352
  56.4 1.1 %shard_map.56 = bf16[224,2048]{1,0:T(8,128)(2,1)} custom-call(bf16[64,224]{1,0:T(8,128)(2,1)S(1)} %get-tuple-element.33.mix_ref, bf16[8,2,8,1024]{3,2,1,0:T(8,128)(2,1)S(1)} %bitcast.17, bf16[224,1024]{1,0:T(8,128)(2,1)S(1)} %shard_map.55.half_ref), custom_call_target="tpu_custom_call" | custom-call | flops 29360128 | bytes 917504 | tf_op jit(solution)/shard_map/pallas_call | solution.py:359
  (2 shorter events, 0.0 us)
Async XLA Ops:
  0.0 0.8 %copy-start = (bf16[2048,8]{0,1:T(8,128)(2,1)S(1)}, bf16[2048,8]{0,1:T(8,128)(2,1)}, u32[]{:S(2)}) copy-start(bf16[2048,8]{0,1:T(8,128)(2,1)} %param.5) | copy-start | bytes 98308
  1.4 14.7 %all-to-all-start = ((bf16[8,8,1024]{2,1,0:T(8,128)(2,1)}), bf16[8,8,1024]{2,1,0:T(8,128)(2,1)S(1)}, u32[]{:S(2)}, u32[]{:S(2)}) async-start(bf16[8,8,1024]{2,1,0:T(8,128)(2,1)} %broadcast_in_dim.4), calls=%async_computation | async-start | bytes 262144 | tf_op jit(solution)/shard_map/all_to_all | solution.py:279
  16.1 1.5 %collective-permute-start = (bf16[8,8,1024]{2,1,0:T(8,128)(2,1)S(1)}, bf16[8,8,1024]{2,1,0:T(8,128)(2,1)S(1)}, u32[]{:S(2)}, u32[]{:S(2)}) collective-permute-start(bf16[8,8,1024]{2,1,0:T(8,128)(2,1)S(1)} %all-to-all-done.got_ref), channel_id=1, source_target_pairs={{0,8},{8,0},{1,9},{9,1},{2,10},{10,2},{3,11},{11,3},{4,12},{12,4},... | collective-permute-start | bytes 393224 | tf_op jit(solution)/shard_map/ppermute | solution.py:287
  18.2 2.1 %collective-permute-start.1 = (bf16[64,1152]{1,0:T(8,128)(2,1)S(1)}, bf16[64,1152]{1,0:T(8,128)(2,1)S(1)}, u32[]{:S(2)}, u32[]{:S(2)}) collective-permute-start(bf16[64,1152]{1,0:T(8,128)(2,1)S(1)} %get-tuple-element.36), channel_id=1, source_target_pairs={{0,8},{8,0},{1,9},{9,1},{2,10},{10,2},{3,11},{11,3},{4,12},{12,4},... | collective-permute-start | bytes 442376 | tf_op jit(solution)/shard_map/ppermute | solution.py:309
  34.7 1.8 %collective-permute-start.2 = (bf16[16,8,1152]{2,1,0:T(8,128)(2,1)S(1)}, bf16[16,8,1152]{2,1,0:T(8,128)(2,1)S(1)}, u32[]{:S(2)}, u32[]{:S(2)}) collective-permute-start(bf16[16,8,1152]{2,1,0:T(8,128)(2,1)S(1)} %all_to_all.15), channel_id=1, source_target_pairs={{0,8},{8,0},{1,9},{9,1},{2,10},{10,2},{3,11},{11,3},{4,12},{12,4},... | collective-permute-start | bytes 884744 | tf_op jit(solution)/shard_map/ppermute | solution.py:325
  39.6 1.6 %collective-permute-start.3 = (bf16[64,1024]{1,0:T(8,128)(2,1)S(1)}, bf16[64,1024]{1,0:T(8,128)(2,1)S(1)}, u32[]{:S(2)}, u32[]{:S(2)}) collective-permute-start(bf16[64,1024]{1,0:T(8,128)(2,1)S(1)} %get-tuple-element.46), channel_id=1, source_target_pairs={{0,8},{8,0},{1,9},{9,1},{2,10},{10,2},{3,11},{11,3},{4,12},{12,4},... | collective-permute-start | bytes 393224 | tf_op jit(solution)/shard_map/ppermute | solution.py:340
  54.8 1.5 %collective-permute-start.4 = (bf16[16,8,1024]{2,1,0:T(8,128)(2,1)S(1)}, bf16[16,8,1024]{2,1,0:T(8,128)(2,1)S(1)}, u32[]{:S(2)}, u32[]{:S(2)}) collective-permute-start(bf16[16,8,1024]{2,1,0:T(8,128)(2,1)S(1)} %all_to_all.16), channel_id=1, source_target_pairs={{0,8},{8,0},{1,9},{9,1},{2,10},{10,2},{3,11},{11,3},{4,12},{12,4},... | collective-permute-start | bytes 786440 | tf_op jit(solution)/shard_map/ppermute | solution.py:352

commit v5 on v4

--- a/solution.py
+++ b/solution.py
@@ -55,40 +55,71 @@
     return pl.ds(pl.multiple_of(start, LANES), count)
 
 
+def held_masks(experts):
+    return [((2 + 2 * k) % experts, experts - 1 - 2 * k) for k in range(experts // 2)]
+
+
+def gather_keys(keys, experts, chips):
+    axes = ("chip", "core", "expert")
+    blocks = []
+    for masks in held_masks(experts):
+        pairs = [
+            (((chip * 2 + core) * experts + e), ((chip * 2 + core) * experts + (e ^ mask)))
+            for chip in range(chips)
+            for core, mask in enumerate(masks)
+            if mask
+            for e in range(experts)
+        ]
+        blocks.append(lax.ppermute(keys, axes, pairs))
+    return blocks
+
+
+def stack_kernel(*refs):
+    keys_ref, *blocks, out_ref = refs
+    for k, block in enumerate(blocks[:-1]):
+        out_ref[k] = block[...]
+    out_ref[len(blocks) - 1] = jnp.where(
+        lax.axis_index("core") == 0, keys_ref[...], blocks[-1][...]
+    )
+
+
 def first_fetch_kernel(tok_ref, w_in_ref, near_tok, near_w, sem):
-    half = w_in_ref.shape[0] // 2
     rows = near_w.shape[0]
-    start = lax.axis_index("core") * half
+    start = lax.axis_index("core") * rows
     pairs = [(tok_ref, near_tok), (w_in_ref.at[block_rows(start, rows)], near_w)]
     for copy in copy_parts(sem, pairs):
         copy.wait()
 
 
-def own_logits_kernel(got_ref, tok_ref, w_in_ref, part_ref, near_own, near_other, sem):
-    slots = part_ref.shape[0]
-    half = got_ref.shape[2]
-    core = lax.axis_index("core")
-    rows = near_own.shape[0]
-    copies = copy_parts(sem, [
-        (w_in_ref.at[block_rows(core * half + (half - rows), rows)], near_own),
-        (w_in_ref.at[block_rows((1 - core) * half, near_other.shape[0])], near_other),
-    ])
-    own, _ = column_halves(half)
-    part_ref[...] = lax.dot_general(
-        got_ref[...].reshape(slots, half), tok_ref[:, own], ROWS_BY_ROWS, preferred_element_type=F32
-    )
+def held_logits(stack_ref, tok_ref):
+    blocks, rows, width = stack_ref.shape
+    return lax.dot_general(
+        stack_ref[...].reshape(blocks * rows, width), tok_ref[...], ROWS_BY_ROWS,
+        preferred_element_type=F32,
+    )
+
+
+def held_logits_kernel(stack_ref, tok_ref, w_in_ref, part_ref, near_w, sem):
+    start = (1 - lax.axis_index("core")) * (w_in_ref.shape[0] // 2)
+    copies = copy_parts(sem, [(w_in_ref.at[block_rows(start, near_w.shape[0])], near_w)])
+    part_ref[...] = held_logits(stack_ref, tok_ref)
     for copy in copies:
         copy.wait()
 
 
-def send_sums_kernel(swapped_ref, part_ref, tok_ref, logits_ref, weights_ref, stats_ref, send_ref):
-    half = swapped_ref.shape[2]
-    slots = part_ref.shape[0]
+def send_sums_kernel(
+    swapped_ref, part_ref, tok_ref, logits_ref, weights_ref, stats_ref, send_ref, sorted_ref
+):
+    half = tok_ref.shape[1] // 2
     _, other = column_halves(half)
-    logits = part_ref[...] + lax.dot_general(
-        swapped_ref[...].reshape(slots, half), tok_ref[:, other], ROWS_BY_ROWS,
-        preferred_element_type=F32,
-    )
+    experts, rows, count = sorted_ref.shape
+    expert, core = lax.axis_index("expert"), lax.axis_index("core")
+    theirs = held_logits(swapped_ref, tok_ref)
+    for k, (even, odd) in enumerate(held_masks(experts)):
+        held = slice(k * rows, (k + 1) * rows)
+        sorted_ref[expert ^ jnp.where(core == 0, even, odd)] = part_ref[held, :]
+        sorted_ref[expert ^ jnp.where(core == 0, odd, even)] = theirs[held, :]
+    logits = sorted_ref[...].reshape(experts * rows, count)
     logits_ref[...] = logits
     top = jnp.max(logits, axis=1, keepdims=True)
     weights = jnp.exp(logits - top).astype(BF16)
@@ -152,22 +183,16 @@
 
 
 def own_hidden_kernel(
-    mine_ref, w_first_ref, w_second_ref, w_in_ref, w_out_ref, acc_ref, near_in, near_out, sem
+    mine_ref, w_own_ref, w_out_ref, acc_ref, near_out, sem
 ):
-    half = w_in_ref.shape[0] // 2
-    rows = near_in.shape[0]
-    start = (1 - lax.axis_index("core")) * half + (half - rows)
-    copies = copy_parts(sem, [
-        (w_in_ref.at[block_rows(start, rows)], near_in),
-        (w_out_ref.at[pl.ds(0, near_out.shape[0])], near_out),
-    ])
-    acc_ref[...] = row_blocks_dot(slot_inputs_of(mine_ref), (w_first_ref, w_second_ref))
+    copies = copy_parts(sem, [(w_out_ref.at[pl.ds(0, near_out.shape[0])], near_out)])
+    acc_ref[...] = row_blocks_dot(slot_inputs_of(mine_ref), (w_own_ref,))
     for copy in copies:
         copy.wait()
 
 
 def send_terms_kernel(
-    acc_ref, swapped_ref, w_first_ref, w_second_ref, w_third_ref, w_near_ref, w_out_ref,
+    acc_ref, swapped_ref, w_first_ref, w_second_ref, w_near_ref, w_out_ref,
     send_ref, hidden_ref, rest, sem,
 ):
     _, other = column_halves(w_out_ref.shape[1] // 2)
@@ -177,9 +202,7 @@
         (w_out_ref.at[pl.ds(near + i * step, step)], rest.at[pl.ds(i * step, step)])
         for i in range(pieces)
     ])
-    summed = acc_ref[...] + row_blocks_dot(
-        slot_inputs_of(swapped_ref), (w_first_ref, w_second_ref, w_third_ref)
-    )
+    summed = acc_ref[...] + row_blocks_dot(slot_inputs_of(swapped_ref), (w_first_ref, w_second_ref))
     hidden = jax.nn.gelu(summed, approximate=True).astype(BF16)
     hidden_ref[...] = hidden
     sent = jnp.dot(hidden[:, :near], w_near_ref[:, other], preferred_element_type=F32)
@@ -270,30 +293,27 @@
     experts, chips = lax.axis_size("expert"), lax.axis_size("chip")
     slots = experts * per_expert
     units = w_in.shape[1]
-    own_rows = share(half, 3, 4)
-    other_rows = (share(half, 1, 4), share(half, 1, 2), half - share(half, 1, 4) - share(half, 1, 2))
-    near_units = share(units, 1, 6)
-
-    keys = lax.dynamic_slice_in_dim(slot_keys.T, lax.axis_index("core") * half, half, 1)
-    keys = jnp.broadcast_to(keys[None], (experts, per_expert, half))
-    got = lax.all_to_all(keys, "expert", split_axis=0, concat_axis=0, tiled=True)
-    near_tok, w_own_first = call(
+    other_rows = share(half, 1, 2)
+    near_units = share(units, 1, 3)
+
+    keys = slot_keys.T
+    blocks = gather_keys(keys, experts, chips)
+    near_tok, w_own = call(
         first_fetch_kernel,
-        [(token_rows.shape, BF16), ((own_rows, units), BF16)],
+        [(token_rows.shape, BF16), ((half, units), BF16)],
         token_rows, w_in,
         copies=2, in_hbm=(0, 1), stay=(0, 1),
     )
-    got, near_tok, w_own_first = lax.optimization_barrier((got, near_tok, w_own_first))
-    swapped = lax.ppermute(got, "core", SWAP)
-    part, w_own_second, w_other_first = call(
-        own_logits_kernel,
-        [
-            ((slots, count), F32),
-            ((half - own_rows, units), BF16),
-            ((other_rows[0], units), BF16),
-        ],
-        got, near_tok, w_in,
-        copies=2, in_hbm=(2,), stay=(1, 2), flops=2 * slots * count * half,
+    *blocks, near_tok, w_own = lax.optimization_barrier((*blocks, near_tok, w_own))
+    (stack,) = call(
+        stack_kernel, [((experts // 2, per_expert, width), BF16)], keys, *blocks
+    )
+    swapped = lax.ppermute(stack, "core", SWAP)
+    part, w_other_first = call(
+        held_logits_kernel,
+        [((slots // 2, count), F32), ((other_rows, units), BF16)],
+        stack, near_tok, w_in,
+        copies=1, in_hbm=(2,), stay=(1,), flops=2 * slots * count * half,
     )
     logits, weights, stats, send = call(
         send_sums_kernel,
@@ -304,12 +324,13 @@
             ((slots, half + LANES), BF16),
         ],
         swapped, part, near_tok,
+        scratch=[pltpu.VMEM((experts, per_expert, count), F32)],
         flops=4 * slots * count * half,
     )
     came = lax.ppermute(send, "core", SWAP)
     keep, mix, w_other_second = call(
-        functools.partial(keep_sums_kernel, other_rows[0]),
-        [((slots, half), F32), ((slots, count), BF16), ((other_rows[1], units), BF16)],
+        functools.partial(keep_sums_kernel, other_rows),
+        [((slots, half), F32), ((slots, count), BF16), ((half - other_rows, units), BF16)],
         logits, weights, near_tok, w_in,
         copies=1, in_hbm=(3,), stay=(2,), flops=2 * slots * count * half,
     )
@@ -323,19 +344,19 @@
     flat = packed.reshape((experts * chips,) + packed.shape[2:])
     mine = lax.all_to_all(flat, both, split_axis=0, concat_axis=0, tiled=True)
     swapped = lax.ppermute(mine, "core", SWAP)
-    acc, w_other_third, w_near = call(
+    acc, w_near = call(
         own_hidden_kernel,
-        [((slots, units), F32), ((other_rows[2], units), BF16), ((near_units, width), BF16)],
-        mine.reshape(packed.shape), w_own_first, w_own_second, w_in, w_out,
-        copies=2, in_hbm=(3, 4), stay=(1, 2), flops=2 * slots * half * units, limit=16 << 20,
-    )
-    w_other = (w_other_first, w_other_second, w_other_third)
-    pieces = math.gcd((units - near_units) // LANES, 5)
+        [((slots, units), F32), ((near_units, width), BF16)],
+        mine.reshape(packed.shape), w_own, w_out,
+        copies=1, in_hbm=(2,), stay=(1,), flops=2 * slots * half * units, limit=16 << 20,
+    )
+    w_other = (w_other_first, w_other_second)
+    pieces = math.gcd((units - near_units) // LANES, 4)
     send, hidden, w_rest = call(
         send_terms_kernel,
         [((slots, half), BF16), ((slots, units), BF16), ((units - near_units, width), BF16)],
         acc, swapped.reshape(packed.shape), *w_other, w_near, w_out,
-        copies=pieces, in_hbm=(6,), stay=(2,), flops=4 * slots * half * units, limit=16 << 20,
+        copies=pieces, in_hbm=(5,), stay=(2,), flops=4 * slots * half * units, limit=16 << 20,
     )
     came = lax.ppermute(send, "core", SWAP)
     (keep,) = call(

time: 57.9 us -> 55.9 us (0.965)
  waiting for transfers between devices: 6.93 us -> 4.25 us
  starting transfers between devices: 8.47 us -> 10.5 us
  local copies, waits for them, and re-layouts: 1.43 us -> 0.01 us
    ppermute x1 -> x5, starting transfers between devices: 0.01 us -> 9.84 us  [the longest x4 6.44 us: gather_keys(): blocks.append(lax.ppermute(keys, axes, pairs))]
    all_to_all x1 -> x0, starting transfers between devices: 7.31 us -> none  [on_device(): lax.all_to_all(keys, 'expert', split_axis=0, concat_axis=0, tiled=True)]
    all_to_all x1 -> x0, waiting for transfers between devices: 5.37 us -> none  [on_device(): lax.all_to_all(keys, 'expert', split_axis=0, concat_axis=0, tiled=True)]
    ppermute x1 -> x5, waiting for transfers between devices: 0.01 us -> 2.69 us  [the longest x4 2.69 us: gather_keys(): blocks.append(lax.ppermute(keys, axes, pairs))]
    unnamed x2, local copies, waits for them, and re-layouts: 0.76 us -> 0.01 us
    broadcast_in_dim x1 -> x0, local copies, waits for them, and re-layouts: 0.67 us -> none  [on_device(): keys = jnp.broadcast_to(keys[None], (experts, per_expert, half))]
    pallas_call x10 -> x11, Pallas kernels: 11.7 us -> 11.6 us  [call(): pl.pallas_call(kernel, out_shape=shapes, in_specs=[pl.BlockSpec(memory_sp...]
  transfers between devices with their start and end apart: 6 -> 9, of which waited for: 3 -> 3; matrix products, arithmetic and copies ran while one was open for 0% -> 0% of each run, Pallas kernels for 13% -> 14%
where the time goes in v5:
time: 55.9 us; the launch traced here: 55.6 us
  blocking collectives  28.1 us (50%)
  Pallas kernels  12.6 us (23%)
  starting transfers between devices  10.5 us (19%)
  waiting for transfers between devices  4.25 us (8%)
    all_to_all x2, blocking collectives, on_device(): mine = lax.all_to_all(flat, both, split_axis=0, concat_axis=0, tiled=True)  28.1 us
    pallas_call x11, Pallas kernels, call(): pl.pallas_call(kernel, out_shape=shapes, in_specs=[pl.BlockSpec(memory_sp...  11.6 us
    ppermute x4, starting transfers between devices, gather_keys(): blocks.append(lax.ppermute(keys, axes, pairs))  6.44 us
    ppermute x1, starting transfers between devices, on_device(): swapped = lax.ppermute(stack, 'core', SWAP)  3.4 us
    ppermute x4, waiting for transfers between devices, gather_keys(): blocks.append(lax.ppermute(keys, axes, pairs))  2.69 us
    ppermute x2, waiting for transfers between devices, on_device(): swapped = lax.ppermute(mine, 'core', SWAP)  1.23 us
  transfers between devices with their start and end apart: 9, of which 3 were waited for; matrix products, arithmetic and copies ran while one was open for 0% of the time, Pallas kernels for 14%

profile of v5, /device:TPU:0, one launch (start us, length us, event | category | flops | bytes accessed | tf_op | source)
XLA Modules:
  0.0 55.6 jit_solution(3725565431070774307)
XLA Ops:
  0.0 0.7 %collective-permute-start.3 = (bf16[8,2048]{1,0:T(8,128)(2,1)}, bf16[8,2048]{1,0:T(8,128)(2,1)S(1)}, u32[]{:S(2)}, u32[]{:S(2)}) collective-permute-start(bf16[8,2048]{1,0:T(8,128)(2,1)} %bitcast.17), channel_id=1, source_target_pairs={{8,9},{9,8},{10,11},{11,10},{12,13},{13,12},{14,15},{15,14},{24,25... | collective-permute-start | bytes 98312 | tf_op jit(solution)/shard_map/ppermute | solution.py:73
  0.7 5.1 %collective-permute-start.2 = (bf16[8,2048]{1,0:T(8,128)(2,1)}, bf16[8,2048]{1,0:T(8,128)(2,1)S(1)}, u32[]{:S(2)}, u32[]{:S(2)}) collective-permute-start(bf16[8,2048]{1,0:T(8,128)(2,1)} %bitcast.18), channel_id=1, source_target_pairs={{0,6},{1,7},{2,4},{3,5},{4,2},{5,3},{6,0},{7,1},{8,11},{9,10},{10,... | collective-permute-start | bytes 98312 | tf_op jit(solution)/shard_map/ppermute | solution.py:73
  5.8 0.0 collective-permute-start.1
  5.8 0.6 %collective-permute-start = (bf16[8,2048]{1,0:T(8,128)(2,1)}, bf16[8,2048]{1,0:T(8,128)(2,1)S(1)}, u32[]{:S(2)}, u32[]{:S(2)}) collective-permute-start(bf16[8,2048]{1,0:T(8,128)(2,1)} %bitcast.20), channel_id=1, source_target_pairs={{0,2},{1,3},{2,0},{3,1},{4,6},{5,7},{6,4},{7,5},{8,15},{9,14},{10,... | collective-permute-start | bytes 98312 | tf_op jit(solution)/shard_map/ppermute | solution.py:73
  6.4 0.0 copy-start
  6.4 2.2 %shard_map.46 = (bf16[224,2048]{1,0:T(8,128)(2,1)S(1)}, bf16[1024,1536]{1,0:T(8,128)(2,1)S(1)}) custom-call(bf16[224,2048]{1,0:T(8,128)(2,1)} %bitcast.27, bf16[2048,1536]{1,0:T(8,128)(2,1)} %bitcast.22), custom_call_target="tpu_custom_call" | custom-call | bytes 4063232 | tf_op jit(solution)/shard_map/pallas_call | solution.py:263
  8.7 0.0 collective-permute-done.3.refs_4_
  8.7 0.0 collective-permute-done.2.refs_3_
  8.7 2.7 %collective-permute-done.1.refs_2_ = bf16[8,2048]{1,0:T(8,128)(2,1)S(1)} collective-permute-done((bf16[8,2048]{1,0:T(8,128)(2,1)}, bf16[8,2048]{1,0:T(8,128)(2,1)S(1)}, u32[]{:S(2)}, u32[]{:S(2)}) %collective-permute-start.1) | collective-permute-done | bytes 32800 | tf_op jit(solution)/shard_map/ppermute | solution.py:73
  11.4 0.0 collective-permute-done.refs_1_
  11.4 0.0 copy-done
  11.4 3.4 %collective-permute-start.4 = (bf16[4,8,2048]{2,1,0:T(8,128)(2,1)S(1)}, bf16[4,8,2048]{2,1,0:T(8,128)(2,1)S(1)}, u32[]{:S(2)}, u32[]{:S(2)}) collective-permute-start(bf16[4,8,2048]{2,1,0:T(8,128)(2,1)S(1)} %shard_map.47.stack_ref), channel_id=1, source_target_pairs={{0,8},{8,0},{1,9},{9,1},{2,10},{10,2},{3,11},{11,3},{4,12},{12,4},... | collective-permute-start | bytes 393224 | tf_op jit(solution)/shard_map/ppermute | solution.py:311
  14.8 1.6 %shard_map.48 = (f32[32,224]{1,0:T(8,128)S(1)}, bf16[512,1536]{1,0:T(8,128)(2,1)S(1)}) custom-call(bf16[4,8,2048]{2,1,0:T(8,128)(2,1)S(1)} %shard_map.47.stack_ref, bf16[224,2048]{1,0:T(8,128)(2,1)S(1)} %get-tuple-element.33.tok_ref, bf16[2048,1536]{1,0:T(8,128)(2,1)} %bitcast.23), custom_call_target="tpu_custom_call" | custom-call | flops 29360128 | bytes 1601536 | tf_op jit(solution)/shard_map/pallas_call | solution.py:263
  16.4 0.0 collective-permute-done.4.swapped_ref
  16.4 0.8 %shard_map.49 = (f32[64,224]{1,0:T(8,128)S(1)}, bf16[64,224]{1,0:T(8,128)(2,1)S(1)}, f32[64,128]{1,0:T(8,128)S(1)}, bf16[64,1152]{1,0:T(8,128)(2,1)S(1)}) custom-call(bf16[4,8,2048]{2,1,0:T(8,128)(2,1)S(1)} %collective-permute-done.4.swapped_ref, f32[32,224]{1,0:T(8,128)S(1)} %get-tuple-element.34.part_ref, bf16[224,2048]{1,0:T(8,128)(2,1)S(1)} %get-tuple-element.33.tok_ref), custom_call_target="tpu_custom_call" | custom-call | flops 58720256 | bytes 266240 | tf_op jit(solution)/shard_map/pallas_call | solution.py:263
  17.2 0.1 collective-permute-start.5
  17.3 1.5 %shard_map.50 = (f32[64,1024]{1,0:T(8,128)S(1)}, bf16[64,224]{1,0:T(8,128)(2,1)S(1)}, bf16[512,1536]{1,0:T(8,128)(2,1)S(1)}) custom-call(f32[64,224]{1,0:T(8,128)S(1)} %get-tuple-element.35.logits_ref, bf16[64,224]{1,0:T(8,128)(2,1)S(1)} %get-tuple-element.36.weights_ref, bf16[224,2048]{1,0:T(8,128)(2,1)S(1)} %get-tuple-element.33.tok_ref, ...), custom_call_target="tpu_custom_call" | custom-call | flops 29360128 | bytes 1863680 | tf_op jit(solution)/shard_map/pallas_call | solution.py:263
  18.8 0.0 collective-permute-done.5.came_ref
  18.8 0.3 shard_map.51
  19.1 14.5 %all_to_all.10 = bf16[16,8,1152]{2,1,0:T(8,128)(2,1)S(1)} all-to-all(bf16[16,8,1152]{2,1,0:T(8,128)(2,1)S(1)} %bitcast.12), channel_id=1, replica_groups=mesh['chip'=2,'core'=2,'expert'=8] {'expert','chip'}, dimensions={0} | all-to-all | bytes 589824 | tf_op jit(solution)/shard_map/all_to_all | solution.py:345
  33.6 0.0 collective-permute-start.6
  33.6 1.6 %shard_map.52 = (f32[64,1536]{1,0:T(8,128)S(1)}, bf16[512,2048]{1,0:T(8,128)(2,1)S(1)}) custom-call(bf16[8,2,8,1152]{3,2,1,0:T(8,128)(2,1)S(1)} %bitcast.11, bf16[1024,1536]{1,0:T(8,128)(2,1)S(1)} %get-tuple-element.41.w_own_ref, bf16[1536,2048]{1,0:T(8,128)(2,1)} %bitcast.25), custom_call_target="tpu_custom_call" | custom-call | flops 201326592 | bytes 2490368 | tf_op jit(solution)/shard_map/pallas_call | solution.py:263
  35.2 0.0 collective-permute-done.6
  35.3 2.5 %shard_map.53 = (bf16[64,1024]{1,0:T(8,128)(2,1)S(1)}, bf16[64,1536]{1,0:T(8,128)(2,1)S(1)}, bf16[1024,2048]{1,0:T(8,128)(2,1)S(1)}) custom-call(f32[64,1536]{1,0:T(8,128)S(1)} %get-tuple-element.42.acc_ref, bf16[8,2,8,1152]{3,2,1,0:T(8,128)(2,1)S(1)} %bitcast.15, bf16[512,1536]{1,0:T(8,128)(2,1)S(1)} %get-tuple-element.43.w_first_ref, ...), custom_call_target="tpu_custom_call" | custom-call | flops 402653184 | bytes 4521984 | tf_op jit(solution)/shard_map/pallas_call | solution.py:263
  37.8 0.6 %collective-permute-start.7 = (bf16[64,1024]{1,0:T(8,128)(2,1)S(1)}, bf16[64,1024]{1,0:T(8,128)(2,1)S(1)}, u32[]{:S(2)}, u32[]{:S(2)}) collective-permute-start(bf16[64,1024]{1,0:T(8,128)(2,1)S(1)} %get-tuple-element.48), channel_id=1, source_target_pairs={{0,8},{8,0},{1,9},{9,1},{2,10},{10,2},{3,11},{11,3},{4,12},{12,4},... | collective-permute-start | bytes 393224 | tf_op jit(solution)/shard_map/ppermute | solution.py:361
  38.4 0.7 %shard_map.54.keep_ref = f32[64,1024]{1,0:T(8,128)S(1)} custom-call(bf16[64,1536]{1,0:T(8,128)(2,1)S(1)} %get-tuple-element.46.hidden_ref, bf16[512,2048]{1,0:T(8,128)(2,1)S(1)} %get-tuple-element.45.w_near_ref, bf16[1024,2048]{1,0:T(8,128)(2,1)S(1)} %get-tuple-element.47.w_rest_ref), custom_call_target="tpu_custom_call" | custom-call | flops 201326592 | bytes 262144 | tf_op jit(solution)/shard_map/pallas_call | solution.py:263
  39.0 0.3 collective-permute-done.7.came_ref
  39.4 13.6 %all_to_all.11 = bf16[16,8,1024]{2,1,0:T(8,128)(2,1)S(1)} all-to-all(bf16[16,8,1024]{2,1,0:T(8,128)(2,1)S(1)} %bitcast.14), channel_id=1, replica_groups=mesh['chip'=2,'core'=2,'expert'=8] {'expert','chip'}, dimensions={0} | all-to-all | bytes 524288 | tf_op jit(solution)/shard_map/all_to_all | solution.py:372
  53.0 0.0 collective-permute-start.8
  53.0 0.3 shard_map.56.half_ref
  53.3 1.2 %collective-permute-done.8 = bf16[16,8,1024]{2,1,0:T(8,128)(2,1)S(1)} collective-permute-done((bf16[16,8,1024]{2,1,0:T(8,128)(2,1)S(1)}, bf16[16,8,1024]{2,1,0:T(8,128)(2,1)S(1)}, u32[]{:S(2)}, u32[]{:S(2)}) %collective-permute-start.8) | collective-permute-done | bytes 262176 | tf_op jit(solution)/shard_map/ppermute | solution.py:373
  54.5 1.1 %shard_map.57 = bf16[224,2048]{1,0:T(8,128)(2,1)} custom-call(bf16[64,224]{1,0:T(8,128)(2,1)S(1)} %get-tuple-element.37.mix_ref, bf16[8,2,8,1024]{3,2,1,0:T(8,128)(2,1)S(1)} %bitcast.16, bf16[224,1024]{1,0:T(8,128)(2,1)S(1)} %shard_map.56.half_ref), custom_call_target="tpu_custom_call" | custom-call | flops 29360128 | bytes 917504 | tf_op jit(solution)/shard_map/pallas_call | solution.py:380
  (2 shorter events, 0.0 us)
Async XLA Ops:
  0.0 8.7 %collective-permute-start.3 = (bf16[8,2048]{1,0:T(8,128)(2,1)}, bf16[8,2048]{1,0:T(8,128)(2,1)S(1)}, u32[]{:S(2)}, u32[]{:S(2)}) collective-permute-start(bf16[8,2048]{1,0:T(8,128)(2,1)} %bitcast.17), channel_id=1, source_target_pairs={{8,9},{9,8},{10,11},{11,10},{12,13},{13,12},{14,15},{15,14},{24,25... | collective-permute-start | bytes 98312 | tf_op jit(solution)/shard_map/ppermute | solution.py:73
  0.7 8.0 %collective-permute-start.2 = (bf16[8,2048]{1,0:T(8,128)(2,1)}, bf16[8,2048]{1,0:T(8,128)(2,1)S(1)}, u32[]{:S(2)}, u32[]{:S(2)}) collective-permute-start(bf16[8,2048]{1,0:T(8,128)(2,1)} %bitcast.18), channel_id=1, source_target_pairs={{0,6},{1,7},{2,4},{3,5},{4,2},{5,3},{6,0},{7,1},{8,11},{9,10},{10,... | collective-permute-start | bytes 98312 | tf_op jit(solution)/shard_map/ppermute | solution.py:73
  5.8 5.6 %collective-permute-start.1 = (bf16[8,2048]{1,0:T(8,128)(2,1)}, bf16[8,2048]{1,0:T(8,128)(2,1)S(1)}, u32[]{:S(2)}, u32[]{:S(2)}) collective-permute-start(bf16[8,2048]{1,0:T(8,128)(2,1)} %bitcast.19), channel_id=1, source_target_pairs={{0,4},{1,5},{2,6},{3,7},{4,0},{5,1},{6,2},{7,3},{8,13},{9,12},{10,... | collective-permute-start | bytes 98312 | tf_op jit(solution)/shard_map/ppermute | solution.py:73
  5.8 5.6 %collective-permute-start = (bf16[8,2048]{1,0:T(8,128)(2,1)}, bf16[8,2048]{1,0:T(8,128)(2,1)S(1)}, u32[]{:S(2)}, u32[]{:S(2)}) collective-permute-start(bf16[8,2048]{1,0:T(8,128)(2,1)} %bitcast.20), channel_id=1, source_target_pairs={{0,2},{1,3},{2,0},{3,1},{4,6},{5,7},{6,4},{7,5},{8,15},{9,14},{10,... | collective-permute-start | bytes 98312 | tf_op jit(solution)/shard_map/ppermute | solution.py:73
  6.4 4.9 %copy-start = (bf16[2048,8]{0,1:T(8,128)(2,1)S(1)}, bf16[2048,8]{0,1:T(8,128)(2,1)}, u32[]{:S(2)}) copy-start(bf16[2048,8]{0,1:T(8,128)(2,1)} %param.5) | copy-start | bytes 98308
  11.4 5.0 %collective-permute-start.4 = (bf16[4,8,2048]{2,1,0:T(8,128)(2,1)S(1)}, bf16[4,8,2048]{2,1,0:T(8,128)(2,1)S(1)}, u32[]{:S(2)}, u32[]{:S(2)}) collective-permute-start(bf16[4,8,2048]{2,1,0:T(8,128)(2,1)S(1)} %shard_map.47.stack_ref), channel_id=1, source_target_pairs={{0,8},{8,0},{1,9},{9,1},{2,10},{10,2},{3,11},{11,3},{4,12},{12,4},... | collective-permute-start | bytes 393224 | tf_op jit(solution)/shard_map/ppermute | solution.py:311
  17.2 1.6 %collective-permute-start.5 = (bf16[64,1152]{1,0:T(8,128)(2,1)S(1)}, bf16[64,1152]{1,0:T(8,128)(2,1)S(1)}, u32[]{:S(2)}, u32[]{:S(2)}) collective-permute-start(bf16[64,1152]{1,0:T(8,128)(2,1)S(1)} %get-tuple-element.40), channel_id=1, source_target_pairs={{0,8},{8,0},{1,9},{9,1},{2,10},{10,2},{3,11},{11,3},{4,12},{12,4},... | collective-permute-start | bytes 442376 | tf_op jit(solution)/shard_map/ppermute | solution.py:330
  33.6 1.6 %collective-permute-start.6 = (bf16[16,8,1152]{2,1,0:T(8,128)(2,1)S(1)}, bf16[16,8,1152]{2,1,0:T(8,128)(2,1)S(1)}, u32[]{:S(2)}, u32[]{:S(2)}) collective-permute-start(bf16[16,8,1152]{2,1,0:T(8,128)(2,1)S(1)} %all_to_all.10), channel_id=1, source_target_pairs={{0,8},{8,0},{1,9},{9,1},{2,10},{10,2},{3,11},{11,3},{4,12},{12,4},... | collective-permute-start | bytes 884744 | tf_op jit(solution)/shard_map/ppermute | solution.py:346
  37.8 1.6 %collective-permute-start.7 = (bf16[64,1024]{1,0:T(8,128)(2,1)S(1)}, bf16[64,1024]{1,0:T(8,128)(2,1)S(1)}, u32[]{:S(2)}, u32[]{:S(2)}) collective-permute-start(bf16[64,1024]{1,0:T(8,128)(2,1)S(1)} %get-tuple-element.48), channel_id=1, source_target_pairs={{0,8},{8,0},{1,9},{9,1},{2,10},{10,2},{3,11},{11,3},{4,12},{12,4},... | collective-permute-start | bytes 393224 | tf_op jit(solution)/shard_map/ppermute | solution.py:361
  53.0 1.5 %collective-permute-start.8 = (bf16[16,8,1024]{2,1,0:T(8,128)(2,1)S(1)}, bf16[16,8,1024]{2,1,0:T(8,128)(2,1)S(1)}, u32[]{:S(2)}, u32[]{:S(2)}) collective-permute-start(bf16[16,8,1024]{2,1,0:T(8,128)(2,1)S(1)} %all_to_all.11), channel_id=1, source_target_pairs={{0,8},{8,0},{1,9},{9,1},{2,10},{10,2},{3,11},{11,3},{4,12},{12,4},... | collective-permute-start | bytes 786440 | tf_op jit(solution)/shard_map/ppermute | solution.py:373

commit v6 on v5

--- a/solution.py
+++ b/solution.py
@@ -56,7 +56,7 @@
 
 
 def held_masks(experts):
-    return [((2 + 2 * k) % experts, experts - 1 - 2 * k) for k in range(experts // 2)]
+    return [((experts - 2 * k) % experts, 2 * k + 1) for k in range(experts // 2)]
 
 
 def gather_keys(keys, experts, chips):
@@ -76,11 +76,9 @@
 
 def stack_kernel(*refs):
     keys_ref, *blocks, out_ref = refs
-    for k, block in enumerate(blocks[:-1]):
-        out_ref[k] = block[...]
-    out_ref[len(blocks) - 1] = jnp.where(
-        lax.axis_index("core") == 0, keys_ref[...], blocks[-1][...]
-    )
+    out_ref[0] = jnp.where(lax.axis_index("core") == 0, keys_ref[...], blocks[0][...])
+    for k, block in enumerate(blocks[1:]):
+        out_ref[k + 1] = block[...]
 
 
 def first_fetch_kernel(tok_ref, w_in_ref, near_tok, near_w, sem):

time: 55.9 us -> 55.9 us (level)
  starting transfers between devices: 10.5 us -> 7.52 us
  blocking collectives: 28.1 us -> 30.5 us
    ppermute x1, starting transfers between devices: 3.4 us -> 0.17 us  [on_device(): swapped = lax.ppermute(stack, 'core', SWAP)]
    all_to_all x2, blocking collectives: 28.1 us -> 30.5 us  [on_device(): mine = lax.all_to_all(flat, both, split_axis=0, concat_axis=0, tiled=True)]
  transfers between devices with their start and end apart: 9 -> 9, of which waited for: 3 -> 4; matrix products, arithmetic and copies ran while one was open for 0% -> 0% of each run, Pallas kernels for 14% -> 14%
where the time goes in v6:
time: 55.9 us; the launch traced here: 55.6 us
  blocking collectives  30.5 us (55%)
  Pallas kernels  12.6 us (23%)
  starting transfers between devices  7.52 us (13%)
  waiting for transfers between devices  4.79 us (9%)
    all_to_all x2, blocking collectives, on_device(): mine = lax.all_to_all(flat, both, split_axis=0, concat_axis=0, tiled=True)  30.5 us
    pallas_call x11, Pallas kernels, call(): pl.pallas_call(kernel, out_shape=shapes, in_specs=[pl.BlockSpec(memory_sp...  11.6 us
    ppermute x4, starting transfers between devices, gather_keys(): blocks.append(lax.ppermute(keys, axes, pairs))  6.3 us
    ppermute x4, waiting for transfers between devices, gather_keys(): blocks.append(lax.ppermute(keys, axes, pairs))  3.23 us
    ppermute x2, waiting for transfers between devices, on_device(): swapped = lax.ppermute(mine, 'core', SWAP)  1.23 us
  transfers between devices with their start and end apart: 9, of which 4 were waited for; matrix products, arithmetic and copies ran while one was open for 0% of the time, Pallas kernels for 14%

profile of v6, /device:TPU:0, one launch (start us, length us, event | category | flops | bytes accessed | tf_op | source)
XLA Modules:
  0.0 55.6 jit_solution(15179198438142017659)
XLA Ops:
  0.0 3.1 %collective-permute-start.3 = (bf16[8,2048]{1,0:T(8,128)(2,1)}, bf16[8,2048]{1,0:T(8,128)(2,1)S(1)}, u32[]{:S(2)}, u32[]{:S(2)}) collective-permute-start(bf16[8,2048]{1,0:T(8,128)(2,1)} %bitcast.17), channel_id=1, source_target_pairs={{0,2},{1,3},{2,0},{3,1},{4,6},{5,7},{6,4},{7,5},{8,15},{9,14},{10,... | collective-permute-start | bytes 98312 | tf_op jit(solution)/shard_map/ppermute | solution.py:73
  3.1 2.6 %collective-permute-start.2 = (bf16[8,2048]{1,0:T(8,128)(2,1)}, bf16[8,2048]{1,0:T(8,128)(2,1)S(1)}, u32[]{:S(2)}, u32[]{:S(2)}) collective-permute-start(bf16[8,2048]{1,0:T(8,128)(2,1)} %bitcast.18), channel_id=1, source_target_pairs={{0,4},{1,5},{2,6},{3,7},{4,0},{5,1},{6,2},{7,3},{8,13},{9,12},{10,... | collective-permute-start | bytes 98312 | tf_op jit(solution)/shard_map/ppermute | solution.py:73
  5.6 0.0 collective-permute-start.1
  5.6 0.7 %collective-permute-start = (bf16[8,2048]{1,0:T(8,128)(2,1)}, bf16[8,2048]{1,0:T(8,128)(2,1)S(1)}, u32[]{:S(2)}, u32[]{:S(2)}) collective-permute-start(bf16[8,2048]{1,0:T(8,128)(2,1)} %bitcast.20), channel_id=1, source_target_pairs={{8,9},{9,8},{10,11},{11,10},{12,13},{13,12},{14,15},{15,14},{24,25... | collective-permute-start | bytes 98312 | tf_op jit(solution)/shard_map/ppermute | solution.py:73
  6.3 0.0 copy-start
  6.3 2.2 %shard_map.46 = (bf16[224,2048]{1,0:T(8,128)(2,1)S(1)}, bf16[1024,1536]{1,0:T(8,128)(2,1)S(1)}) custom-call(bf16[224,2048]{1,0:T(8,128)(2,1)} %bitcast.27, bf16[2048,1536]{1,0:T(8,128)(2,1)} %bitcast.22), custom_call_target="tpu_custom_call" | custom-call | bytes 4063232 | tf_op jit(solution)/shard_map/pallas_call | solution.py:261
  8.5 0.0 collective-permute-done.3.refs_4_
  8.5 0.2 collective-permute-done.2.refs_3_
  8.8 3.0 %collective-permute-done.1.refs_2_ = bf16[8,2048]{1,0:T(8,128)(2,1)S(1)} collective-permute-done((bf16[8,2048]{1,0:T(8,128)(2,1)}, bf16[8,2048]{1,0:T(8,128)(2,1)S(1)}, u32[]{:S(2)}, u32[]{:S(2)}) %collective-permute-start.1) | collective-permute-done | bytes 32800 | tf_op jit(solution)/shard_map/ppermute | solution.py:73
  11.8 0.0 collective-permute-done.refs_1_
  11.8 0.0 copy-done
  11.8 0.2 collective-permute-start.4
  12.0 1.6 %shard_map.48 = (f32[32,224]{1,0:T(8,128)S(1)}, bf16[512,1536]{1,0:T(8,128)(2,1)S(1)}) custom-call(bf16[4,8,2048]{2,1,0:T(8,128)(2,1)S(1)} %shard_map.47.stack_ref, bf16[224,2048]{1,0:T(8,128)(2,1)S(1)} %get-tuple-element.33.tok_ref, bf16[2048,1536]{1,0:T(8,128)(2,1)} %bitcast.23), custom_call_target="tpu_custom_call" | custom-call | flops 29360128 | bytes 1601536 | tf_op jit(solution)/shard_map/pallas_call | solution.py:261
  13.6 0.0 collective-permute-done.4.swapped_ref
  13.6 0.8 %shard_map.49 = (f32[64,224]{1,0:T(8,128)S(1)}, bf16[64,224]{1,0:T(8,128)(2,1)S(1)}, f32[64,128]{1,0:T(8,128)S(1)}, bf16[64,1152]{1,0:T(8,128)(2,1)S(1)}) custom-call(bf16[4,8,2048]{2,1,0:T(8,128)(2,1)S(1)} %collective-permute-done.4.swapped_ref, f32[32,224]{1,0:T(8,128)S(1)} %get-tuple-element.34.part_ref, bf16[224,2048]{1,0:T(8,128)(2,1)S(1)} %get-tuple-element.33.tok_ref), custom_call_target="tpu_custom_call" | custom-call | flops 58720256 | bytes 266240 | tf_op jit(solution)/shard_map/pallas_call | solution.py:261
  14.4 0.5 collective-permute-start.5
  14.9 1.5 %shard_map.50 = (f32[64,1024]{1,0:T(8,128)S(1)}, bf16[64,224]{1,0:T(8,128)(2,1)S(1)}, bf16[512,1536]{1,0:T(8,128)(2,1)S(1)}) custom-call(f32[64,224]{1,0:T(8,128)S(1)} %get-tuple-element.35.logits_ref, bf16[64,224]{1,0:T(8,128)(2,1)S(1)} %get-tuple-element.36.weights_ref, bf16[224,2048]{1,0:T(8,128)(2,1)S(1)} %get-tuple-element.33.tok_ref, ...), custom_call_target="tpu_custom_call" | custom-call | flops 29360128 | bytes 1863680 | tf_op jit(solution)/shard_map/pallas_call | solution.py:261
  16.3 0.0 collective-permute-done.5.came_ref
  16.4 0.3 shard_map.51
  16.7 16.9 %all_to_all.10 = bf16[16,8,1152]{2,1,0:T(8,128)(2,1)S(1)} all-to-all(bf16[16,8,1152]{2,1,0:T(8,128)(2,1)S(1)} %bitcast.12), channel_id=1, replica_groups=mesh['chip'=2,'core'=2,'expert'=8] {'expert','chip'}, dimensions={0} | all-to-all | bytes 589824 | tf_op jit(solution)/shard_map/all_to_all | solution.py:343
  33.6 0.0 collective-permute-start.6
  33.6 1.6 %shard_map.52 = (f32[64,1536]{1,0:T(8,128)S(1)}, bf16[512,2048]{1,0:T(8,128)(2,1)S(1)}) custom-call(bf16[8,2,8,1152]{3,2,1,0:T(8,128)(2,1)S(1)} %bitcast.11, bf16[1024,1536]{1,0:T(8,128)(2,1)S(1)} %get-tuple-element.41.w_own_ref, bf16[1536,2048]{1,0:T(8,128)(2,1)} %bitcast.25), custom_call_target="tpu_custom_call" | custom-call | flops 201326592 | bytes 2490368 | tf_op jit(solution)/shard_map/pallas_call | solution.py:261
  35.2 0.0 collective-permute-done.6
  35.2 2.5 %shard_map.53 = (bf16[64,1024]{1,0:T(8,128)(2,1)S(1)}, bf16[64,1536]{1,0:T(8,128)(2,1)S(1)}, bf16[1024,2048]{1,0:T(8,128)(2,1)S(1)}) custom-call(f32[64,1536]{1,0:T(8,128)S(1)} %get-tuple-element.42.acc_ref, bf16[8,2,8,1152]{3,2,1,0:T(8,128)(2,1)S(1)} %bitcast.15, bf16[512,1536]{1,0:T(8,128)(2,1)S(1)} %get-tuple-element.43.w_first_ref, ...), custom_call_target="tpu_custom_call" | custom-call | flops 402653184 | bytes 4521984 | tf_op jit(solution)/shard_map/pallas_call | solution.py:261
  37.7 0.6 %collective-permute-start.7 = (bf16[64,1024]{1,0:T(8,128)(2,1)S(1)}, bf16[64,1024]{1,0:T(8,128)(2,1)S(1)}, u32[]{:S(2)}, u32[]{:S(2)}) collective-permute-start(bf16[64,1024]{1,0:T(8,128)(2,1)S(1)} %get-tuple-element.48), channel_id=1, source_target_pairs={{0,8},{8,0},{1,9},{9,1},{2,10},{10,2},{3,11},{11,3},{4,12},{12,4},... | collective-permute-start | bytes 393224 | tf_op jit(solution)/shard_map/ppermute | solution.py:359
  38.3 0.7 %shard_map.54.keep_ref = f32[64,1024]{1,0:T(8,128)S(1)} custom-call(bf16[64,1536]{1,0:T(8,128)(2,1)S(1)} %get-tuple-element.46.hidden_ref, bf16[512,2048]{1,0:T(8,128)(2,1)S(1)} %get-tuple-element.45.w_near_ref, bf16[1024,2048]{1,0:T(8,128)(2,1)S(1)} %get-tuple-element.47.w_rest_ref), custom_call_target="tpu_custom_call" | custom-call | flops 201326592 | bytes 262144 | tf_op jit(solution)/shard_map/pallas_call | solution.py:261
  39.0 0.3 collective-permute-done.7.came_ref
  39.3 13.6 %all_to_all.11 = bf16[16,8,1024]{2,1,0:T(8,128)(2,1)S(1)} all-to-all(bf16[16,8,1024]{2,1,0:T(8,128)(2,1)S(1)} %bitcast.14), channel_id=1, replica_groups=mesh['chip'=2,'core'=2,'expert'=8] {'expert','chip'}, dimensions={0} | all-to-all | bytes 524288 | tf_op jit(solution)/shard_map/all_to_all | solution.py:370
  52.9 0.0 collective-permute-start.8
  53.0 0.3 shard_map.56.half_ref
  53.3 1.2 %collective-permute-done.8 = bf16[16,8,1024]{2,1,0:T(8,128)(2,1)S(1)} collective-permute-done((bf16[16,8,1024]{2,1,0:T(8,128)(2,1)S(1)}, bf16[16,8,1024]{2,1,0:T(8,128)(2,1)S(1)}, u32[]{:S(2)}, u32[]{:S(2)}) %collective-permute-start.8) | collective-permute-done | bytes 262176 | tf_op jit(solution)/shard_map/ppermute | solution.py:371
  54.5 1.1 %shard_map.57 = bf16[224,2048]{1,0:T(8,128)(2,1)} custom-call(bf16[64,224]{1,0:T(8,128)(2,1)S(1)} %get-tuple-element.37.mix_ref, bf16[8,2,8,1024]{3,2,1,0:T(8,128)(2,1)S(1)} %bitcast.16, bf16[224,1024]{1,0:T(8,128)(2,1)S(1)} %shard_map.56.half_ref), custom_call_target="tpu_custom_call" | custom-call | flops 29360128 | bytes 917504 | tf_op jit(solution)/shard_map/pallas_call | solution.py:378
  (2 shorter events, 0.0 us)
Async XLA Ops:
  0.0 8.5 %collective-permute-start.3 = (bf16[8,2048]{1,0:T(8,128)(2,1)}, bf16[8,2048]{1,0:T(8,128)(2,1)S(1)}, u32[]{:S(2)}, u32[]{:S(2)}) collective-permute-start(bf16[8,2048]{1,0:T(8,128)(2,1)} %bitcast.17), channel_id=1, source_target_pairs={{0,2},{1,3},{2,0},{3,1},{4,6},{5,7},{6,4},{7,5},{8,15},{9,14},{10,... | collective-permute-start | bytes 98312 | tf_op jit(solution)/shard_map/ppermute | solution.py:73
  3.1 5.7 %collective-permute-start.2 = (bf16[8,2048]{1,0:T(8,128)(2,1)}, bf16[8,2048]{1,0:T(8,128)(2,1)S(1)}, u32[]{:S(2)}, u32[]{:S(2)}) collective-permute-start(bf16[8,2048]{1,0:T(8,128)(2,1)} %bitcast.18), channel_id=1, source_target_pairs={{0,4},{1,5},{2,6},{3,7},{4,0},{5,1},{6,2},{7,3},{8,13},{9,12},{10,... | collective-permute-start | bytes 98312 | tf_op jit(solution)/shard_map/ppermute | solution.py:73
  5.6 6.1 %collective-permute-start.1 = (bf16[8,2048]{1,0:T(8,128)(2,1)}, bf16[8,2048]{1,0:T(8,128)(2,1)S(1)}, u32[]{:S(2)}, u32[]{:S(2)}) collective-permute-start(bf16[8,2048]{1,0:T(8,128)(2,1)} %bitcast.19), channel_id=1, source_target_pairs={{0,6},{1,7},{2,4},{3,5},{4,2},{5,3},{6,0},{7,1},{8,11},{9,10},{10,... | collective-permute-start | bytes 98312 | tf_op jit(solution)/shard_map/ppermute | solution.py:73
  5.6 6.1 %collective-permute-start = (bf16[8,2048]{1,0:T(8,128)(2,1)}, bf16[8,2048]{1,0:T(8,128)(2,1)S(1)}, u32[]{:S(2)}, u32[]{:S(2)}) collective-permute-start(bf16[8,2048]{1,0:T(8,128)(2,1)} %bitcast.20), channel_id=1, source_target_pairs={{8,9},{9,8},{10,11},{11,10},{12,13},{13,12},{14,15},{15,14},{24,25... | collective-permute-start | bytes 98312 | tf_op jit(solution)/shard_map/ppermute | solution.py:73
  6.3 5.5 %copy-start = (bf16[2048,8]{0,1:T(8,128)(2,1)S(1)}, bf16[2048,8]{0,1:T(8,128)(2,1)}, u32[]{:S(2)}) copy-start(bf16[2048,8]{0,1:T(8,128)(2,1)} %param.5) | copy-start | bytes 98308
  11.8 1.8 %collective-permute-start.4 = (bf16[4,8,2048]{2,1,0:T(8,128)(2,1)S(1)}, bf16[4,8,2048]{2,1,0:T(8,128)(2,1)S(1)}, u32[]{:S(2)}, u32[]{:S(2)}) collective-permute-start(bf16[4,8,2048]{2,1,0:T(8,128)(2,1)S(1)} %shard_map.47.stack_ref), channel_id=1, source_target_pairs={{0,8},{8,0},{1,9},{9,1},{2,10},{10,2},{3,11},{11,3},{4,12},{12,4},... | collective-permute-start | bytes 393224 | tf_op jit(solution)/shard_map/ppermute | solution.py:309
  14.4 2.0 %collective-permute-start.5 = (bf16[64,1152]{1,0:T(8,128)(2,1)S(1)}, bf16[64,1152]{1,0:T(8,128)(2,1)S(1)}, u32[]{:S(2)}, u32[]{:S(2)}) collective-permute-start(bf16[64,1152]{1,0:T(8,128)(2,1)S(1)} %get-tuple-element.40), channel_id=1, source_target_pairs={{0,8},{8,0},{1,9},{9,1},{2,10},{10,2},{3,11},{11,3},{4,12},{12,4},... | collective-permute-start | bytes 442376 | tf_op jit(solution)/shard_map/ppermute | solution.py:328
  33.6 1.6 %collective-permute-start.6 = (bf16[16,8,1152]{2,1,0:T(8,128)(2,1)S(1)}, bf16[16,8,1152]{2,1,0:T(8,128)(2,1)S(1)}, u32[]{:S(2)}, u32[]{:S(2)}) collective-permute-start(bf16[16,8,1152]{2,1,0:T(8,128)(2,1)S(1)} %all_to_all.10), channel_id=1, source_target_pairs={{0,8},{8,0},{1,9},{9,1},{2,10},{10,2},{3,11},{11,3},{4,12},{12,4},... | collective-permute-start | bytes 884744 | tf_op jit(solution)/shard_map/ppermute | solution.py:344
  37.7 1.6 %collective-permute-start.7 = (bf16[64,1024]{1,0:T(8,128)(2,1)S(1)}, bf16[64,1024]{1,0:T(8,128)(2,1)S(1)}, u32[]{:S(2)}, u32[]{:S(2)}) collective-permute-start(bf16[64,1024]{1,0:T(8,128)(2,1)S(1)} %get-tuple-element.48), channel_id=1, source_target_pairs={{0,8},{8,0},{1,9},{9,1},{2,10},{10,2},{3,11},{11,3},{4,12},{12,4},... | collective-permute-start | bytes 393224 | tf_op jit(solution)/shard_map/ppermute | solution.py:359
  52.9 1.5 %collective-permute-start.8 = (bf16[16,8,1024]{2,1,0:T(8,128)(2,1)S(1)}, bf16[16,8,1024]{2,1,0:T(8,128)(2,1)S(1)}, u32[]{:S(2)}, u32[]{:S(2)}) collective-permute-start(bf16[16,8,1024]{2,1,0:T(8,128)(2,1)S(1)} %all_to_all.11), channel_id=1, source_target_pairs={{0,8},{8,0},{1,9},{9,1},{2,10},{10,2},{3,11},{11,3},{4,12},{12,4},... | collective-permute-start | bytes 786440 | tf_op jit(solution)/shard_map/ppermute | solution.py:371

commit v7 on v6

--- a/solution.py
+++ b/solution.py
@@ -11,6 +11,7 @@
 F32 = jnp.float32
 BF16 = jnp.bfloat16
 LANES = 128
+COVER_FLOPS = 10**9
 SWAP = ((0, 1), (1, 0))
 ROWS_BY_ROWS = (((1,), (1,)), ((), ()))
 
@@ -20,6 +21,10 @@
     own = pl.ds(pl.multiple_of(core * half, LANES), half)
     other = pl.ds(pl.multiple_of((1 - core) * half, LANES), half)
     return own, other
+
+
+def row_halves(ref):
+    return column_halves(ref.shape[0] // 2)
 
 
 def three_terms(value):
@@ -67,7 +72,6 @@
             (((chip * 2 + core) * experts + e), ((chip * 2 + core) * experts + (e ^ mask)))
             for chip in range(chips)
             for core, mask in enumerate(masks)
-            if mask
             for e in range(experts)
         ]
         blocks.append(lax.ppermute(keys, axes, pairs))
@@ -75,18 +79,14 @@
 
 
 def stack_kernel(*refs):
-    keys_ref, *blocks, out_ref = refs
-    out_ref[0] = jnp.where(lax.axis_index("core") == 0, keys_ref[...], blocks[0][...])
-    for k, block in enumerate(blocks[1:]):
-        out_ref[k + 1] = block[...]
-
-
-def first_fetch_kernel(tok_ref, w_in_ref, near_tok, near_w, sem):
-    rows = near_w.shape[0]
-    start = lax.axis_index("core") * rows
-    pairs = [(tok_ref, near_tok), (w_in_ref.at[block_rows(start, rows)], near_w)]
-    for copy in copy_parts(sem, pairs):
-        copy.wait()
+    for k, block in enumerate(refs[:-1]):
+        refs[-1][k] = block[...]
+
+
+def fetch_kernel(far_ref, near_ref, sem):
+    copy = pltpu.make_async_copy(far_ref, near_ref, sem.at[0])
+    copy.start()
+    copy.wait()
 
 
 def held_logits(stack_ref, tok_ref):
@@ -97,12 +97,8 @@
     )
 
 
-def held_logits_kernel(stack_ref, tok_ref, w_in_ref, part_ref, near_w, sem):
-    start = (1 - lax.axis_index("core")) * (w_in_ref.shape[0] // 2)
-    copies = copy_parts(sem, [(w_in_ref.at[block_rows(start, near_w.shape[0])], near_w)])
+def held_logits_kernel(stack_ref, tok_ref, part_ref):
     part_ref[...] = held_logits(stack_ref, tok_ref)
-    for copy in copies:
-        copy.wait()
 
 
 def send_sums_kernel(
@@ -129,19 +125,12 @@
     stats_ref[...] = jnp.where(lane == 0, top, total)
 
 
-def keep_sums_kernel(
-    skip, logits_ref, weights_ref, tok_ref, w_in_ref, keep_ref, mix_ref, near_w, sem
-):
-    half = keep_ref.shape[1]
-    start = (1 - lax.axis_index("core")) * half + skip
-    copies = copy_parts(sem, [(w_in_ref.at[block_rows(start, near_w.shape[0])], near_w)])
-    own, _ = column_halves(half)
+def keep_sums_kernel(logits_ref, weights_ref, tok_ref, keep_ref, mix_ref):
+    own, _ = column_halves(keep_ref.shape[1])
     keep_ref[...] = jnp.dot(weights_ref[...], tok_ref[:, own], preferred_element_type=F32)
     logits = logits_ref[...]
     raised = jnp.exp(logits - jnp.max(logits, axis=0, keepdims=True))
     mix_ref[...] = (raised / jnp.sum(raised, axis=0, keepdims=True)).astype(BF16)
-    for copy in copies:
-        copy.wait()
 
 
 def chip_sum_kernel(keep_ref, stats_ref, came_ref, out_ref):
@@ -171,54 +160,25 @@
     return (summed / total).reshape(seqs * rows, half).astype(BF16)
 
 
-def row_blocks_dot(left, blocks):
-    start, total = 0, 0
-    for block in blocks:
-        rows = block.shape[0]
-        total += jnp.dot(left[:, start : start + rows], block[...], preferred_element_type=F32)
-        start += rows
-    return total
-
-
-def own_hidden_kernel(
-    mine_ref, w_own_ref, w_out_ref, acc_ref, near_out, sem
-):
-    copies = copy_parts(sem, [(w_out_ref.at[pl.ds(0, near_out.shape[0])], near_out)])
-    acc_ref[...] = row_blocks_dot(slot_inputs_of(mine_ref), (w_own_ref,))
-    for copy in copies:
-        copy.wait()
-
-
-def send_terms_kernel(
-    acc_ref, swapped_ref, w_first_ref, w_second_ref, w_near_ref, w_out_ref,
-    send_ref, hidden_ref, rest, sem,
-):
-    _, other = column_halves(w_out_ref.shape[1] // 2)
-    near, pieces = w_near_ref.shape[0], sem.shape[0]
-    step = rest.shape[0] // pieces
-    copies = copy_parts(sem, [
-        (w_out_ref.at[pl.ds(near + i * step, step)], rest.at[pl.ds(i * step, step)])
-        for i in range(pieces)
-    ])
-    summed = acc_ref[...] + row_blocks_dot(slot_inputs_of(swapped_ref), (w_first_ref, w_second_ref))
+def own_hidden_kernel(mine_ref, w_in_ref, acc_ref):
+    own, _ = row_halves(w_in_ref)
+    acc_ref[...] = jnp.dot(slot_inputs_of(mine_ref), w_in_ref[own, :], preferred_element_type=F32)
+
+
+def send_terms_kernel(acc_ref, swapped_ref, w_in_ref, w_out_ref, send_ref, hidden_ref):
+    _, other = row_halves(w_in_ref)
+    summed = acc_ref[...] + jnp.dot(
+        slot_inputs_of(swapped_ref), w_in_ref[other, :], preferred_element_type=F32
+    )
     hidden = jax.nn.gelu(summed, approximate=True).astype(BF16)
     hidden_ref[...] = hidden
-    sent = jnp.dot(hidden[:, :near], w_near_ref[:, other], preferred_element_type=F32)
-    for i, copy in enumerate(copies):
-        copy.wait()
-        rows = pl.ds(near + i * step, step)
-        sent += jnp.dot(
-            hidden_ref[:, rows], rest[pl.ds(i * step, step), other], preferred_element_type=F32
-        )
-    send_ref[...] = sent.astype(BF16)
-
-
-def keep_terms_kernel(hidden_ref, w_near_ref, w_rest_ref, keep_ref):
+    _, other = column_halves(send_ref.shape[1])
+    send_ref[...] = jnp.dot(hidden, w_out_ref[:, other], preferred_element_type=F32).astype(BF16)
+
+
+def keep_terms_kernel(hidden_ref, w_out_ref, keep_ref):
     own, _ = column_halves(keep_ref.shape[1])
-    near = w_near_ref.shape[0]
-    keep_ref[...] = jnp.dot(
-        hidden_ref[:, :near], w_near_ref[:, own], preferred_element_type=F32
-    ) + jnp.dot(hidden_ref[:, near:], w_rest_ref[:, own], preferred_element_type=F32)
+    keep_ref[...] = jnp.dot(hidden_ref[...], w_out_ref[:, own], preferred_element_type=F32)
 
 
 def pair_sum_kernel(keep_ref, came_ref, out_ref):
@@ -279,10 +239,6 @@
     ])
 
 
-def share(count, numerator, denominator):
-    return max(LANES, count * numerator // denominator // LANES * LANES)
-
-
 def on_device(tokens, slot_keys, w_in, w_out):
     token_rows, w_in, w_out = tokens[0], w_in[0], w_out[0]
     count, width = token_rows.shape
@@ -291,27 +247,20 @@
     experts, chips = lax.axis_size("expert"), lax.axis_size("chip")
     slots = experts * per_expert
     units = w_in.shape[1]
-    other_rows = share(half, 1, 2)
-    near_units = share(units, 1, 3)
 
     keys = slot_keys.T
     blocks = gather_keys(keys, experts, chips)
-    near_tok, w_own = call(
-        first_fetch_kernel,
-        [(token_rows.shape, BF16), ((half, units), BF16)],
-        token_rows, w_in,
-        copies=2, in_hbm=(0, 1), stay=(0, 1),
-    )
-    *blocks, near_tok, w_own = lax.optimization_barrier((*blocks, near_tok, w_own))
+    (token_rows,) = call(
+        fetch_kernel, [(token_rows.shape, BF16)], token_rows, copies=1, in_hbm=(0,), stay=(0,)
+    )
+    *blocks, token_rows = lax.optimization_barrier((*blocks, token_rows))
     (stack,) = call(
-        stack_kernel, [((experts // 2, per_expert, width), BF16)], keys, *blocks
+        stack_kernel, [((experts // 2, per_expert, width), BF16)], *blocks
     )
     swapped = lax.ppermute(stack, "core", SWAP)
-    part, w_other_first = call(
-        held_logits_kernel,
-        [((slots // 2, count), F32), ((other_rows, units), BF16)],
-        stack, near_tok, w_in,
-        copies=1, in_hbm=(2,), stay=(1,), flops=2 * slots * count * half,
+    (part,) = call(
+        held_logits_kernel, [((slots // 2, count), F32)], stack, token_rows,
+        flops=2 * slots * count * half,
     )
     logits, weights, stats, send = call(
         send_sums_kernel,
@@ -321,47 +270,42 @@
             ((slots, LANES), F32),
             ((slots, half + LANES), BF16),
         ],
-        swapped, part, near_tok,
+        swapped, part, token_rows,
         scratch=[pltpu.VMEM((experts, per_expert, count), F32)],
         flops=4 * slots * count * half,
     )
     came = lax.ppermute(send, "core", SWAP)
-    keep, mix, w_other_second = call(
-        functools.partial(keep_sums_kernel, other_rows),
-        [((slots, half), F32), ((slots, count), BF16), ((half - other_rows, units), BF16)],
-        logits, weights, near_tok, w_in,
-        copies=1, in_hbm=(3,), stay=(2,), flops=2 * slots * count * half,
+    keep, mix = call(
+        keep_sums_kernel,
+        [((slots, half), F32), ((slots, count), BF16)],
+        logits, weights, token_rows,
+        flops=2 * slots * count * half,
     )
     (packed,) = call(
         chip_sum_kernel,
         [((experts, chips, per_expert, half + LANES), BF16)],
         keep, stats, came,
-        limit=16 << 20,
+        flops=COVER_FLOPS, limit=16 << 20,
     )
     both = ("expert", "chip")
     flat = packed.reshape((experts * chips,) + packed.shape[2:])
     mine = lax.all_to_all(flat, both, split_axis=0, concat_axis=0, tiled=True)
     swapped = lax.ppermute(mine, "core", SWAP)
-    acc, w_near = call(
+    (acc,) = call(
         own_hidden_kernel,
-        [((slots, units), F32), ((near_units, width), BF16)],
-        mine.reshape(packed.shape), w_own, w_out,
-        copies=1, in_hbm=(2,), stay=(1,), flops=2 * slots * half * units, limit=16 << 20,
-    )
-    w_other = (w_other_first, w_other_second)
-    pieces = math.gcd((units - near_units) // LANES, 4)
-    send, hidden, w_rest = call(
+        [((slots, units), F32)],
+        mine.reshape(packed.shape), w_in,
+        flops=2 * slots * half * units, limit=16 << 20,
+    )
+    send, hidden = call(
         send_terms_kernel,
-        [((slots, half), BF16), ((slots, units), BF16), ((units - near_units, width), BF16)],
-        acc, swapped.reshape(packed.shape), *w_other, w_near, w_out,
-        copies=pieces, in_hbm=(5,), stay=(2,), flops=4 * slots * half * units, limit=16 << 20,
+        [((slots, half), BF16), ((slots, units), BF16)],
+        acc, swapped.reshape(packed.shape), w_in, w_out,
+        flops=4 * slots * half * units, limit=16 << 20,
     )
     came = lax.ppermute(send, "core", SWAP)
     (keep,) = call(
-        keep_terms_kernel,
-        [((slots, half), F32)],
-        hidden, w_near, w_rest,
-        flops=2 * slots * half * units,
+        keep_terms_kernel, [((slots, half), F32)], hidden, w_out, flops=2 * slots * half * units
     )
     (packed,) = call(
         pair_sum_kernel, [((experts, chips, per_expert, half), BF16)], keep, came, limit=16 << 20

time: 55.9 us -> 53 us (0.948)
  Pallas kernels: 12.6 us -> 7.2 us
  waiting for transfers between devices: 4.79 us -> 7.9 us
  blocking collectives: 30.5 us -> 29.9 us
    pallas_call x11, Pallas kernels: 11.6 us -> 6.12 us  [call(): pl.pallas_call(kernel, out_shape=shapes, in_specs=[pl.BlockSpec(memory_sp...]
    ppermute x2, waiting for transfers between devices: 0.33 us -> 1.56 us  [on_device(): came = lax.ppermute(send, 'core', SWAP)]
    ppermute x1, waiting for transfers between devices: 0.01 us -> 0.88 us  [on_device(): swapped = lax.ppermute(stack, 'core', SWAP)]
    ppermute x4, starting transfers between devices: 6.3 us -> 7.05 us  [gather_keys(): blocks.append(lax.ppermute(keys, axes, pairs))]
    ppermute x2, waiting for transfers between devices: 1.23 us -> 1.96 us  [on_device(): swapped = lax.ppermute(mine, 'core', SWAP)]
    ppermute x2, starting transfers between devices: 1.05 us -> 0.41 us  [on_device(): came = lax.ppermute(send, 'core', SWAP)]
    all_to_all x2, blocking collectives: 30.5 us -> 29.9 us  [on_device(): mine = lax.all_to_all(flat, both, split_axis=0, concat_axis=0, tiled=True)]
  transfers between devices with their start and end apart: 9 -> 9, of which waited for: 4 -> 7; matrix products, arithmetic and copies ran while one was open for 0% -> 0% of each run, Pallas kernels for 14% -> 7%
where the time goes in v7:
time: 53 us; the launch traced here: 52.8 us
  blocking collectives  29.9 us (56%)
  waiting for transfers between devices  7.9 us (15%)
  starting transfers between devices  7.64 us (14%)
  Pallas kernels  7.2 us (14%)
    all_to_all x2, blocking collectives, on_device(): mine = lax.all_to_all(flat, both, split_axis=0, concat_axis=0, tiled=True)  29.9 us
    ppermute x4, starting transfers between devices, gather_keys(): blocks.append(lax.ppermute(keys, axes, pairs))  7.05 us
    pallas_call x11, Pallas kernels, call(): pl.pallas_call(kernel, out_shape=shapes, in_specs=[pl.BlockSpec(memory_sp...  6.12 us
    ppermute x4, waiting for transfers between devices, gather_keys(): blocks.append(lax.ppermute(keys, axes, pairs))  3.51 us
    ppermute x2, waiting for transfers between devices, on_device(): swapped = lax.ppermute(mine, 'core', SWAP)  1.96 us
    ppermute x2, waiting for transfers between devices, on_device(): came = lax.ppermute(send, 'core', SWAP)  1.56 us
    pallas_call x1, Pallas kernels, on_device(): pl.pallas_call(mix_kernel, out_shape=jax.ShapeDtypeStruct((count, width),...  1.08 us
  transfers between devices with their start and end apart: 9, of which 7 were waited for; matrix products, arithmetic and copies ran while one was open for 0% of the time, Pallas kernels for 7%

profile of v7, /device:TPU:0, one launch (start us, length us, event | category | flops | bytes accessed | tf_op | source)
XLA Modules:
  0.0 52.8 jit_solution(14655182185034146032)
XLA Ops:
  0.0 0.0 copy-start
  0.0 3.1 %collective-permute-start.3 = (bf16[8,2048]{1,0:T(8,128)(2,1)}, bf16[8,2048]{1,0:T(8,128)(2,1)S(1)}, u32[]{:S(2)}, u32[]{:S(2)}) collective-permute-start(bf16[8,2048]{1,0:T(8,128)(2,1)} %bitcast.22), channel_id=1, source_target_pairs={{0,2},{1,3},{2,0},{3,1},{4,6},{5,7},{6,4},{7,5},{8,15},{9,14},{10,... | collective-permute-start | bytes 98312 | tf_op jit(solution)/shard_map/ppermute | solution.py:77
  3.1 2.6 %collective-permute-start.2 = (bf16[8,2048]{1,0:T(8,128)(2,1)}, bf16[8,2048]{1,0:T(8,128)(2,1)S(1)}, u32[]{:S(2)}, u32[]{:S(2)}) collective-permute-start(bf16[8,2048]{1,0:T(8,128)(2,1)} %bitcast.23), channel_id=1, source_target_pairs={{0,4},{1,5},{2,6},{3,7},{4,0},{5,1},{6,2},{7,3},{8,13},{9,12},{10,... | collective-permute-start | bytes 98312 | tf_op jit(solution)/shard_map/ppermute | solution.py:77
  5.6 0.0 collective-permute-start.1
  5.6 1.4 %collective-permute-start = (bf16[8,2048]{1,0:T(8,128)(2,1)}, bf16[8,2048]{1,0:T(8,128)(2,1)S(1)}, u32[]{:S(2)}, u32[]{:S(2)}) collective-permute-start(bf16[8,2048]{1,0:T(8,128)(2,1)} %bitcast.25), channel_id=1, source_target_pairs={{0,0},{1,1},{2,2},{3,3},{4,4},{5,5},{6,6},{7,7},{8,9},{9,8},{10,11... | collective-permute-start | bytes 98312 | tf_op jit(solution)/shard_map/ppermute | solution.py:77
  7.1 1.2 %shard_map.46.tok_ref = bf16[224,2048]{1,0:T(8,128)(2,1)S(1)} custom-call(bf16[224,2048]{1,0:T(8,128)(2,1)} %bitcast.21), custom_call_target="tpu_custom_call" | custom-call | bytes 917504 | tf_op jit(solution)/shard_map/pallas_call | solution.py:221
  8.2 0.0 collective-permute-done.3.refs_3_
  8.3 0.5 %collective-permute-done.2.refs_2_ = bf16[8,2048]{1,0:T(8,128)(2,1)S(1)} collective-permute-done((bf16[8,2048]{1,0:T(8,128)(2,1)}, bf16[8,2048]{1,0:T(8,128)(2,1)S(1)}, u32[]{:S(2)}, u32[]{:S(2)}) %collective-permute-start.2) | collective-permute-done | bytes 32800 | tf_op jit(solution)/shard_map/ppermute | solution.py:77
  8.8 3.0 %collective-permute-done.1.refs_1_ = bf16[8,2048]{1,0:T(8,128)(2,1)S(1)} collective-permute-done((bf16[8,2048]{1,0:T(8,128)(2,1)}, bf16[8,2048]{1,0:T(8,128)(2,1)S(1)}, u32[]{:S(2)}, u32[]{:S(2)}) %collective-permute-start.1) | collective-permute-done | bytes 32800 | tf_op jit(solution)/shard_map/ppermute | solution.py:77
  11.8 0.0 collective-permute-done.refs_0_
  11.8 0.2 collective-permute-start.4
  11.9 0.4 shard_map.48.part_ref
  12.3 0.9 %collective-permute-done.4.swapped_ref = bf16[4,8,2048]{2,1,0:T(8,128)(2,1)S(1)} collective-permute-done((bf16[4,8,2048]{2,1,0:T(8,128)(2,1)S(1)}, bf16[4,8,2048]{2,1,0:T(8,128)(2,1)S(1)}, u32[]{:S(2)}, u32[]{:S(2)}) %collective-permute-start.4) | collective-permute-done | bytes 131104 | tf_op jit(solution)/shard_map/ppermute | solution.py:260
  13.2 0.8 %shard_map.49 = (f32[64,224]{1,0:T(8,128)S(1)}, bf16[64,224]{1,0:T(8,128)(2,1)S(1)}, f32[64,128]{1,0:T(8,128)S(1)}, bf16[64,1152]{1,0:T(8,128)(2,1)S(1)}) custom-call(bf16[4,8,2048]{2,1,0:T(8,128)(2,1)S(1)} %collective-permute-done.4.swapped_ref, f32[32,224]{1,0:T(8,128)S(1)} %shard_map.48.part_ref, bf16[224,2048]{1,0:T(8,128)(2,1)S(1)} %shard_map.46.tok_ref), custom_call_target="tpu_custom_call" | custom-call | flops 58720256 | bytes 266240 | tf_op jit(solution)/shard_map/pallas_call | solution.py:221
  14.0 0.0 copy-start.1
  14.0 0.2 collective-permute-start.5
  14.2 0.2 shard_map.50
  14.4 1.0 %collective-permute-done.5.came_ref = bf16[64,1152]{1,0:T(8,128)(2,1)S(1)} collective-permute-done((bf16[64,1152]{1,0:T(8,128)(2,1)S(1)}, bf16[64,1152]{1,0:T(8,128)(2,1)S(1)}, u32[]{:S(2)}, u32[]{:S(2)}) %collective-permute-start.5) | collective-permute-done | bytes 147488 | tf_op jit(solution)/shard_map/ppermute | solution.py:277
  15.4 0.3 shard_map.51
  15.8 16.5 %all_to_all.10 = bf16[16,8,1152]{2,1,0:T(8,128)(2,1)S(1)} all-to-all(bf16[16,8,1152]{2,1,0:T(8,128)(2,1)S(1)} %bitcast.19), channel_id=1, replica_groups=mesh['chip'=2,'core'=2,'expert'=8] {'expert','chip'}, dimensions={0} | all-to-all | bytes 589824 | tf_op jit(solution)/shard_map/all_to_all | solution.py:292
  32.3 0.0 collective-permute-start.6
  32.3 0.0 copy-done
  32.3 0.9 %shard_map.52.acc_ref = f32[64,1536]{1,0:T(8,128)S(1)} custom-call(bf16[8,2,8,1152]{3,2,1,0:T(8,128)(2,1)S(1)} %bitcast.15, bf16[2048,1536]{1,0:T(8,128)(2,1)S(1)} %bitcast.11), custom_call_target="tpu_custom_call" | custom-call | flops 201326592 | bytes 393216 | tf_op jit(solution)/shard_map/pallas_call | solution.py:221
  33.1 0.7 %collective-permute-done.6 = bf16[16,8,1152]{2,1,0:T(8,128)(2,1)S(1)} collective-permute-done((bf16[16,8,1152]{2,1,0:T(8,128)(2,1)S(1)}, bf16[16,8,1152]{2,1,0:T(8,128)(2,1)S(1)}, u32[]{:S(2)}, u32[]{:S(2)}) %collective-permute-start.6) | collective-permute-done | bytes 294944 | tf_op jit(solution)/shard_map/ppermute | solution.py:293
  33.8 0.0 copy-done.1
  33.8 1.4 %shard_map.53 = (bf16[64,1024]{1,0:T(8,128)(2,1)S(1)}, bf16[64,1536]{1,0:T(8,128)(2,1)S(1)}) custom-call(f32[64,1536]{1,0:T(8,128)S(1)} %shard_map.52.acc_ref, bf16[8,2,8,1152]{3,2,1,0:T(8,128)(2,1)S(1)} %bitcast.18, bf16[2048,1536]{1,0:T(8,128)(2,1)S(1)} %bitcast.12, bf16[1536,2048]{1,0:T(8,128)(2,1)S(1)} %bitcast.13), custom_call_target="tpu_custom_call" | custom-call | flops 402653184 | bytes 327680 | tf_op jit(solution)/shard_map/pallas_call | solution.py:221
  35.3 0.2 collective-permute-start.7
  35.5 0.7 %shard_map.54.keep_ref = f32[64,1024]{1,0:T(8,128)S(1)} custom-call(bf16[64,1536]{1,0:T(8,128)(2,1)S(1)} %get-tuple-element.29.hidden_ref, bf16[1536,2048]{1,0:T(8,128)(2,1)S(1)} %bitcast.14), custom_call_target="tpu_custom_call" | custom-call | flops 201326592 | bytes 262144 | tf_op jit(solution)/shard_map/pallas_call | solution.py:221
  36.1 0.6 %collective-permute-done.7.came_ref = bf16[64,1024]{1,0:T(8,128)(2,1)S(1)} collective-permute-done((bf16[64,1024]{1,0:T(8,128)(2,1)S(1)}, bf16[64,1024]{1,0:T(8,128)(2,1)S(1)}, u32[]{:S(2)}, u32[]{:S(2)}) %collective-permute-start.7) | collective-permute-done | bytes 131104 | tf_op jit(solution)/shard_map/ppermute | solution.py:306
  36.7 13.4 %all_to_all.11 = bf16[16,8,1024]{2,1,0:T(8,128)(2,1)S(1)} all-to-all(bf16[16,8,1024]{2,1,0:T(8,128)(2,1)S(1)} %bitcast.17), channel_id=1, replica_groups=mesh['chip'=2,'core'=2,'expert'=8] {'expert','chip'}, dimensions={0} | all-to-all | bytes 524288 | tf_op jit(solution)/shard_map/all_to_all | solution.py:314
  50.1 0.0 collective-permute-start.8
  50.1 0.3 shard_map.56.half_ref
  50.4 1.2 %collective-permute-done.8 = bf16[16,8,1024]{2,1,0:T(8,128)(2,1)S(1)} collective-permute-done((bf16[16,8,1024]{2,1,0:T(8,128)(2,1)S(1)}, bf16[16,8,1024]{2,1,0:T(8,128)(2,1)S(1)}, u32[]{:S(2)}, u32[]{:S(2)}) %collective-permute-start.8) | collective-permute-done | bytes 262176 | tf_op jit(solution)/shard_map/ppermute | solution.py:315
  51.7 1.1 %shard_map.57 = bf16[224,2048]{1,0:T(8,128)(2,1)} custom-call(bf16[64,224]{1,0:T(8,128)(2,1)S(1)} %get-tuple-element.25.mix_ref, bf16[8,2,8,1024]{3,2,1,0:T(8,128)(2,1)S(1)} %bitcast.20, bf16[224,1024]{1,0:T(8,128)(2,1)S(1)} %shard_map.56.half_ref), custom_call_target="tpu_custom_call" | custom-call | flops 29360128 | bytes 917504 | tf_op jit(solution)/shard_map/pallas_call | solution.py:322
  (2 shorter events, 0.0 us)
Async XLA Ops:
  0.0 32.3 %copy-start = (bf16[1,2048,1536]{2,1,0:T(8,128)(2,1)S(1)}, bf16[1,2048,1536]{2,1,0:T(8,128)(2,1)}, u32[]{:S(2)}) copy-start(bf16[1,2048,1536]{2,1,0:T(8,128)(2,1)} %param.6) | copy-start | bytes 18874372
  0.0 8.2 %collective-permute-start.3 = (bf16[8,2048]{1,0:T(8,128)(2,1)}, bf16[8,2048]{1,0:T(8,128)(2,1)S(1)}, u32[]{:S(2)}, u32[]{:S(2)}) collective-permute-start(bf16[8,2048]{1,0:T(8,128)(2,1)} %bitcast.22), channel_id=1, source_target_pairs={{0,2},{1,3},{2,0},{3,1},{4,6},{5,7},{6,4},{7,5},{8,15},{9,14},{10,... | collective-permute-start | bytes 98312 | tf_op jit(solution)/shard_map/ppermute | solution.py:77
  3.1 5.7 %collective-permute-start.2 = (bf16[8,2048]{1,0:T(8,128)(2,1)}, bf16[8,2048]{1,0:T(8,128)(2,1)S(1)}, u32[]{:S(2)}, u32[]{:S(2)}) collective-permute-start(bf16[8,2048]{1,0:T(8,128)(2,1)} %bitcast.23), channel_id=1, source_target_pairs={{0,4},{1,5},{2,6},{3,7},{4,0},{5,1},{6,2},{7,3},{8,13},{9,12},{10,... | collective-permute-start | bytes 98312 | tf_op jit(solution)/shard_map/ppermute | solution.py:77
  5.6 6.1 %collective-permute-start.1 = (bf16[8,2048]{1,0:T(8,128)(2,1)}, bf16[8,2048]{1,0:T(8,128)(2,1)S(1)}, u32[]{:S(2)}, u32[]{:S(2)}) collective-permute-start(bf16[8,2048]{1,0:T(8,128)(2,1)} %bitcast.24), channel_id=1, source_target_pairs={{0,6},{1,7},{2,4},{3,5},{4,2},{5,3},{6,0},{7,1},{8,11},{9,10},{10,... | collective-permute-start | bytes 98312 | tf_op jit(solution)/shard_map/ppermute | solution.py:77
  5.6 6.1 %collective-permute-start = (bf16[8,2048]{1,0:T(8,128)(2,1)}, bf16[8,2048]{1,0:T(8,128)(2,1)S(1)}, u32[]{:S(2)}, u32[]{:S(2)}) collective-permute-start(bf16[8,2048]{1,0:T(8,128)(2,1)} %bitcast.25), channel_id=1, source_target_pairs={{0,0},{1,1},{2,2},{3,3},{4,4},{5,5},{6,6},{7,7},{8,9},{9,8},{10,11... | collective-permute-start | bytes 98312 | tf_op jit(solution)/shard_map/ppermute | solution.py:77
  11.8 1.4 %collective-permute-start.4 = (bf16[4,8,2048]{2,1,0:T(8,128)(2,1)S(1)}, bf16[4,8,2048]{2,1,0:T(8,128)(2,1)S(1)}, u32[]{:S(2)}, u32[]{:S(2)}) collective-permute-start(bf16[4,8,2048]{2,1,0:T(8,128)(2,1)S(1)} %shard_map.47.stack_ref), channel_id=1, source_target_pairs={{0,8},{8,0},{1,9},{9,1},{2,10},{10,2},{3,11},{11,3},{4,12},{12,4},... | collective-permute-start | bytes 393224 | tf_op jit(solution)/shard_map/ppermute | solution.py:260
  14.0 19.9 %copy-start.1 = (bf16[1,1536,2048]{2,1,0:T(8,128)(2,1)S(1)}, bf16[1,1536,2048]{2,1,0:T(8,128)(2,1)}, u32[]{:S(2)}) copy-start(bf16[1,1536,2048]{2,1,0:T(8,128)(2,1)} %param.7) | copy-start | bytes 18874372
  14.0 1.4 %collective-permute-start.5 = (bf16[64,1152]{1,0:T(8,128)(2,1)S(1)}, bf16[64,1152]{1,0:T(8,128)(2,1)S(1)}, u32[]{:S(2)}, u32[]{:S(2)}) collective-permute-start(bf16[64,1152]{1,0:T(8,128)(2,1)S(1)} %get-tuple-element.28), channel_id=1, source_target_pairs={{0,8},{8,0},{1,9},{9,1},{2,10},{10,2},{3,11},{11,3},{4,12},{12,4},... | collective-permute-start | bytes 442376 | tf_op jit(solution)/shard_map/ppermute | solution.py:277
  32.3 1.6 %collective-permute-start.6 = (bf16[16,8,1152]{2,1,0:T(8,128)(2,1)S(1)}, bf16[16,8,1152]{2,1,0:T(8,128)(2,1)S(1)}, u32[]{:S(2)}, u32[]{:S(2)}) collective-permute-start(bf16[16,8,1152]{2,1,0:T(8,128)(2,1)S(1)} %all_to_all.10), channel_id=1, source_target_pairs={{0,8},{8,0},{1,9},{9,1},{2,10},{10,2},{3,11},{11,3},{4,12},{12,4},... | collective-permute-start | bytes 884744 | tf_op jit(solution)/shard_map/ppermute | solution.py:293
  35.3 1.4 %collective-permute-start.7 = (bf16[64,1024]{1,0:T(8,128)(2,1)S(1)}, bf16[64,1024]{1,0:T(8,128)(2,1)S(1)}, u32[]{:S(2)}, u32[]{:S(2)}) collective-permute-start(bf16[64,1024]{1,0:T(8,128)(2,1)S(1)} %get-tuple-element.30), channel_id=1, source_target_pairs={{0,8},{8,0},{1,9},{9,1},{2,10},{10,2},{3,11},{11,3},{4,12},{12,4},... | collective-permute-start | bytes 393224 | tf_op jit(solution)/shard_map/ppermute | solution.py:306
  50.1 1.5 %collective-permute-start.8 = (bf16[16,8,1024]{2,1,0:T(8,128)(2,1)S(1)}, bf16[16,8,1024]{2,1,0:T(8,128)(2,1)S(1)}, u32[]{:S(2)}, u32[]{:S(2)}) collective-permute-start(bf16[16,8,1024]{2,1,0:T(8,128)(2,1)S(1)} %all_to_all.11), channel_id=1, source_target_pairs={{0,8},{8,0},{1,9},{9,1},{2,10},{10,2},{3,11},{11,3},{4,12},{12,4},... | collective-permute-start | bytes 786440 | tf_op jit(solution)/shard_map/ppermute | solution.py:315

commit v8 on v7

--- a/solution.py
+++ b/solution.py
@@ -17,9 +17,10 @@
 
 
 def column_halves(half):
-    core = lax.axis_index("core")
-    own = pl.ds(pl.multiple_of(core * half, LANES), half)
-    other = pl.ds(pl.multiple_of((1 - core) * half, LANES), half)
+    high = lax.axis_index("expert") // (lax.axis_size("expert") // 2)
+    side = (lax.axis_index("core") + high) % 2
+    own = pl.ds(pl.multiple_of(side * half, LANES), half)
+    other = pl.ds(pl.multiple_of((1 - side) * half, LANES), half)
     return own, other
 
 
@@ -61,7 +62,9 @@
 
 
 def held_masks(experts):
-    return [((experts - 2 * k) % experts, 2 * k + 1) for k in range(experts // 2)]
+    odd = list(range(1, experts, 2))
+    odd[-2:] = odd[:-3:-1]
+    return [((experts - 2 * k) % experts, mask) for k, mask in enumerate(odd)]
 
 
 def gather_keys(keys, experts, chips):
@@ -287,9 +290,20 @@
         keep, stats, came,
         flops=COVER_FLOPS, limit=16 << 20,
     )
-    both = ("expert", "chip")
+    groups = [
+        [
+            (chip * 2 + (side + 2 * e // experts) % 2) * experts + e
+            for e in range(experts)
+            for chip in range(chips)
+        ]
+        for side in range(2)
+    ]
+    exchange = functools.partial(
+        lax.all_to_all, axis_name=("chip", "core", "expert"), split_axis=0, concat_axis=0,
+        axis_index_groups=groups, tiled=True,
+    )
     flat = packed.reshape((experts * chips,) + packed.shape[2:])
-    mine = lax.all_to_all(flat, both, split_axis=0, concat_axis=0, tiled=True)
+    mine = exchange(flat)
     swapped = lax.ppermute(mine, "core", SWAP)
     (acc,) = call(
         own_hidden_kernel,
@@ -311,7 +325,7 @@
         pair_sum_kernel, [((experts, chips, per_expert, half), BF16)], keep, came, limit=16 << 20
     )
     flat = packed.reshape((experts * chips,) + packed.shape[2:])
-    mine = lax.all_to_all(flat, both, split_axis=0, concat_axis=0, tiled=True)
+    mine = exchange(flat)
     swapped = lax.ppermute(mine, "core", SWAP)
     (own_half,) = call(
         own_mix_kernel,

time: 53 us -> 51.4 us (0.970)
  blocking collectives: 29.9 us -> 27.9 us
  starting transfers between devices: 7.64 us -> 8.63 us
  waiting for transfers between devices: 7.9 us -> 7.24 us
    all_to_all x2, blocking collectives: 29.9 us -> 27.9 us  [on_device(): mine = exchange(flat)]
    ppermute x2, starting transfers between devices: 0.01 us -> 1.08 us  [on_device(): swapped = lax.ppermute(mine, 'core', SWAP)]
    ppermute x2, waiting for transfers between devices: 1.96 us -> 1.42 us  [on_device(): swapped = lax.ppermute(mine, 'core', SWAP)]
where the time goes in v8:
time: 51.4 us; the launch traced here: 51.1 us
  blocking collectives  27.9 us (54%)
  starting transfers between devices  8.63 us (17%)
  waiting for transfers between devices  7.24 us (14%)
  Pallas kernels  7.22 us (14%)
    all_to_all x2, blocking collectives, on_device(): mine = exchange(flat)  27.9 us
    ppermute x4, starting transfers between devices, gather_keys(): blocks.append(lax.ppermute(keys, axes, pairs))  7.05 us
    pallas_call x11, Pallas kernels, call(): pl.pallas_call(kernel, out_shape=shapes, in_specs=[pl.BlockSpec(memory_sp...  6.13 us
    ppermute x4, waiting for transfers between devices, gather_keys(): blocks.append(lax.ppermute(keys, axes, pairs))  3.32 us
    ppermute x2, waiting for transfers between devices, on_device(): came = lax.ppermute(send, 'core', SWAP)  1.54 us
    ppermute x2, waiting for transfers between devices, on_device(): swapped = lax.ppermute(mine, 'core', SWAP)  1.42 us
    pallas_call x1, Pallas kernels, on_device(): pl.pallas_call(mix_kernel, out_shape=jax.ShapeDtypeStruct((count, width),...  1.09 us
    ppermute x2, starting transfers between devices, on_device(): swapped = lax.ppermute(mine, 'core', SWAP)  1.08 us
  transfers between devices with their start and end apart: 9, of which 7 were waited for; matrix products, arithmetic and copies ran while one was open for 0% of the time, Pallas kernels for 7%

profile of v8, /device:TPU:0, one launch (start us, length us, event | category | flops | bytes accessed | tf_op | source)
XLA Modules:
  0.0 51.1 jit_solution(14762025495614906323)
XLA Ops:
  0.0 0.0 copy-start
  0.0 3.1 %collective-permute-start.3 = (bf16[8,2048]{1,0:T(8,128)(2,1)}, bf16[8,2048]{1,0:T(8,128)(2,1)S(1)}, u32[]{:S(2)}, u32[]{:S(2)}) collective-permute-start(bf16[8,2048]{1,0:T(8,128)(2,1)} %bitcast.22), channel_id=1, source_target_pairs={{0,2},{1,3},{2,0},{3,1},{4,6},{5,7},{6,4},{7,5},{8,13},{9,12},{10,... | collective-permute-start | bytes 98312 | tf_op jit(solution)/shard_map/ppermute | solution.py:80
  3.1 2.6 %collective-permute-start.2 = (bf16[8,2048]{1,0:T(8,128)(2,1)}, bf16[8,2048]{1,0:T(8,128)(2,1)S(1)}, u32[]{:S(2)}, u32[]{:S(2)}) collective-permute-start(bf16[8,2048]{1,0:T(8,128)(2,1)} %bitcast.23), channel_id=1, source_target_pairs={{0,4},{1,5},{2,6},{3,7},{4,0},{5,1},{6,2},{7,3},{8,15},{9,14},{10,... | collective-permute-start | bytes 98312 | tf_op jit(solution)/shard_map/ppermute | solution.py:80
  5.6 0.0 collective-permute-start.1
  5.6 1.4 %collective-permute-start = (bf16[8,2048]{1,0:T(8,128)(2,1)}, bf16[8,2048]{1,0:T(8,128)(2,1)S(1)}, u32[]{:S(2)}, u32[]{:S(2)}) collective-permute-start(bf16[8,2048]{1,0:T(8,128)(2,1)} %bitcast.25), channel_id=1, source_target_pairs={{0,0},{1,1},{2,2},{3,3},{4,4},{5,5},{6,6},{7,7},{8,9},{9,8},{10,11... | collective-permute-start | bytes 98312 | tf_op jit(solution)/shard_map/ppermute | solution.py:80
  7.1 1.2 %shard_map.46.tok_ref = bf16[224,2048]{1,0:T(8,128)(2,1)S(1)} custom-call(bf16[224,2048]{1,0:T(8,128)(2,1)} %bitcast.21), custom_call_target="tpu_custom_call" | custom-call | bytes 917504 | tf_op jit(solution)/shard_map/pallas_call | solution.py:224
  8.2 0.0 collective-permute-done.3.refs_3_
  8.3 0.2 collective-permute-done.2.refs_2_
  8.4 3.1 %collective-permute-done.1.refs_1_ = bf16[8,2048]{1,0:T(8,128)(2,1)S(1)} collective-permute-done((bf16[8,2048]{1,0:T(8,128)(2,1)}, bf16[8,2048]{1,0:T(8,128)(2,1)S(1)}, u32[]{:S(2)}, u32[]{:S(2)}) %collective-permute-start.1) | collective-permute-done | bytes 32800 | tf_op jit(solution)/shard_map/ppermute | solution.py:80
  11.6 0.0 collective-permute-done.refs_0_
  11.6 0.1 collective-permute-start.4
  11.7 0.4 shard_map.48.part_ref
  12.0 1.0 %collective-permute-done.4.swapped_ref = bf16[4,8,2048]{2,1,0:T(8,128)(2,1)S(1)} collective-permute-done((bf16[4,8,2048]{2,1,0:T(8,128)(2,1)S(1)}, bf16[4,8,2048]{2,1,0:T(8,128)(2,1)S(1)}, u32[]{:S(2)}, u32[]{:S(2)}) %collective-permute-start.4) | collective-permute-done | bytes 131104 | tf_op jit(solution)/shard_map/ppermute | solution.py:263
  13.0 0.8 %shard_map.49 = (f32[64,224]{1,0:T(8,128)S(1)}, bf16[64,224]{1,0:T(8,128)(2,1)S(1)}, f32[64,128]{1,0:T(8,128)S(1)}, bf16[64,1152]{1,0:T(8,128)(2,1)S(1)}) custom-call(bf16[4,8,2048]{2,1,0:T(8,128)(2,1)S(1)} %collective-permute-done.4.swapped_ref, f32[32,224]{1,0:T(8,128)S(1)} %shard_map.48.part_ref, bf16[224,2048]{1,0:T(8,128)(2,1)S(1)} %shard_map.46.tok_ref), custom_call_target="tpu_custom_call" | custom-call | flops 58720256 | bytes 266240 | tf_op jit(solution)/shard_map/pallas_call | solution.py:224
  13.8 0.0 copy-start.1
  13.8 0.2 collective-permute-start.5
  14.0 0.2 shard_map.50
  14.2 1.0 %collective-permute-done.5.came_ref = bf16[64,1152]{1,0:T(8,128)(2,1)S(1)} collective-permute-done((bf16[64,1152]{1,0:T(8,128)(2,1)S(1)}, bf16[64,1152]{1,0:T(8,128)(2,1)S(1)}, u32[]{:S(2)}, u32[]{:S(2)}) %collective-permute-start.5) | collective-permute-done | bytes 147488 | tf_op jit(solution)/shard_map/ppermute | solution.py:280
  15.2 0.3 shard_map.51
  15.6 14.9 %all_to_all.10 = bf16[16,8,1152]{2,1,0:T(8,128)(2,1)S(1)} all-to-all(bf16[16,8,1152]{2,1,0:T(8,128)(2,1)S(1)} %bitcast.19), channel_id=1, replica_groups={{0,16,1,17,2,18,3,19,12,28,13,29,14,30,15,31},{8,24,9,25,10,26,11,27,4,..., dimensions={0} | all-to-all | bytes 589824 | tf_op jit(solution)/shard_map/all_to_all | solution.py:306
  30.5 0.2 collective-permute-start.6
  30.7 0.0 copy-done
  30.7 0.9 %shard_map.52.acc_ref = f32[64,1536]{1,0:T(8,128)S(1)} custom-call(bf16[8,2,8,1152]{3,2,1,0:T(8,128)(2,1)S(1)} %bitcast.15, bf16[2048,1536]{1,0:T(8,128)(2,1)S(1)} %bitcast.11), custom_call_target="tpu_custom_call" | custom-call | flops 201326592 | bytes 393216 | tf_op jit(solution)/shard_map/pallas_call | solution.py:224
  31.5 0.6 %collective-permute-done.6 = bf16[16,8,1152]{2,1,0:T(8,128)(2,1)S(1)} collective-permute-done((bf16[16,8,1152]{2,1,0:T(8,128)(2,1)S(1)}, bf16[16,8,1152]{2,1,0:T(8,128)(2,1)S(1)}, u32[]{:S(2)}, u32[]{:S(2)}) %collective-permute-start.6) | collective-permute-done | bytes 294944 | tf_op jit(solution)/shard_map/ppermute | solution.py:307
  32.1 0.0 copy-done.1
  32.1 1.4 %shard_map.53 = (bf16[64,1024]{1,0:T(8,128)(2,1)S(1)}, bf16[64,1536]{1,0:T(8,128)(2,1)S(1)}) custom-call(f32[64,1536]{1,0:T(8,128)S(1)} %shard_map.52.acc_ref, bf16[8,2,8,1152]{3,2,1,0:T(8,128)(2,1)S(1)} %bitcast.18, bf16[2048,1536]{1,0:T(8,128)(2,1)S(1)} %bitcast.12, bf16[1536,2048]{1,0:T(8,128)(2,1)S(1)} %bitcast.13), custom_call_target="tpu_custom_call" | custom-call | flops 402653184 | bytes 327680 | tf_op jit(solution)/shard_map/pallas_call | solution.py:224
  33.5 0.2 collective-permute-start.7
  33.8 0.7 %shard_map.54.keep_ref = f32[64,1024]{1,0:T(8,128)S(1)} custom-call(bf16[64,1536]{1,0:T(8,128)(2,1)S(1)} %get-tuple-element.29.hidden_ref, bf16[1536,2048]{1,0:T(8,128)(2,1)S(1)} %bitcast.14), custom_call_target="tpu_custom_call" | custom-call | flops 201326592 | bytes 262144 | tf_op jit(solution)/shard_map/pallas_call | solution.py:224
  34.4 0.5 %collective-permute-done.7.came_ref = bf16[64,1024]{1,0:T(8,128)(2,1)S(1)} collective-permute-done((bf16[64,1024]{1,0:T(8,128)(2,1)S(1)}, bf16[64,1024]{1,0:T(8,128)(2,1)S(1)}, u32[]{:S(2)}, u32[]{:S(2)}) %collective-permute-start.7) | collective-permute-done | bytes 131104 | tf_op jit(solution)/shard_map/ppermute | solution.py:320
  35.0 13.0 %all_to_all.11 = bf16[16,8,1024]{2,1,0:T(8,128)(2,1)S(1)} all-to-all(bf16[16,8,1024]{2,1,0:T(8,128)(2,1)S(1)} %bitcast.17), channel_id=1, replica_groups={{0,16,1,17,2,18,3,19,12,28,13,29,14,30,15,31},{8,24,9,25,10,26,11,27,4,..., dimensions={0} | all-to-all | bytes 524288 | tf_op jit(solution)/shard_map/all_to_all | solution.py:328
  47.9 0.9 %collective-permute-start.8 = (bf16[16,8,1024]{2,1,0:T(8,128)(2,1)S(1)}, bf16[16,8,1024]{2,1,0:T(8,128)(2,1)S(1)}, u32[]{:S(2)}, u32[]{:S(2)}) collective-permute-start(bf16[16,8,1024]{2,1,0:T(8,128)(2,1)S(1)} %all_to_all.11), channel_id=1, source_target_pairs={{0,8},{8,0},{1,9},{9,1},{2,10},{10,2},{3,11},{11,3},{4,12},{12,4},... | collective-permute-start | bytes 786440 | tf_op jit(solution)/shard_map/ppermute | solution.py:329
  48.8 0.3 shard_map.56.half_ref
  49.1 0.9 %collective-permute-done.8 = bf16[16,8,1024]{2,1,0:T(8,128)(2,1)S(1)} collective-permute-done((bf16[16,8,1024]{2,1,0:T(8,128)(2,1)S(1)}, bf16[16,8,1024]{2,1,0:T(8,128)(2,1)S(1)}, u32[]{:S(2)}, u32[]{:S(2)}) %collective-permute-start.8) | collective-permute-done | bytes 262176 | tf_op jit(solution)/shard_map/ppermute | solution.py:329
  50.0 1.1 %shard_map.57 = bf16[224,2048]{1,0:T(8,128)(2,1)} custom-call(bf16[64,224]{1,0:T(8,128)(2,1)S(1)} %get-tuple-element.25.mix_ref, bf16[8,2,8,1024]{3,2,1,0:T(8,128)(2,1)S(1)} %bitcast.20, bf16[224,1024]{1,0:T(8,128)(2,1)S(1)} %shard_map.56.half_ref), custom_call_target="tpu_custom_call" | custom-call | flops 29360128 | bytes 917504 | tf_op jit(solution)/shard_map/pallas_call | solution.py:336
  (2 shorter events, 0.0 us)
Async XLA Ops:
  0.0 30.7 %copy-start = (bf16[1,2048,1536]{2,1,0:T(8,128)(2,1)S(1)}, bf16[1,2048,1536]{2,1,0:T(8,128)(2,1)}, u32[]{:S(2)}) copy-start(bf16[1,2048,1536]{2,1,0:T(8,128)(2,1)} %param.6) | copy-start | bytes 18874372
  0.0 8.2 %collective-permute-start.3 = (bf16[8,2048]{1,0:T(8,128)(2,1)}, bf16[8,2048]{1,0:T(8,128)(2,1)S(1)}, u32[]{:S(2)}, u32[]{:S(2)}) collective-permute-start(bf16[8,2048]{1,0:T(8,128)(2,1)} %bitcast.22), channel_id=1, source_target_pairs={{0,2},{1,3},{2,0},{3,1},{4,6},{5,7},{6,4},{7,5},{8,13},{9,12},{10,... | collective-permute-start | bytes 98312 | tf_op jit(solution)/shard_map/ppermute | solution.py:80
  3.1 5.4 %collective-permute-start.2 = (bf16[8,2048]{1,0:T(8,128)(2,1)}, bf16[8,2048]{1,0:T(8,128)(2,1)S(1)}, u32[]{:S(2)}, u32[]{:S(2)}) collective-permute-start(bf16[8,2048]{1,0:T(8,128)(2,1)} %bitcast.23), channel_id=1, source_target_pairs={{0,4},{1,5},{2,6},{3,7},{4,0},{5,1},{6,2},{7,3},{8,15},{9,14},{10,... | collective-permute-start | bytes 98312 | tf_op jit(solution)/shard_map/ppermute | solution.py:80
  5.6 5.9 %collective-permute-start.1 = (bf16[8,2048]{1,0:T(8,128)(2,1)}, bf16[8,2048]{1,0:T(8,128)(2,1)S(1)}, u32[]{:S(2)}, u32[]{:S(2)}) collective-permute-start(bf16[8,2048]{1,0:T(8,128)(2,1)} %bitcast.24), channel_id=1, source_target_pairs={{0,6},{1,7},{2,4},{3,5},{4,2},{5,3},{6,0},{7,1},{8,11},{9,10},{10,... | collective-permute-start | bytes 98312 | tf_op jit(solution)/shard_map/ppermute | solution.py:80
  5.6 5.9 %collective-permute-start = (bf16[8,2048]{1,0:T(8,128)(2,1)}, bf16[8,2048]{1,0:T(8,128)(2,1)S(1)}, u32[]{:S(2)}, u32[]{:S(2)}) collective-permute-start(bf16[8,2048]{1,0:T(8,128)(2,1)} %bitcast.25), channel_id=1, source_target_pairs={{0,0},{1,1},{2,2},{3,3},{4,4},{5,5},{6,6},{7,7},{8,9},{9,8},{10,11... | collective-permute-start | bytes 98312 | tf_op jit(solution)/shard_map/ppermute | solution.py:80
  11.6 1.4 %collective-permute-start.4 = (bf16[4,8,2048]{2,1,0:T(8,128)(2,1)S(1)}, bf16[4,8,2048]{2,1,0:T(8,128)(2,1)S(1)}, u32[]{:S(2)}, u32[]{:S(2)}) collective-permute-start(bf16[4,8,2048]{2,1,0:T(8,128)(2,1)S(1)} %shard_map.47.stack_ref), channel_id=1, source_target_pairs={{0,8},{8,0},{1,9},{9,1},{2,10},{10,2},{3,11},{11,3},{4,12},{12,4},... | collective-permute-start | bytes 393224 | tf_op jit(solution)/shard_map/ppermute | solution.py:263
  13.8 18.3 %copy-start.1 = (bf16[1,1536,2048]{2,1,0:T(8,128)(2,1)S(1)}, bf16[1,1536,2048]{2,1,0:T(8,128)(2,1)}, u32[]{:S(2)}) copy-start(bf16[1,1536,2048]{2,1,0:T(8,128)(2,1)} %param.7) | copy-start | bytes 18874372
  13.8 1.4 %collective-permute-start.5 = (bf16[64,1152]{1,0:T(8,128)(2,1)S(1)}, bf16[64,1152]{1,0:T(8,128)(2,1)S(1)}, u32[]{:S(2)}, u32[]{:S(2)}) collective-permute-start(bf16[64,1152]{1,0:T(8,128)(2,1)S(1)} %get-tuple-element.28), channel_id=1, source_target_pairs={{0,8},{8,0},{1,9},{9,1},{2,10},{10,2},{3,11},{11,3},{4,12},{12,4},... | collective-permute-start | bytes 442376 | tf_op jit(solution)/shard_map/ppermute | solution.py:280
  30.5 1.6 %collective-permute-start.6 = (bf16[16,8,1152]{2,1,0:T(8,128)(2,1)S(1)}, bf16[16,8,1152]{2,1,0:T(8,128)(2,1)S(1)}, u32[]{:S(2)}, u32[]{:S(2)}) collective-permute-start(bf16[16,8,1152]{2,1,0:T(8,128)(2,1)S(1)} %all_to_all.10), channel_id=1, source_target_pairs={{0,8},{8,0},{1,9},{9,1},{2,10},{10,2},{3,11},{11,3},{4,12},{12,4},... | collective-permute-start | bytes 884744 | tf_op jit(solution)/shard_map/ppermute | solution.py:307
  33.5 1.4 %collective-permute-start.7 = (bf16[64,1024]{1,0:T(8,128)(2,1)S(1)}, bf16[64,1024]{1,0:T(8,128)(2,1)S(1)}, u32[]{:S(2)}, u32[]{:S(2)}) collective-permute-start(bf16[64,1024]{1,0:T(8,128)(2,1)S(1)} %get-tuple-element.30), channel_id=1, source_target_pairs={{0,8},{8,0},{1,9},{9,1},{2,10},{10,2},{3,11},{11,3},{4,12},{12,4},... | collective-permute-start | bytes 393224 | tf_op jit(solution)/shard_map/ppermute | solution.py:320
  47.9 2.1 %collective-permute-start.8 = (bf16[16,8,1024]{2,1,0:T(8,128)(2,1)S(1)}, bf16[16,8,1024]{2,1,0:T(8,128)(2,1)S(1)}, u32[]{:S(2)}, u32[]{:S(2)}) collective-permute-start(bf16[16,8,1024]{2,1,0:T(8,128)(2,1)S(1)} %all_to_all.11), channel_id=1, source_target_pairs={{0,8},{8,0},{1,9},{9,1},{2,10},{10,2},{3,11},{11,3},{4,12},{12,4},... | collective-permute-start | bytes 786440 | tf_op jit(solution)/shard_map/ppermute | solution.py:329

commit v9 on v8

--- a/solution.py
+++ b/solution.py
@@ -1,5 +1,6 @@
 import functools
 import math
+import random
 
 import jax
 import jax.numpy as jnp
@@ -11,6 +12,7 @@
 F32 = jnp.float32
 BF16 = jnp.bfloat16
 LANES = 128
+PEER_SEED = 19
 COVER_FLOPS = 10**9
 SWAP = ((0, 1), (1, 0))
 ROWS_BY_ROWS = (((1,), (1,)), ((), ()))
@@ -26,6 +28,17 @@
 
 def row_halves(ref):
     return column_halves(ref.shape[0] // 2)
+
+
+def peer_order(experts, chips):
+    order = [(e, chip) for e in range(experts) for chip in range(chips)]
+    random.Random(PEER_SEED).shuffle(order)
+    return order
+
+
+def by_chip(experts, chips):
+    places = {peer: place for place, peer in enumerate(peer_order(experts, chips))}
+    return [[places[e, chip] for e in range(experts)] for chip in range(chips)]
 
 
 def three_terms(value):
@@ -138,7 +151,8 @@
 
 def chip_sum_kernel(keep_ref, stats_ref, came_ref, out_ref):
     half = keep_ref.shape[1]
-    experts, chips, rows, _ = out_ref.shape
+    peers, rows, _ = out_ref.shape
+    experts = keep_ref.shape[0] // rows
     top, total = stats_ref[:, 0:1], stats_ref[:, 1:2]
     came_top, came_total = read_stats(came_ref[:, half:].astype(F32))
     new_top = jnp.maximum(top, came_top)
@@ -147,20 +161,25 @@
     tile = stats_tile(new_top, total * scale + came_total * came_scale).astype(BF16)
     sums = sums.reshape(experts, rows, half)
     tile = tile.reshape(experts, rows, LANES)
-    for chip in range(chips):
-        out_ref[:, chip, :, :half] = sums
-        out_ref[:, chip, :, half:] = tile
+    for place, (e, _) in enumerate(peer_order(experts, peers // experts)):
+        out_ref[place, :, :half] = sums[e]
+        out_ref[place, :, half:] = tile[e]
 
 
 def slot_inputs_of(ref):
-    seqs, chips, rows, width = ref.shape
+    peers, rows, width = ref.shape
     half = width - LANES
-    stats = [read_stats(ref[:, chip, :, half:].astype(F32)) for chip in range(chips)]
+    seqs = lax.axis_size("expert")
+    blocks = [
+        jnp.concatenate([ref[place] for place in places], axis=0).astype(F32)
+        for places in by_chip(seqs, peers // seqs)
+    ]
+    stats = [read_stats(block[:, half:]) for block in blocks]
     top = functools.reduce(jnp.maximum, [s[0] for s in stats])
     scales = [jnp.exp(s[0] - top) for s in stats]
     total = sum(scale * s[1] for scale, s in zip(scales, stats))
-    summed = sum(ref[:, chip, :, :half].astype(F32) * scales[chip] for chip in range(chips))
-    return (summed / total).reshape(seqs * rows, half).astype(BF16)
+    summed = sum(block[:, :half] * scale for block, scale in zip(blocks, scales))
+    return (summed / total).astype(BF16)
 
 
 def own_hidden_kernel(mine_ref, w_in_ref, acc_ref):
@@ -185,18 +204,21 @@
 
 
 def pair_sum_kernel(keep_ref, came_ref, out_ref):
-    seqs, chips, rows, half = out_ref.shape
+    peers, rows, half = out_ref.shape
+    seqs = keep_ref.shape[0] // rows
     sums = (keep_ref[...] + came_ref[...].astype(F32)).astype(BF16).reshape(seqs, rows, half)
-    for chip in range(chips):
-        out_ref[:, chip] = sums
+    for place, (e, _) in enumerate(peer_order(seqs, peers // seqs)):
+        out_ref[place] = sums[e]
 
 
 def mixed_half(mix_ref, ref):
-    experts, chips, rows, half = ref.shape
-    summed = sum(ref[:, chip].astype(F32) for chip in range(chips))
-    slot_outputs = summed.reshape(experts * rows, half).astype(BF16)
+    experts = lax.axis_size("expert")
+    summed = sum(
+        jnp.concatenate([ref[place] for place in places], axis=0).astype(F32)
+        for places in by_chip(experts, ref.shape[0] // experts)
+    )
     return lax.dot_general(
-        mix_ref[...], slot_outputs, (((0,), (0,)), ((), ())), preferred_element_type=F32
+        mix_ref[...], summed.astype(BF16), (((0,), (0,)), ((), ())), preferred_element_type=F32
     ).astype(BF16)
 
 
@@ -286,15 +308,14 @@
     )
     (packed,) = call(
         chip_sum_kernel,
-        [((experts, chips, per_expert, half + LANES), BF16)],
+        [((experts * chips, per_expert, half + LANES), BF16)],
         keep, stats, came,
         flops=COVER_FLOPS, limit=16 << 20,
     )
     groups = [
         [
             (chip * 2 + (side + 2 * e // experts) % 2) * experts + e
-            for e in range(experts)
-            for chip in range(chips)
+            for e, chip in peer_order(experts, chips)
         ]
         for side in range(2)
     ]
@@ -302,19 +323,18 @@
         lax.all_to_all, axis_name=("chip", "core", "expert"), split_axis=0, concat_axis=0,
         axis_index_groups=groups, tiled=True,
     )
-    flat = packed.reshape((experts * chips,) + packed.shape[2:])
-    mine = exchange(flat)
+    mine = exchange(packed)
     swapped = lax.ppermute(mine, "core", SWAP)
     (acc,) = call(
         own_hidden_kernel,
         [((slots, units), F32)],
-        mine.reshape(packed.shape), w_in,
+        mine, w_in,
         flops=2 * slots * half * units, limit=16 << 20,
     )
     send, hidden = call(
         send_terms_kernel,
         [((slots, half), BF16), ((slots, units), BF16)],
-        acc, swapped.reshape(packed.shape), w_in, w_out,
+        acc, swapped, w_in, w_out,
         flops=4 * slots * half * units, limit=16 << 20,
     )
     came = lax.ppermute(send, "core", SWAP)
@@ -322,15 +342,14 @@
         keep_terms_kernel, [((slots, half), F32)], hidden, w_out, flops=2 * slots * half * units
     )
     (packed,) = call(
-        pair_sum_kernel, [((experts, chips, per_expert, half), BF16)], keep, came, limit=16 << 20
-    )
-    flat = packed.reshape((experts * chips,) + packed.shape[2:])
-    mine = exchange(flat)
+        pair_sum_kernel, [((experts * chips, per_expert, half), BF16)], keep, came, limit=16 << 20
+    )
+    mine = exchange(packed)
     swapped = lax.ppermute(mine, "core", SWAP)
     (own_half,) = call(
         own_mix_kernel,
         [((count, half), BF16)],
-        mix, mine.reshape(packed.shape),
+        mix, mine,
         stay=(0,), flops=2 * slots * count * half, limit=16 << 20,
     )
     mixed = pl.pallas_call(
@@ -343,7 +362,7 @@
         cost_estimate=pl.CostEstimate(
             flops=2 * slots * count * half, bytes_accessed=2 * count * width, transcendentals=0
         ),
-    )(mix, swapped.reshape(packed.shape), own_half)
+    )(mix, swapped, own_half)
     return mixed[None]
 
 

time: 51.4 us -> 48.3 us (0.940)
  blocking collectives: 27.9 us -> 24.2 us
  starting transfers between devices: 8.63 us -> 9.24 us
    all_to_all x2, blocking collectives: 27.9 us -> 24.2 us  [on_device(): mine = exchange(packed)]
    ppermute x2, starting transfers between devices: 1.08 us -> 1.65 us  [on_device(): swapped = lax.ppermute(mine, 'core', SWAP)]
where the time goes in v9:
time: 48.3 us; the launch traced here: 48 us
  blocking collectives  24.2 us (50%)
  starting transfers between devices  9.24 us (19%)
  Pallas kernels  7.22 us (15%)
  waiting for transfers between devices  7.18 us (15%)
    all_to_all x2, blocking collectives, on_device(): mine = exchange(packed)  24.2 us
    ppermute x4, starting transfers between devices, gather_keys(): blocks.append(lax.ppermute(keys, axes, pairs))  7.05 us
    pallas_call x11, Pallas kernels, call(): pl.pallas_call(kernel, out_shape=shapes, in_specs=[pl.BlockSpec(memory_sp...  6.13 us
    ppermute x4, waiting for transfers between devices, gather_keys(): blocks.append(lax.ppermute(keys, axes, pairs))  3.32 us
    ppermute x2, starting transfers between devices, on_device(): swapped = lax.ppermute(mine, 'core', SWAP)  1.65 us
    ppermute x2, waiting for transfers between devices, on_device(): came = lax.ppermute(send, 'core', SWAP)  1.51 us
    ppermute x2, waiting for transfers between devices, on_device(): swapped = lax.ppermute(mine, 'core', SWAP)  1.4 us
    pallas_call x1, Pallas kernels, on_device(): pl.pallas_call(mix_kernel, out_shape=jax.ShapeDtypeStruct((count, width),...  1.08 us
  transfers between devices with their start and end apart: 9, of which 7 were waited for; matrix products, arithmetic and copies ran while one was open for 0% of the time, Pallas kernels for 7%

profile of v9, /device:TPU:0, one launch (start us, length us, event | category | flops | bytes accessed | tf_op | source)
XLA Modules:
  0.0 48.0 jit_solution(7908007089402873528)
XLA Ops:
  0.0 0.0 copy-start
  0.0 3.1 %collective-permute-start.3 = (bf16[8,2048]{1,0:T(8,128)(2,1)}, bf16[8,2048]{1,0:T(8,128)(2,1)S(1)}, u32[]{:S(2)}, u32[]{:S(2)}) collective-permute-start(bf16[8,2048]{1,0:T(8,128)(2,1)} %bitcast.10), channel_id=1, source_target_pairs={{0,2},{1,3},{2,0},{3,1},{4,6},{5,7},{6,4},{7,5},{8,13},{9,12},{10,... | collective-permute-start | bytes 98312 | tf_op jit(solution)/shard_map/ppermute | solution.py:93
  3.1 2.6 %collective-permute-start.2 = (bf16[8,2048]{1,0:T(8,128)(2,1)}, bf16[8,2048]{1,0:T(8,128)(2,1)S(1)}, u32[]{:S(2)}, u32[]{:S(2)}) collective-permute-start(bf16[8,2048]{1,0:T(8,128)(2,1)} %bitcast.11), channel_id=1, source_target_pairs={{0,4},{1,5},{2,6},{3,7},{4,0},{5,1},{6,2},{7,3},{8,15},{9,14},{10,... | collective-permute-start | bytes 98312 | tf_op jit(solution)/shard_map/ppermute | solution.py:93
  5.6 0.0 collective-permute-start.1
  5.6 1.4 %collective-permute-start = (bf16[8,2048]{1,0:T(8,128)(2,1)}, bf16[8,2048]{1,0:T(8,128)(2,1)S(1)}, u32[]{:S(2)}, u32[]{:S(2)}) collective-permute-start(bf16[8,2048]{1,0:T(8,128)(2,1)} %bitcast.13), channel_id=1, source_target_pairs={{0,0},{1,1},{2,2},{3,3},{4,4},{5,5},{6,6},{7,7},{8,9},{9,8},{10,11... | collective-permute-start | bytes 98312 | tf_op jit(solution)/shard_map/ppermute | solution.py:93
  7.1 1.2 %shard_map.46.tok_ref = bf16[224,2048]{1,0:T(8,128)(2,1)S(1)} custom-call(bf16[224,2048]{1,0:T(8,128)(2,1)} %bitcast.9), custom_call_target="tpu_custom_call" | custom-call | bytes 917504 | tf_op jit(solution)/shard_map/pallas_call | solution.py:246
  8.2 0.0 collective-permute-done.3.refs_3_
  8.3 0.2 collective-permute-done.2.refs_2_
  8.4 3.1 %collective-permute-done.1.refs_1_ = bf16[8,2048]{1,0:T(8,128)(2,1)S(1)} collective-permute-done((bf16[8,2048]{1,0:T(8,128)(2,1)}, bf16[8,2048]{1,0:T(8,128)(2,1)S(1)}, u32[]{:S(2)}, u32[]{:S(2)}) %collective-permute-start.1) | collective-permute-done | bytes 32800 | tf_op jit(solution)/shard_map/ppermute | solution.py:93
  11.6 0.0 collective-permute-done.refs_0_
  11.6 0.1 collective-permute-start.4
  11.7 0.4 shard_map.48.part_ref
  12.0 1.0 %collective-permute-done.4.swapped_ref = bf16[4,8,2048]{2,1,0:T(8,128)(2,1)S(1)} collective-permute-done((bf16[4,8,2048]{2,1,0:T(8,128)(2,1)S(1)}, bf16[4,8,2048]{2,1,0:T(8,128)(2,1)S(1)}, u32[]{:S(2)}, u32[]{:S(2)}) %collective-permute-start.4) | collective-permute-done | bytes 131104 | tf_op jit(solution)/shard_map/ppermute | solution.py:285
  13.0 0.8 %shard_map.49 = (f32[64,224]{1,0:T(8,128)S(1)}, bf16[64,224]{1,0:T(8,128)(2,1)S(1)}, f32[64,128]{1,0:T(8,128)S(1)}, bf16[64,1152]{1,0:T(8,128)(2,1)S(1)}) custom-call(bf16[4,8,2048]{2,1,0:T(8,128)(2,1)S(1)} %collective-permute-done.4.swapped_ref, f32[32,224]{1,0:T(8,128)S(1)} %shard_map.48.part_ref, bf16[224,2048]{1,0:T(8,128)(2,1)S(1)} %shard_map.46.tok_ref), custom_call_target="tpu_custom_call" | custom-call | flops 58720256 | bytes 266240 | tf_op jit(solution)/shard_map/pallas_call | solution.py:246
  13.8 0.0 copy-start.1
  13.8 0.2 collective-permute-start.5
  14.0 0.2 shard_map.50
  14.2 1.0 %collective-permute-done.5.came_ref = bf16[64,1152]{1,0:T(8,128)(2,1)S(1)} collective-permute-done((bf16[64,1152]{1,0:T(8,128)(2,1)S(1)}, bf16[64,1152]{1,0:T(8,128)(2,1)S(1)}, u32[]{:S(2)}, u32[]{:S(2)}) %collective-permute-start.5) | collective-permute-done | bytes 147488 | tf_op jit(solution)/shard_map/ppermute | solution.py:302
  15.2 0.3 shard_map.51
  15.6 13.2 %all_to_all.10.mine_ref = bf16[16,8,1152]{2,1,0:T(8,128)(2,1)S(1)} all-to-all(bf16[16,8,1152]{2,1,0:T(8,128)(2,1)S(1)} %shard_map.51), channel_id=1, replica_groups={{13,29,0,1,28,15,19,2,18,3,17,30,31,12,14,16},{5,21,8,9,20,7,27,10,26,1..., dimensions={0} | all-to-all | bytes 589824 | tf_op jit(solution)/shard_map/all_to_all | solution.py:326
  28.7 0.2 collective-permute-start.6
  28.9 0.0 copy-done
  28.9 0.9 %shard_map.52.acc_ref = f32[64,1536]{1,0:T(8,128)S(1)} custom-call(bf16[16,8,1152]{2,1,0:T(8,128)(2,1)S(1)} %all_to_all.10.mine_ref, bf16[2048,1536]{1,0:T(8,128)(2,1)S(1)} %bitcast.5), custom_call_target="tpu_custom_call" | custom-call | flops 201326592 | bytes 393216 | tf_op jit(solution)/shard_map/pallas_call | solution.py:246
  29.8 0.5 %collective-permute-done.6.swapped_ref = bf16[16,8,1152]{2,1,0:T(8,128)(2,1)S(1)} collective-permute-done((bf16[16,8,1152]{2,1,0:T(8,128)(2,1)S(1)}, bf16[16,8,1152]{2,1,0:T(8,128)(2,1)S(1)}, u32[]{:S(2)}, u32[]{:S(2)}) %collective-permute-start.6) | collective-permute-done | bytes 294944 | tf_op jit(solution)/shard_map/ppermute | solution.py:327
  30.3 0.0 copy-done.1
  30.3 1.4 %shard_map.53 = (bf16[64,1024]{1,0:T(8,128)(2,1)S(1)}, bf16[64,1536]{1,0:T(8,128)(2,1)S(1)}) custom-call(f32[64,1536]{1,0:T(8,128)S(1)} %shard_map.52.acc_ref, bf16[16,8,1152]{2,1,0:T(8,128)(2,1)S(1)} %collective-permute-done.6.swapped_ref, bf16[2048,1536]{1,0:T(8,128)(2,1)S(1)} %bitcast.6, bf16[1536,2048]{1,0:T(8,128)(2,1)S(1)} %bitcast.7), custom_call_target="tpu_custom_call" | custom-call | flops 402653184 | bytes 327680 | tf_op jit(solution)/shard_map/pallas_call | solution.py:246
  31.7 0.3 collective-permute-start.7
  32.0 0.7 %shard_map.54.keep_ref = f32[64,1024]{1,0:T(8,128)S(1)} custom-call(bf16[64,1536]{1,0:T(8,128)(2,1)S(1)} %get-tuple-element.29.hidden_ref, bf16[1536,2048]{1,0:T(8,128)(2,1)S(1)} %bitcast.8), custom_call_target="tpu_custom_call" | custom-call | flops 201326592 | bytes 262144 | tf_op jit(solution)/shard_map/pallas_call | solution.py:246
  32.7 0.5 %collective-permute-done.7.came_ref = bf16[64,1024]{1,0:T(8,128)(2,1)S(1)} collective-permute-done((bf16[64,1024]{1,0:T(8,128)(2,1)S(1)}, bf16[64,1024]{1,0:T(8,128)(2,1)S(1)}, u32[]{:S(2)}, u32[]{:S(2)}) %collective-permute-start.7) | collective-permute-done | bytes 131104 | tf_op jit(solution)/shard_map/ppermute | solution.py:340
  33.2 11.1 %all_to_all.11.mine_ref = bf16[16,8,1024]{2,1,0:T(8,128)(2,1)S(1)} all-to-all(bf16[16,8,1024]{2,1,0:T(8,128)(2,1)S(1)} %shard_map.55), channel_id=1, replica_groups={{13,29,0,1,28,15,19,2,18,3,17,30,31,12,14,16},{5,21,8,9,20,7,27,10,26,1..., dimensions={0} | all-to-all | bytes 524288 | tf_op jit(solution)/shard_map/all_to_all | solution.py:347
  44.3 1.5 %collective-permute-start.8 = (bf16[16,8,1024]{2,1,0:T(8,128)(2,1)S(1)}, bf16[16,8,1024]{2,1,0:T(8,128)(2,1)S(1)}, u32[]{:S(2)}, u32[]{:S(2)}) collective-permute-start(bf16[16,8,1024]{2,1,0:T(8,128)(2,1)S(1)} %all_to_all.11.mine_ref), channel_id=1, source_target_pairs={{0,8},{8,0},{1,9},{9,1},{2,10},{10,2},{3,11},{11,3},{4,12},{12,4},... | collective-permute-start | bytes 786440 | tf_op jit(solution)/shard_map/ppermute | solution.py:348
  45.7 0.3 shard_map.56.half_ref
  46.0 0.9 %collective-permute-done.8.swapped_ref = bf16[16,8,1024]{2,1,0:T(8,128)(2,1)S(1)} collective-permute-done((bf16[16,8,1024]{2,1,0:T(8,128)(2,1)S(1)}, bf16[16,8,1024]{2,1,0:T(8,128)(2,1)S(1)}, u32[]{:S(2)}, u32[]{:S(2)}) %collective-permute-start.8) | collective-permute-done | bytes 262176 | tf_op jit(solution)/shard_map/ppermute | solution.py:348
  46.9 1.1 %shard_map.57 = bf16[224,2048]{1,0:T(8,128)(2,1)} custom-call(bf16[64,224]{1,0:T(8,128)(2,1)S(1)} %get-tuple-element.25.mix_ref, bf16[16,8,1024]{2,1,0:T(8,128)(2,1)S(1)} %collective-permute-done.8.swapped_ref, bf16[224,1024]{1,0:T(8,128)(2,1)S(1)} %shard_map.56.half_ref), custom_call_target="tpu_custom_call" | custom-call | flops 29360128 | bytes 917504 | tf_op jit(solution)/shard_map/pallas_call | solution.py:355
  (2 shorter events, 0.0 us)
Async XLA Ops:
  0.0 28.9 %copy-start = (bf16[1,2048,1536]{2,1,0:T(8,128)(2,1)S(1)}, bf16[1,2048,1536]{2,1,0:T(8,128)(2,1)}, u32[]{:S(2)}) copy-start(bf16[1,2048,1536]{2,1,0:T(8,128)(2,1)} %param.6) | copy-start | bytes 18874372
  0.0 8.2 %collective-permute-start.3 = (bf16[8,2048]{1,0:T(8,128)(2,1)}, bf16[8,2048]{1,0:T(8,128)(2,1)S(1)}, u32[]{:S(2)}, u32[]{:S(2)}) collective-permute-start(bf16[8,2048]{1,0:T(8,128)(2,1)} %bitcast.10), channel_id=1, source_target_pairs={{0,2},{1,3},{2,0},{3,1},{4,6},{5,7},{6,4},{7,5},{8,13},{9,12},{10,... | collective-permute-start | bytes 98312 | tf_op jit(solution)/shard_map/ppermute | solution.py:93
  3.1 5.4 %collective-permute-start.2 = (bf16[8,2048]{1,0:T(8,128)(2,1)}, bf16[8,2048]{1,0:T(8,128)(2,1)S(1)}, u32[]{:S(2)}, u32[]{:S(2)}) collective-permute-start(bf16[8,2048]{1,0:T(8,128)(2,1)} %bitcast.11), channel_id=1, source_target_pairs={{0,4},{1,5},{2,6},{3,7},{4,0},{5,1},{6,2},{7,3},{8,15},{9,14},{10,... | collective-permute-start | bytes 98312 | tf_op jit(solution)/shard_map/ppermute | solution.py:93
  5.6 5.9 %collective-permute-start.1 = (bf16[8,2048]{1,0:T(8,128)(2,1)}, bf16[8,2048]{1,0:T(8,128)(2,1)S(1)}, u32[]{:S(2)}, u32[]{:S(2)}) collective-permute-start(bf16[8,2048]{1,0:T(8,128)(2,1)} %bitcast.12), channel_id=1, source_target_pairs={{0,6},{1,7},{2,4},{3,5},{4,2},{5,3},{6,0},{7,1},{8,11},{9,10},{10,... | collective-permute-start | bytes 98312 | tf_op jit(solution)/shard_map/ppermute | solution.py:93
  5.6 5.9 %collective-permute-start = (bf16[8,2048]{1,0:T(8,128)(2,1)}, bf16[8,2048]{1,0:T(8,128)(2,1)S(1)}, u32[]{:S(2)}, u32[]{:S(2)}) collective-permute-start(bf16[8,2048]{1,0:T(8,128)(2,1)} %bitcast.13), channel_id=1, source_target_pairs={{0,0},{1,1},{2,2},{3,3},{4,4},{5,5},{6,6},{7,7},{8,9},{9,8},{10,11... | collective-permute-start | bytes 98312 | tf_op jit(solution)/shard_map/ppermute | solution.py:93
  11.6 1.4 %collective-permute-start.4 = (bf16[4,8,2048]{2,1,0:T(8,128)(2,1)S(1)}, bf16[4,8,2048]{2,1,0:T(8,128)(2,1)S(1)}, u32[]{:S(2)}, u32[]{:S(2)}) collective-permute-start(bf16[4,8,2048]{2,1,0:T(8,128)(2,1)S(1)} %shard_map.47.stack_ref), channel_id=1, source_target_pairs={{0,8},{8,0},{1,9},{9,1},{2,10},{10,2},{3,11},{11,3},{4,12},{12,4},... | collective-permute-start | bytes 393224 | tf_op jit(solution)/shard_map/ppermute | solution.py:285
  13.8 16.5 %copy-start.1 = (bf16[1,1536,2048]{2,1,0:T(8,128)(2,1)S(1)}, bf16[1,1536,2048]{2,1,0:T(8,128)(2,1)}, u32[]{:S(2)}) copy-start(bf16[1,1536,2048]{2,1,0:T(8,128)(2,1)} %param.7) | copy-start | bytes 18874372
  13.8 1.4 %collective-permute-start.5 = (bf16[64,1152]{1,0:T(8,128)(2,1)S(1)}, bf16[64,1152]{1,0:T(8,128)(2,1)S(1)}, u32[]{:S(2)}, u32[]{:S(2)}) collective-permute-start(bf16[64,1152]{1,0:T(8,128)(2,1)S(1)} %get-tuple-element.28), channel_id=1, source_target_pairs={{0,8},{8,0},{1,9},{9,1},{2,10},{10,2},{3,11},{11,3},{4,12},{12,4},... | collective-permute-start | bytes 442376 | tf_op jit(solution)/shard_map/ppermute | solution.py:302
  28.7 1.6 %collective-permute-start.6 = (bf16[16,8,1152]{2,1,0:T(8,128)(2,1)S(1)}, bf16[16,8,1152]{2,1,0:T(8,128)(2,1)S(1)}, u32[]{:S(2)}, u32[]{:S(2)}) collective-permute-start(bf16[16,8,1152]{2,1,0:T(8,128)(2,1)S(1)} %all_to_all.10.mine_ref), channel_id=1, source_target_pairs={{0,8},{8,0},{1,9},{9,1},{2,10},{10,2},{3,11},{11,3},{4,12},{12,4},... | collective-permute-start | bytes 884744 | tf_op jit(solution)/shard_map/ppermute | solution.py:327
  31.7 1.4 %collective-permute-start.7 = (bf16[64,1024]{1,0:T(8,128)(2,1)S(1)}, bf16[64,1024]{1,0:T(8,128)(2,1)S(1)}, u32[]{:S(2)}, u32[]{:S(2)}) collective-permute-start(bf16[64,1024]{1,0:T(8,128)(2,1)S(1)} %get-tuple-element.30), channel_id=1, source_target_pairs={{0,8},{8,0},{1,9},{9,1},{2,10},{10,2},{3,11},{11,3},{4,12},{12,4},... | collective-permute-start | bytes 393224 | tf_op jit(solution)/shard_map/ppermute | solution.py:340
  44.3 2.6 %collective-permute-start.8 = (bf16[16,8,1024]{2,1,0:T(8,128)(2,1)S(1)}, bf16[16,8,1024]{2,1,0:T(8,128)(2,1)S(1)}, u32[]{:S(2)}, u32[]{:S(2)}) collective-permute-start(bf16[16,8,1024]{2,1,0:T(8,128)(2,1)S(1)} %all_to_all.11.mine_ref), channel_id=1, source_target_pairs={{0,8},{8,0},{1,9},{9,1},{2,10},{10,2},{3,11},{11,3},{4,12},{12,4},... | collective-permute-start | bytes 786440 | tf_op jit(solution)/shard_map/ppermute | solution.py:348

commit v10 on v9

--- a/solution.py
+++ b/solution.py
@@ -211,10 +211,10 @@
         out_ref[place] = sums[e]
 
 
-def mixed_half(mix_ref, ref):
+def mixed_half(mix_ref, ref, cols=slice(None)):
     experts = lax.axis_size("expert")
     summed = sum(
-        jnp.concatenate([ref[place] for place in places], axis=0).astype(F32)
+        jnp.concatenate([ref[place, :, cols] for place in places], axis=0).astype(F32)
         for places in by_chip(experts, ref.shape[0] // experts)
     )
     return lax.dot_general(
@@ -227,13 +227,18 @@
 
 
 def mix_kernel(mix_ref, swapped_ref, half_ref, out_ref, rest, sem):
-    own, other = column_halves(half_ref.shape[1])
+    half = half_ref.shape[1]
+    own, other = column_halves(half)
     copies = copy_parts(sem, [(half_ref, out_ref.at[:, own])])
-    rest[...] = mixed_half(mix_ref, swapped_ref)
-    last = pltpu.make_async_copy(rest, out_ref.at[:, other], sem.at[1])
-    last.start()
-    copies[0].wait()
-    last.wait()
+    step = half // 2
+    for i in range(2):
+        cols = slice(i * step, (i + 1) * step)
+        rest[:, cols] = mixed_half(mix_ref, swapped_ref, cols)
+        place = pl.ds(pl.multiple_of(other.start + i * step, LANES), step)
+        copies.append(pltpu.make_async_copy(rest.at[:, cols], out_ref.at[:, place], sem.at[1 + i]))
+        copies[-1].start()
+    for copy in copies:
+        copy.wait()
 
 
 def call(kernel, outs, *args, scratch=(), copies=0, in_hbm=(), stay=(), flops=0, limit=8 << 20):
@@ -357,7 +362,7 @@
         out_shape=jax.ShapeDtypeStruct((count, width), BF16),
         in_specs=[pl.BlockSpec(memory_space=pltpu.VMEM)] * 3,
         out_specs=pl.BlockSpec(memory_space=pltpu.HBM),
-        scratch_shapes=[pltpu.VMEM((count, half), BF16), pltpu.SemaphoreType.DMA((2,))],
+        scratch_shapes=[pltpu.VMEM((count, half), BF16), pltpu.SemaphoreType.DMA((3,))],
         compiler_params=pltpu.CompilerParams(vmem_limit_bytes=16 << 20),
         cost_estimate=pl.CostEstimate(
             flops=2 * slots * count * half, bytes_accessed=2 * count * width, transcendentals=0

time: 48.3 us -> 48.2 us (level)
  no operation moved by 1% of the time
where the time goes in v10:
time: 48.2 us; the launch traced here: 47.9 us
  blocking collectives  24.2 us (50%)
  starting transfers between devices  9.24 us (19%)
  waiting for transfers between devices  7.18 us (15%)
  Pallas kernels  7.17 us (15%)
    all_to_all x2, blocking collectives, on_device(): mine = exchange(packed)  24.2 us
    ppermute x4, starting transfers between devices, gather_keys(): blocks.append(lax.ppermute(keys, axes, pairs))  7.05 us
    pallas_call x11, Pallas kernels, call(): pl.pallas_call(kernel, out_shape=shapes, in_specs=[pl.BlockSpec(memory_sp...  6.13 us
    ppermute x4, waiting for transfers between devices, gather_keys(): blocks.append(lax.ppermute(keys, axes, pairs))  3.32 us
    ppermute x2, starting transfers between devices, on_device(): swapped = lax.ppermute(mine, 'core', SWAP)  1.65 us
    ppermute x2, waiting for transfers between devices, on_device(): came = lax.ppermute(send, 'core', SWAP)  1.51 us
    ppermute x2, waiting for transfers between devices, on_device(): swapped = lax.ppermute(mine, 'core', SWAP)  1.4 us
    pallas_call x1, Pallas kernels, on_device(): pl.pallas_call(mix_kernel, out_shape=jax.ShapeDtypeStruct((count, width),...  1.03 us
  transfers between devices with their start and end apart: 9, of which 7 were waited for; matrix products, arithmetic and copies ran while one was open for 0% of the time, Pallas kernels for 7%

profile of v10, /device:TPU:0, one launch (start us, length us, event | category | flops | bytes accessed | tf_op | source)
XLA Modules:
  0.0 47.9 jit_solution(10446086571306847816)
XLA Ops:
  0.0 0.0 copy-start
  0.0 3.1 %collective-permute-start.3 = (bf16[8,2048]{1,0:T(8,128)(2,1)}, bf16[8,2048]{1,0:T(8,128)(2,1)S(1)}, u32[]{:S(2)}, u32[]{:S(2)}) collective-permute-start(bf16[8,2048]{1,0:T(8,128)(2,1)} %bitcast.10), channel_id=1, source_target_pairs={{0,2},{1,3},{2,0},{3,1},{4,6},{5,7},{6,4},{7,5},{8,13},{9,12},{10,... | collective-permute-start | bytes 98312 | tf_op jit(solution)/shard_map/ppermute | solution.py:93
  3.1 2.6 %collective-permute-start.2 = (bf16[8,2048]{1,0:T(8,128)(2,1)}, bf16[8,2048]{1,0:T(8,128)(2,1)S(1)}, u32[]{:S(2)}, u32[]{:S(2)}) collective-permute-start(bf16[8,2048]{1,0:T(8,128)(2,1)} %bitcast.11), channel_id=1, source_target_pairs={{0,4},{1,5},{2,6},{3,7},{4,0},{5,1},{6,2},{7,3},{8,15},{9,14},{10,... | collective-permute-start | bytes 98312 | tf_op jit(solution)/shard_map/ppermute | solution.py:93
  5.6 0.0 collective-permute-start.1
  5.6 1.4 %collective-permute-start = (bf16[8,2048]{1,0:T(8,128)(2,1)}, bf16[8,2048]{1,0:T(8,128)(2,1)S(1)}, u32[]{:S(2)}, u32[]{:S(2)}) collective-permute-start(bf16[8,2048]{1,0:T(8,128)(2,1)} %bitcast.13), channel_id=1, source_target_pairs={{0,0},{1,1},{2,2},{3,3},{4,4},{5,5},{6,6},{7,7},{8,9},{9,8},{10,11... | collective-permute-start | bytes 98312 | tf_op jit(solution)/shard_map/ppermute | solution.py:93
  7.1 1.2 %shard_map.46.tok_ref = bf16[224,2048]{1,0:T(8,128)(2,1)S(1)} custom-call(bf16[224,2048]{1,0:T(8,128)(2,1)} %bitcast.9), custom_call_target="tpu_custom_call" | custom-call | bytes 917504 | tf_op jit(solution)/shard_map/pallas_call | solution.py:251
  8.2 0.0 collective-permute-done.3.refs_3_
  8.3 0.2 collective-permute-done.2.refs_2_
  8.4 3.1 %collective-permute-done.1.refs_1_ = bf16[8,2048]{1,0:T(8,128)(2,1)S(1)} collective-permute-done((bf16[8,2048]{1,0:T(8,128)(2,1)}, bf16[8,2048]{1,0:T(8,128)(2,1)S(1)}, u32[]{:S(2)}, u32[]{:S(2)}) %collective-permute-start.1) | collective-permute-done | bytes 32800 | tf_op jit(solution)/shard_map/ppermute | solution.py:93
  11.6 0.0 collective-permute-done.refs_0_
  11.6 0.1 collective-permute-start.4
  11.7 0.4 shard_map.48.part_ref
  12.0 1.0 %collective-permute-done.4.swapped_ref = bf16[4,8,2048]{2,1,0:T(8,128)(2,1)S(1)} collective-permute-done((bf16[4,8,2048]{2,1,0:T(8,128)(2,1)S(1)}, bf16[4,8,2048]{2,1,0:T(8,128)(2,1)S(1)}, u32[]{:S(2)}, u32[]{:S(2)}) %collective-permute-start.4) | collective-permute-done | bytes 131104 | tf_op jit(solution)/shard_map/ppermute | solution.py:290
  13.0 0.8 %shard_map.49 = (f32[64,224]{1,0:T(8,128)S(1)}, bf16[64,224]{1,0:T(8,128)(2,1)S(1)}, f32[64,128]{1,0:T(8,128)S(1)}, bf16[64,1152]{1,0:T(8,128)(2,1)S(1)}) custom-call(bf16[4,8,2048]{2,1,0:T(8,128)(2,1)S(1)} %collective-permute-done.4.swapped_ref, f32[32,224]{1,0:T(8,128)S(1)} %shard_map.48.part_ref, bf16[224,2048]{1,0:T(8,128)(2,1)S(1)} %shard_map.46.tok_ref), custom_call_target="tpu_custom_call" | custom-call | flops 58720256 | bytes 266240 | tf_op jit(solution)/shard_map/pallas_call | solution.py:251
  13.8 0.0 copy-start.1
  13.8 0.2 collective-permute-start.5
  14.0 0.2 shard_map.50
  14.2 1.0 %collective-permute-done.5.came_ref = bf16[64,1152]{1,0:T(8,128)(2,1)S(1)} collective-permute-done((bf16[64,1152]{1,0:T(8,128)(2,1)S(1)}, bf16[64,1152]{1,0:T(8,128)(2,1)S(1)}, u32[]{:S(2)}, u32[]{:S(2)}) %collective-permute-start.5) | collective-permute-done | bytes 147488 | tf_op jit(solution)/shard_map/ppermute | solution.py:307
  15.2 0.3 shard_map.51
  15.6 13.2 %all_to_all.10.mine_ref = bf16[16,8,1152]{2,1,0:T(8,128)(2,1)S(1)} all-to-all(bf16[16,8,1152]{2,1,0:T(8,128)(2,1)S(1)} %shard_map.51), channel_id=1, replica_groups={{13,29,0,1,28,15,19,2,18,3,17,30,31,12,14,16},{5,21,8,9,20,7,27,10,26,1..., dimensions={0} | all-to-all | bytes 589824 | tf_op jit(solution)/shard_map/all_to_all | solution.py:331
  28.7 0.2 collective-permute-start.6
  28.9 0.0 copy-done
  28.9 0.9 %shard_map.52.acc_ref = f32[64,1536]{1,0:T(8,128)S(1)} custom-call(bf16[16,8,1152]{2,1,0:T(8,128)(2,1)S(1)} %all_to_all.10.mine_ref, bf16[2048,1536]{1,0:T(8,128)(2,1)S(1)} %bitcast.5), custom_call_target="tpu_custom_call" | custom-call | flops 201326592 | bytes 393216 | tf_op jit(solution)/shard_map/pallas_call | solution.py:251
  29.8 0.5 %collective-permute-done.6.swapped_ref = bf16[16,8,1152]{2,1,0:T(8,128)(2,1)S(1)} collective-permute-done((bf16[16,8,1152]{2,1,0:T(8,128)(2,1)S(1)}, bf16[16,8,1152]{2,1,0:T(8,128)(2,1)S(1)}, u32[]{:S(2)}, u32[]{:S(2)}) %collective-permute-start.6) | collective-permute-done | bytes 294944 | tf_op jit(solution)/shard_map/ppermute | solution.py:332
  30.3 0.0 copy-done.1
  30.3 1.4 %shard_map.53 = (bf16[64,1024]{1,0:T(8,128)(2,1)S(1)}, bf16[64,1536]{1,0:T(8,128)(2,1)S(1)}) custom-call(f32[64,1536]{1,0:T(8,128)S(1)} %shard_map.52.acc_ref, bf16[16,8,1152]{2,1,0:T(8,128)(2,1)S(1)} %collective-permute-done.6.swapped_ref, bf16[2048,1536]{1,0:T(8,128)(2,1)S(1)} %bitcast.6, bf16[1536,2048]{1,0:T(8,128)(2,1)S(1)} %bitcast.7), custom_call_target="tpu_custom_call" | custom-call | flops 402653184 | bytes 327680 | tf_op jit(solution)/shard_map/pallas_call | solution.py:251
  31.7 0.3 collective-permute-start.7
  32.0 0.7 %shard_map.54.keep_ref = f32[64,1024]{1,0:T(8,128)S(1)} custom-call(bf16[64,1536]{1,0:T(8,128)(2,1)S(1)} %get-tuple-element.29.hidden_ref, bf16[1536,2048]{1,0:T(8,128)(2,1)S(1)} %bitcast.8), custom_call_target="tpu_custom_call" | custom-call | flops 201326592 | bytes 262144 | tf_op jit(solution)/shard_map/pallas_call | solution.py:251
  32.7 0.5 %collective-permute-done.7.came_ref = bf16[64,1024]{1,0:T(8,128)(2,1)S(1)} collective-permute-done((bf16[64,1024]{1,0:T(8,128)(2,1)S(1)}, bf16[64,1024]{1,0:T(8,128)(2,1)S(1)}, u32[]{:S(2)}, u32[]{:S(2)}) %collective-permute-start.7) | collective-permute-done | bytes 131104 | tf_op jit(solution)/shard_map/ppermute | solution.py:345
  33.2 11.1 %all_to_all.11.mine_ref = bf16[16,8,1024]{2,1,0:T(8,128)(2,1)S(1)} all-to-all(bf16[16,8,1024]{2,1,0:T(8,128)(2,1)S(1)} %shard_map.55), channel_id=1, replica_groups={{13,29,0,1,28,15,19,2,18,3,17,30,31,12,14,16},{5,21,8,9,20,7,27,10,26,1..., dimensions={0} | all-to-all | bytes 524288 | tf_op jit(solution)/shard_map/all_to_all | solution.py:352
  44.3 1.5 %collective-permute-start.8 = (bf16[16,8,1024]{2,1,0:T(8,128)(2,1)S(1)}, bf16[16,8,1024]{2,1,0:T(8,128)(2,1)S(1)}, u32[]{:S(2)}, u32[]{:S(2)}) collective-permute-start(bf16[16,8,1024]{2,1,0:T(8,128)(2,1)S(1)} %all_to_all.11.mine_ref), channel_id=1, source_target_pairs={{0,8},{8,0},{1,9},{9,1},{2,10},{10,2},{3,11},{11,3},{4,12},{12,4},... | collective-permute-start | bytes 786440 | tf_op jit(solution)/shard_map/ppermute | solution.py:353
  45.7 0.3 shard_map.56.half_ref
  46.0 0.9 %collective-permute-done.8.swapped_ref = bf16[16,8,1024]{2,1,0:T(8,128)(2,1)S(1)} collective-permute-done((bf16[16,8,1024]{2,1,0:T(8,128)(2,1)S(1)}, bf16[16,8,1024]{2,1,0:T(8,128)(2,1)S(1)}, u32[]{:S(2)}, u32[]{:S(2)}) %collective-permute-start.8) | collective-permute-done | bytes 262176 | tf_op jit(solution)/shard_map/ppermute | solution.py:353
  46.9 1.0 %shard_map.57 = bf16[224,2048]{1,0:T(8,128)(2,1)} custom-call(bf16[64,224]{1,0:T(8,128)(2,1)S(1)} %get-tuple-element.25.mix_ref, bf16[16,8,1024]{2,1,0:T(8,128)(2,1)S(1)} %collective-permute-done.8.swapped_ref, bf16[224,1024]{1,0:T(8,128)(2,1)S(1)} %shard_map.56.half_ref), custom_call_target="tpu_custom_call" | custom-call | flops 29360128 | bytes 917504 | tf_op jit(solution)/shard_map/pallas_call | solution.py:360
  (2 shorter events, 0.0 us)
Async XLA Ops:
  0.0 28.9 %copy-start = (bf16[1,2048,1536]{2,1,0:T(8,128)(2,1)S(1)}, bf16[1,2048,1536]{2,1,0:T(8,128)(2,1)}, u32[]{:S(2)}) copy-start(bf16[1,2048,1536]{2,1,0:T(8,128)(2,1)} %param.6) | copy-start | bytes 18874372
  0.0 8.2 %collective-permute-start.3 = (bf16[8,2048]{1,0:T(8,128)(2,1)}, bf16[8,2048]{1,0:T(8,128)(2,1)S(1)}, u32[]{:S(2)}, u32[]{:S(2)}) collective-permute-start(bf16[8,2048]{1,0:T(8,128)(2,1)} %bitcast.10), channel_id=1, source_target_pairs={{0,2},{1,3},{2,0},{3,1},{4,6},{5,7},{6,4},{7,5},{8,13},{9,12},{10,... | collective-permute-start | bytes 98312 | tf_op jit(solution)/shard_map/ppermute | solution.py:93
  3.1 5.4 %collective-permute-start.2 = (bf16[8,2048]{1,0:T(8,128)(2,1)}, bf16[8,2048]{1,0:T(8,128)(2,1)S(1)}, u32[]{:S(2)}, u32[]{:S(2)}) collective-permute-start(bf16[8,2048]{1,0:T(8,128)(2,1)} %bitcast.11), channel_id=1, source_target_pairs={{0,4},{1,5},{2,6},{3,7},{4,0},{5,1},{6,2},{7,3},{8,15},{9,14},{10,... | collective-permute-start | bytes 98312 | tf_op jit(solution)/shard_map/ppermute | solution.py:93
  5.6 5.9 %collective-permute-start.1 = (bf16[8,2048]{1,0:T(8,128)(2,1)}, bf16[8,2048]{1,0:T(8,128)(2,1)S(1)}, u32[]{:S(2)}, u32[]{:S(2)}) collective-permute-start(bf16[8,2048]{1,0:T(8,128)(2,1)} %bitcast.12), channel_id=1, source_target_pairs={{0,6},{1,7},{2,4},{3,5},{4,2},{5,3},{6,0},{7,1},{8,11},{9,10},{10,... | collective-permute-start | bytes 98312 | tf_op jit(solution)/shard_map/ppermute | solution.py:93
  5.6 5.9 %collective-permute-start = (bf16[8,2048]{1,0:T(8,128)(2,1)}, bf16[8,2048]{1,0:T(8,128)(2,1)S(1)}, u32[]{:S(2)}, u32[]{:S(2)}) collective-permute-start(bf16[8,2048]{1,0:T(8,128)(2,1)} %bitcast.13), channel_id=1, source_target_pairs={{0,0},{1,1},{2,2},{3,3},{4,4},{5,5},{6,6},{7,7},{8,9},{9,8},{10,11... | collective-permute-start | bytes 98312 | tf_op jit(solution)/shard_map/ppermute | solution.py:93
  11.6 1.4 %collective-permute-start.4 = (bf16[4,8,2048]{2,1,0:T(8,128)(2,1)S(1)}, bf16[4,8,2048]{2,1,0:T(8,128)(2,1)S(1)}, u32[]{:S(2)}, u32[]{:S(2)}) collective-permute-start(bf16[4,8,2048]{2,1,0:T(8,128)(2,1)S(1)} %shard_map.47.stack_ref), channel_id=1, source_target_pairs={{0,8},{8,0},{1,9},{9,1},{2,10},{10,2},{3,11},{11,3},{4,12},{12,4},... | collective-permute-start | bytes 393224 | tf_op jit(solution)/shard_map/ppermute | solution.py:290
  13.8 16.5 %copy-start.1 = (bf16[1,1536,2048]{2,1,0:T(8,128)(2,1)S(1)}, bf16[1,1536,2048]{2,1,0:T(8,128)(2,1)}, u32[]{:S(2)}) copy-start(bf16[1,1536,2048]{2,1,0:T(8,128)(2,1)} %param.7) | copy-start | bytes 18874372
  13.8 1.4 %collective-permute-start.5 = (bf16[64,1152]{1,0:T(8,128)(2,1)S(1)}, bf16[64,1152]{1,0:T(8,128)(2,1)S(1)}, u32[]{:S(2)}, u32[]{:S(2)}) collective-permute-start(bf16[64,1152]{1,0:T(8,128)(2,1)S(1)} %get-tuple-element.28), channel_id=1, source_target_pairs={{0,8},{8,0},{1,9},{9,1},{2,10},{10,2},{3,11},{11,3},{4,12},{12,4},... | collective-permute-start | bytes 442376 | tf_op jit(solution)/shard_map/ppermute | solution.py:307
  28.7 1.6 %collective-permute-start.6 = (bf16[16,8,1152]{2,1,0:T(8,128)(2,1)S(1)}, bf16[16,8,1152]{2,1,0:T(8,128)(2,1)S(1)}, u32[]{:S(2)}, u32[]{:S(2)}) collective-permute-start(bf16[16,8,1152]{2,1,0:T(8,128)(2,1)S(1)} %all_to_all.10.mine_ref), channel_id=1, source_target_pairs={{0,8},{8,0},{1,9},{9,1},{2,10},{10,2},{3,11},{11,3},{4,12},{12,4},... | collective-permute-start | bytes 884744 | tf_op jit(solution)/shard_map/ppermute | solution.py:332
  31.7 1.4 %collective-permute-start.7 = (bf16[64,1024]{1,0:T(8,128)(2,1)S(1)}, bf16[64,1024]{1,0:T(8,128)(2,1)S(1)}, u32[]{:S(2)}, u32[]{:S(2)}) collective-permute-start(bf16[64,1024]{1,0:T(8,128)(2,1)S(1)} %get-tuple-element.30), channel_id=1, source_target_pairs={{0,8},{8,0},{1,9},{9,1},{2,10},{10,2},{3,11},{11,3},{4,12},{12,4},... | collective-permute-start | bytes 393224 | tf_op jit(solution)/shard_map/ppermute | solution.py:345
  44.3 2.6 %collective-permute-start.8 = (bf16[16,8,1024]{2,1,0:T(8,128)(2,1)S(1)}, bf16[16,8,1024]{2,1,0:T(8,128)(2,1)S(1)}, u32[]{:S(2)}, u32[]{:S(2)}) collective-permute-start(bf16[16,8,1024]{2,1,0:T(8,128)(2,1)S(1)} %all_to_all.11.mine_ref), channel_id=1, source_target_pairs={{0,8},{8,0},{1,9},{9,1},{2,10},{10,2},{3,11},{11,3},{4,12},{12,4},... | collective-permute-start | bytes 786440 | tf_op jit(solution)/shard_map/ppermute | solution.py:353
